TPU v7x, 512 devices: a whole 4x8x8 slice. The times are simulated.
512 devices in a mesh: row: 32 (over z, y_lo), col: 16 (over y_hi, x, core).
Axes of the slice: x: 4, y: 8 (y_hi: 2, y_lo: 4; y = y_hi * 4 + y_lo), z: 8, core: 2. Of those that a mesh axis runs over, the one named last changes fastest.
Arguments:
- features: bfloat16 [16, 4096, 128], P('col', 'row'), may hold values from -6 to 6
- weight1: bfloat16 [128, 128], replicated, may hold values from -0.5 to 0.5
- weight2: bfloat16 [128, 128], replicated, may hold values from -0.5 to 0.5
- tile_values: bfloat16 [32, 16, 96, 128, 128], P('row', 'col'), may hold values from -0.1875 to 0.1875
- tile_coords: int32 [32, 16, 2, 96], P('row', 'col'), may hold values from 0 to 31, as said below
- tile_count: int32 [32, 16], P('row', 'col'), may hold values from 1 to 96, as said below
- out_grad: bfloat16 [16, 4096, 128], P('col', 'row'), may hold values from -6 to 6
Outputs:
- output: bfloat16 [16, 4096, 128], P('col', 'row')
- grad_features: bfloat16 [16, 4096, 128], P('col', 'row')
- grad_weight1: float32 [128, 128], replicated
- grad_weight2: float32 [128, 128], replicated
Inputs may be any that keep to these rules, and one draw needn't show every extreme that they name: On each device tile_coords[r, c, 0, t] is below 16 and tile_coords[r, c, 1, t] below 32; no block position appears twice among a device's 96 slots. `tile_count`: some device has all 96 slots live.
All inputs are finite; a program needn't handle non-finite values.
Results may differ from a plain program's by a relative error of at most 0.034.
Values may be sent and summed in bfloat16 or wider, within the bound.
No kernel may reach another device: no remote copies, remote signals or barrier semaphores. Data moves between devices by JAX's collectives and lax.ppermute only.
A program may use at most 64 MiB of HBM per device.

v0:
```python
import math

import jax
import jax.numpy as jnp
from jax import lax
from jax.sharding import PartitionSpec as P


def forward_part(local_tiles, row_ids, col_ids, live_slots, panel_rows, row_blocks):
    block_side = local_tiles.shape[1]
    feat_width = panel_rows.shape[-1]
    blocks = panel_rows.reshape(-1, block_side, feat_width)[col_ids]
    products = jnp.einsum("tij,tjf->tif", local_tiles, blocks, preferred_element_type=jnp.float32)
    onehot = jnp.where(
        (row_ids[None, :] == jnp.arange(row_blocks, dtype=jnp.int32)[:, None])
        & live_slots[None, :],
        1.0,
        0.0,
    ).astype(jnp.float32)
    return jnp.einsum("rt,tif->rif", onehot, products).reshape(row_blocks * block_side, feat_width)


def transposed_part(local_tiles, row_ids, col_ids, live_slots, panel_rows, col_blocks):
    block_side = local_tiles.shape[1]
    feat_width = panel_rows.shape[-1]
    blocks = panel_rows.reshape(-1, block_side, feat_width)[row_ids]
    products = jnp.einsum("tji,tjf->tif", local_tiles, blocks, preferred_element_type=jnp.float32)
    onehot = jnp.where(
        (col_ids[None, :] == jnp.arange(col_blocks, dtype=jnp.int32)[:, None])
        & live_slots[None, :],
        1.0,
        0.0,
    ).astype(jnp.float32)
    return jnp.einsum("ct,tif->cif", onehot, products).reshape(col_blocks * block_side, feat_width)


def silu_slope(value):
    sigmoid = jax.nn.sigmoid(value)
    return sigmoid * (1.0 + value * (1.0 - sigmoid))


def on_device(features, weight1, weight2, tile_values, tile_coords, tile_count, out_grad):
    local_tiles = tile_values[0, 0]
    row_ids = tile_coords[0, 0, 0]
    col_ids = tile_coords[0, 0, 1]
    slot_total = local_tiles.shape[0]
    live_slots = jnp.arange(slot_total, dtype=jnp.int32) < tile_count[0, 0]
    block_side = local_tiles.shape[1]
    shard_rows = features.shape[1]
    row_blocks = shard_rows * lax.axis_size("col") // block_side
    col_blocks = shard_rows * lax.axis_size("row") // block_side
    node_total = shard_rows * lax.axis_size("row") * lax.axis_size("col")
    grad_local = out_grad[0]
    grad_two = jnp.dot(grad_local, weight2.T, preferred_element_type=jnp.float32).astype(
        jnp.bfloat16
    )
    gathered = lax.all_gather(features, "row", axis=1, tiled=True)[0]
    grad_rows = lax.all_gather(grad_two, "row", axis=0, tiled=True)
    part_one = forward_part(local_tiles, row_ids, col_ids, live_slots, gathered, row_blocks)
    part_three = forward_part(local_tiles, row_ids, col_ids, live_slots, grad_rows, row_blocks)
    agg_sum, grad_hidden = (
        lax.psum_scatter(
            part_one.astype(jnp.bfloat16), "col", scatter_dimension=0, tiled=True
        ).astype(jnp.float32),
        lax.psum_scatter(
            part_three.astype(jnp.bfloat16), "col", scatter_dimension=0, tiled=True
        ).astype(jnp.float32),
    )
    agg_one = agg_sum.astype(jnp.bfloat16)
    pre_one = jnp.dot(agg_one, weight1, preferred_element_type=jnp.float32)
    hidden = jax.nn.silu(pre_one).astype(jnp.bfloat16)
    hidden_rows = lax.all_gather(hidden, "col", axis=0, tiled=True)
    part_two = transposed_part(local_tiles, row_ids, col_ids, live_slots, hidden_rows, col_blocks)
    agg_two = lax.psum_scatter(
        part_two.astype(jnp.bfloat16), "row", scatter_dimension=0, tiled=True
    )
    output = jnp.dot(agg_two, weight2, preferred_element_type=jnp.float32).astype(jnp.bfloat16)
    grad_pre = (grad_hidden * silu_slope(pre_one)).astype(jnp.bfloat16)
    grad_one = jnp.dot(grad_pre, weight1.T, preferred_element_type=jnp.float32).astype(jnp.bfloat16)
    grad_hidden_rows = lax.all_gather(grad_one, "col", axis=0, tiled=True)
    part_four = transposed_part(
        local_tiles, row_ids, col_ids, live_slots, grad_hidden_rows, col_blocks
    )
    grad_features = lax.psum_scatter(
        part_four.astype(jnp.bfloat16), "row", scatter_dimension=0, tiled=True
    )
    contract = (((0,), (0,)), ((), ()))
    weight_one = lax.dot_general(agg_one, grad_pre, contract, preferred_element_type=jnp.float32)
    weight_two = lax.dot_general(agg_two, grad_local, contract, preferred_element_type=jnp.float32)
    sum_one, sum_two = lax.psum((weight_one, weight_two), ("row", "col"))
    factor = 1.0 / math.sqrt(node_total)
    return (output[None], grad_features[None], sum_one * factor, sum_two * factor)


def solution(mesh):
    placed = (
        P("col", "row", None),
        P(),
        P(),
        P("row", "col", None, None, None),
        P("row", "col", None, None),
        P("row", "col"),
        P("col", "row", None),
    )
    return jax.shard_map(
        on_device,
        mesh=mesh,
        in_specs=placed,
        out_specs=(P("col", "row", None), P("col", "row", None), P(), P()),
        check_vma=False,
    )
```

profile of v0, /device:TPU:56, one launch (start us, length us, event | category | flops | bytes accessed | tf_op | source)
XLA Modules:
  0.0 1132.4 jit_solution(11435500891429155768)
XLA Ops:
  7.2 0.0 copy-start
  7.2 0.0 all-gather.5.cloned.1.call-start
  7.2 1.7 convolution_convert_fusion.1
  8.9 0.0 all-gather.5.cloned.1.call-update
  8.9 0.0 all-gather.3.cloned.1.call-start
  9.0 0.7 all-gather.3.cloned.1.call-update
  9.7 0.0 reduce-scatter.9.cloned.1.call-start
  10.4 0.8 fusion.63
  11.2 0.8 slice_bitcast_fusion.1
  11.9 152.4 %all-gather.5.cloned.1.call-done = bf16[4096,128]{1,0:T(8,128)(2,1)} async-done(((bf16[128,128]{1,0:T(8,128)(2,1)}), bf16[4096,128]{1,0:T(8,128)(2,1)}) %all-gather.5.cloned.1.call-update) | async-done | bytes 1048592 | tf_op jit(solution)/shard_map/all_gather | solution.py:58
  164.3 3.9 gather_fusion.2
  168.3 0.0 copy-done
  168.3 5.9 fusion.10
  174.2 5.0 copy.18
  179.1 2.4 fusion.25
  181.6 1.0 copy.14
  182.5 0.0 reduce-scatter.9.cloned.1.call-update
  182.5 0.0 reduce-scatter.5.cloned.1.call-start
  182.6 137.4 %all-gather.3.cloned.1.call-done = bf16[1,4096,128]{2,1,0:T(8,128)(2,1)} async-done(((bf16[1,128,128]{2,1,0:T(8,128)(2,1)}), bf16[1,4096,128]{2,1,0:T(8,128)(2,1)}) %all-gather.3.cloned.1.call-update) | async-done | bytes 1048592 | tf_op jit(solution)/shard_map/all_gather | solution.py:57
  320.0 3.9 gather_fusion
  323.9 5.9 fusion.14
  329.8 5.0 copy.16
  334.8 0.0 copy-start.4
  334.8 2.4 fusion.22
  337.2 1.0 copy.12
  338.2 0.0 reduce-scatter.5.cloned.1.call-update
  338.2 0.0 reduce-scatter.7.cloned.1.call-start
  338.2 72.5 %reduce-scatter.9.cloned.1.call-done = bf16[128,128]{1,0:T(8,128)(2,1)} async-done(((bf16[2048,128]{1,0:T(8,128)(2,1)}), bf16[128,128]{1,0:T(8,128)(2,1)}) %reduce-scatter.9.cloned.1.call-update) | async-done | bytes 32784 | tf_op jit(solution)/shard_map/reduce_scatter | solution.py:65
  410.8 86.4 %reduce-scatter.5.cloned.1.call-done = bf16[128,128]{1,0:T(8,128)(2,1)} async-done(((bf16[2048,128]{1,0:T(8,128)(2,1)}), bf16[128,128]{1,0:T(8,128)(2,1)}) %reduce-scatter.5.cloned.1.call-update) | async-done | bytes 32784 | tf_op jit(solution)/shard_map/reduce_scatter | solution.py:62
  497.2 0.0 copy-done.4
  497.2 0.9 multiply_convert_fusion
  498.1 31.3 %all_gather.13 = bf16[2048,128]{1,0:T(8,128)(2,1)} all-gather(bf16[128,128]{1,0:T(8,128)(2,1)S(1)} %get-tuple-element.7), channel_id=1, replica_groups=mesh['row'=32,'col'=16] {'col'}, dimensions={0}, use_global_device_ids=true | all-gather | bytes 557056 | tf_op jit(solution)/shard_map/all_gather | solution.py:72
  529.4 3.7 gather_fusion.1
  533.2 4.8 fusion.12
  537.9 5.0 copy.17
  542.9 2.4 fusion.16
  545.3 1.4 copy.13
  546.7 0.0 reduce-scatter.7.cloned.1.call-update
  546.7 0.0 all-reduce.3.cloned.1.call-start
  546.8 0.1 convolution_convert_fusion
  546.9 28.6 %all_gather.15 = bf16[2048,128]{1,0:T(8,128)(2,1)} all-gather(bf16[128,128]{1,0:T(8,128)(2,1)S(1)} %convolution_convert_fusion), channel_id=1, replica_groups=mesh['row'=32,'col'=16] {'col'}, dimensions={0}, use_global_device_ids=true | all-gather | bytes 557056 | tf_op jit(solution)/shard_map/all_gather | solution.py:80
  575.5 3.7 gather_fusion.3
  579.3 4.8 fusion.8
  584.1 0.0 copy-start.5
  584.1 0.0 copy-start.2
  584.1 5.0 copy.19
  589.0 0.0 copy-done.5
  589.0 0.8 fusion.72
  589.8 111.7 %reduce-scatter.7.cloned.1.call-done = bf16[128,128]{1,0:T(8,128)(2,1)} async-done(((bf16[4096,128]{1,0:T(8,128)(2,1)}), bf16[128,128]{1,0:T(8,128)(2,1)}) %reduce-scatter.7.cloned.1.call-update) | async-done | bytes 32784 | tf_op jit(solution)/shard_map/reduce_scatter | solution.py:74
  701.6 0.0 copy-done.2
  701.6 1.6 fusion.29
  703.1 0.0 all-reduce.3.cloned.1.call-update
  703.2 0.0 copy-start.1
  703.2 0.0 copy-start.3
  703.2 0.0 reduce-scatter.11.cloned.1.call-start
  703.2 2.4 fusion.19
  705.7 1.4 copy.15
  707.1 0.0 reduce-scatter.11.cloned.1.call-update
  707.1 0.0 copy-done.1
  707.1 0.0 copy-done.3
  707.1 0.8 fusion.28
  707.9 263.2 %all-reduce.3.cloned.1.call-done = (f32[128,128]{1,0:T(8,128)}, f32[128,128]{1,0:T(8,128)}) async-done(((f32[128,128]{1,0:T(8,128)}, f32[128,128]{1,0:T(8,128)}), (f32[128,128]{1,0:T(8,128)}, f32[128,128]{1,0:T(8,128)})) %all-reduce.3.cloned.1.call-update) | async-done | bytes 131088 | tf_op jit(solution)/shard_map/psum | solution.py:90
  971.1 1.5 broadcast_multiply_fusion
  972.6 152.9 %reduce-scatter.11.cloned.1.call-done = bf16[128,128]{1,0:T(8,128)(2,1)} async-done(((bf16[4096,128]{1,0:T(8,128)(2,1)}), bf16[128,128]{1,0:T(8,128)(2,1)}) %reduce-scatter.11.cloned.1.call-update) | async-done | bytes 32784 | tf_op jit(solution)/shard_map/reduce_scatter | solution.py:84
  (3 shorter events, 0.0 us)
Async XLA Ops:
  7.2 161.1 %copy-start = (bf16[1,1,96,128,128]{4,3,2,1,0:T(8,128)(2,1)S(1)}, bf16[1,1,96,128,128]{4,3,2,1,0:T(8,128)(2,1)}, u32[]{:S(2)}) copy-start(bf16[1,1,96,128,128]{4,3,2,1,0:T(8,128)(2,1)} %param.10) | copy-start | bytes 9437188
  7.2 157.2 %all-gather.5.cloned.1.call-start = ((), (), s32[]{:S(2)}) async-start(), calls=%async_computation.7 | async-start | bytes 1081344 | tf_op jit(solution)/shard_map/all_gather | solution.py:58
  8.9 311.0 %all-gather.3.cloned.1.call-start = ((), (), s32[]{:S(2)}) async-start(), calls=%async_computation.4 | async-start | bytes 1081344 | tf_op jit(solution)/shard_map/all_gather | solution.py:57
  9.7 401.1 %reduce-scatter.9.cloned.1.call-start = ((), (), s32[]{:S(2)}) async-start(), calls=%async_computation.8 | async-start | bytes 557056 | tf_op jit(solution)/shard_map/reduce_scatter | solution.py:65
  182.5 314.6 %reduce-scatter.5.cloned.1.call-start = ((), (), s32[]{:S(2)}) async-start(), calls=%async_computation.5 | async-start | bytes 557056 | tf_op jit(solution)/shard_map/reduce_scatter | solution.py:62
  334.8 162.4 %copy-start.4 = (bf16[128,128]{1,0:T(8,128)(2,1)S(1)}, bf16[128,128]{1,0:T(8,128)(2,1)}, u32[]{:S(2)}) copy-start(bf16[128,128]{1,0:T(8,128)(2,1)} %param.8) | copy-start | bytes 98308
  338.2 363.4 %reduce-scatter.7.cloned.1.call-start = ((), (), s32[]{:S(2)}) async-start(), calls=%async_computation.6 | async-start | bytes 1081344 | tf_op jit(solution)/shard_map/reduce_scatter | solution.py:74
  546.7 424.3 %all-reduce.3.cloned.1.call-start = ((), (), s32[]{:S(2)}) async-start(), calls=%async_computation.10 | async-start | bytes 262144 | tf_op jit(solution)/shard_map/psum | solution.py:90
  584.1 5.0 copy-start.5
  584.1 117.5 %copy-start.2 = (bf16[1,128,128]{2,1,0:T(8,128)(2,1)S(1)}, bf16[1,128,128]{2,1,0:T(8,128)(2,1)}, u32[]{:S(2)}) copy-start(bf16[1,128,128]{2,1,0:T(8,128)(2,1)} %param.13) | copy-start | bytes 98308
  703.2 3.9 copy-start.1
  703.2 3.9 copy-start.3
  703.2 422.3 %reduce-scatter.11.cloned.1.call-start = ((), (), s32[]{:S(2)}) async-start(), calls=%async_computation.9 | async-start | bytes 1081344 | tf_op jit(solution)/shard_map/reduce_scatter | solution.py:84
Sparse Core Ops, SparseCore 0:
  10.7 153.6 all-gather.4
  166.4 153.5 all-gather.2
  324.6 86.0 reduce-scatter.8
  415.9 81.1 reduce-scatter.4
  546.9 154.6 reduce-scatter.6
  708.1 262.9 all-reduce.2
  974.4 151.0 reduce-scatter.10
where the time goes:
time: 1140 us; the launch traced here: 1130 us
  waiting for transfers between devices  977 us (86%)
  blocking collectives  59.9 us (5%)
  local copies, waits for them, and re-layouts  40.6 us (4%)
  matrix products  37 us (3%)
  between operations  14.9 us (1%)
    psum x1, waiting for transfers between devices, on_device(): sum_one, sum_two = lax.psum((weight_one, weight_two), ('row', 'col'))  263 us
    reduce_scatter x1, waiting for transfers between devices, on_device(): lax.psum_scatter(part_four.astype(jnp.bfloat16), 'row', scatter_dimension...  153 us
    all_gather x1, waiting for transfers between devices, on_device(): grad_rows = lax.all_gather(grad_two, 'row', axis=0, tiled=True)  152 us
    all_gather x1, waiting for transfers between devices, on_device(): gathered = lax.all_gather(features, 'row', axis=1, tiled=True)[0]  137 us
    reduce_scatter x1, waiting for transfers between devices, on_device(): lax.psum_scatter(part_two.astype(jnp.bfloat16), 'row', scatter_dimension=...  112 us
    reduce_scatter x1, waiting for transfers between devices, on_device(): lax.psum_scatter(part_one.astype(jnp.bfloat16), 'col', scatter_dimension=...  86.4 us
    reduce_scatter x1, waiting for transfers between devices, on_device(): lax.psum_scatter(part_three.astype(jnp.bfloat16), 'col', scatter_dimensio...  72.5 us
    all_gather x1, blocking collectives, on_device(): hidden_rows = lax.all_gather(hidden, 'col', axis=0, tiled=True)  31.3 us
  transfers between devices with their start and end apart: 7, of which 7 were waited for; matrix products, arithmetic and copies ran while one was open for 5% of the time, Pallas kernels for 0%

commit v1 on v0

v1 whole, which is shorter than its diff:
```python
import functools
import math

import jax
import jax.numpy as jnp
from jax import lax
from jax.experimental import pallas as pl
from jax.experimental.pallas import tpu as pltpu
from jax.sharding import PartitionSpec as P


def tile_kernel(transposed, coords_ref, count_ref, tiles_ref, panel_ref, out_ref, acc_ref):
    acc_ref[...] = jnp.zeros_like(acc_ref)
    source, target = (0, 1) if transposed else (1, 0)
    contract = (((0,), (0,)), ((), ())) if transposed else (((1,), (0,)), ((), ()))

    def one_slot(slot, carry):
        product = lax.dot_general(
            tiles_ref[slot],
            panel_ref[coords_ref[source, slot]],
            contract,
            preferred_element_type=jnp.float32,
        )
        acc_ref[coords_ref[target, slot]] += product
        return carry

    lax.fori_loop(0, count_ref[0], one_slot, 0)
    out_ref[...] = acc_ref[...].astype(out_ref.dtype)


def tile_products(transposed, coords, count, tiles, panel, target_blocks):
    side, width = tiles.shape[1], panel.shape[-1]
    blocks = panel.shape[0]
    vmem = pl.BlockSpec(memory_space=pltpu.VMEM)
    smem = pl.BlockSpec(memory_space=pltpu.SMEM)
    return pl.pallas_call(
        functools.partial(tile_kernel, transposed),
        out_shape=jax.ShapeDtypeStruct((target_blocks, side, width), jnp.bfloat16),
        in_specs=[smem, smem, vmem, vmem],
        out_specs=vmem,
        scratch_shapes=[pltpu.VMEM((target_blocks, side, width), jnp.float32)],
        compiler_params=pltpu.CompilerParams(vmem_limit_bytes=40 << 20),
        cost_estimate=pl.CostEstimate(
            flops=2 * tiles.shape[0] * side * side * width,
            transcendentals=0,
            bytes_accessed=2 * (tiles.size + blocks * side * width + target_blocks * side * width),
        ),
    )(coords, count, tiles, panel)


def exchange(blocks, axis):
    return lax.all_to_all(blocks, axis, 0, 0, tiled=True)


def two_halves(value):
    high = lax.reduce_precision(value, 8, 7)
    return high.astype(jnp.bfloat16), (value - high).astype(jnp.bfloat16)


def block_sum(blocks):
    return jnp.sum(blocks.astype(jnp.float32), axis=0)


def on_device(features, weight1, weight2, tile_values, tile_coords, tile_count, out_grad):
    tiles = tile_values[0, 0]
    coords = tile_coords[0, 0]
    count = tile_count[0]
    rows_n, cols_n = lax.axis_size("row"), lax.axis_size("col")
    side, feat = features.shape[1], features.shape[2]
    node_total = side * rows_n * cols_n
    f32 = functools.partial(jnp.dot, preferred_element_type=jnp.float32)
    contract = (((0,), (0,)), ((), ()))

    both = jnp.concatenate([features[0], out_grad[0]], axis=1)
    panel = exchange(jnp.broadcast_to(both[None], (rows_n, side, 2 * feat)), "row")
    parts = tile_products(False, coords, count, tiles, panel, cols_n)

    sums = block_sum(exchange(parts, "col"))
    agg_one = sums[:, :feat].astype(jnp.bfloat16)
    agg_grad = sums[:, feat:].astype(jnp.bfloat16)
    pre_one = f32(agg_one, weight1)
    sigmoid = jax.nn.sigmoid(pre_one)
    hidden = (pre_one * sigmoid).astype(jnp.bfloat16)
    grad_hidden = f32(agg_grad, weight2.T)
    grad_pre = (grad_hidden * (sigmoid * (1.0 + pre_one * (1.0 - sigmoid)))).astype(jnp.bfloat16)
    grad_one = f32(grad_pre, weight1.T).astype(jnp.bfloat16)
    term_one = lax.dot_general(agg_one, grad_pre, contract, preferred_element_type=jnp.float32)
    term_two = lax.dot_general(hidden, agg_grad, contract, preferred_element_type=jnp.float32)

    terms = jnp.concatenate([term_one, term_two], axis=1)
    slice_rows = feat // cols_n
    slices = [h.reshape(cols_n, slice_rows, 2 * feat) for h in two_halves(terms)]
    both = jnp.concatenate([hidden, grad_one], axis=1)
    sent = jnp.concatenate(
        [jnp.broadcast_to(both[None], (cols_n, side, 2 * feat)), *slices], axis=1
    )
    got = exchange(sent, "col")
    terms = block_sum(got[:, side : side + slice_rows]) + block_sum(got[:, side + slice_rows :])
    parts = tile_products(True, coords, count, tiles, got[:, :side], rows_n)

    slices = [
        jnp.broadcast_to(h[None], (rows_n, slice_rows, 2 * feat)) for h in two_halves(terms)
    ]
    got = exchange(jnp.concatenate([parts, *slices], axis=1), "row")
    sums = block_sum(got[:, :side]).astype(jnp.bfloat16)
    terms = block_sum(got[:, side : side + slice_rows]) + block_sum(got[:, side + slice_rows :])
    output = f32(sums[:, :feat], weight2).astype(jnp.bfloat16)
    grad_features = sums[:, feat:]
    weights = lax.all_gather(terms * (1.0 / math.sqrt(node_total)), "col", axis=0, tiled=True)
    return (output[None], grad_features[None], weights[:, :feat], weights[:, feat:])


def solution(mesh):
    placed = (
        P("col", "row", None),
        P(),
        P(),
        P("row", "col", None, None, None),
        P("row", "col", None, None),
        P("row", "col"),
        P("col", "row", None),
    )
    return jax.shard_map(
        on_device,
        mesh=mesh,
        in_specs=placed,
        out_specs=(P("col", "row", None), P("col", "row", None), P(), P()),
        check_vma=False,
    )
```

time: 1140 us -> 272 us (0.24)
  waiting for transfers between devices: 977 us -> 49.1 us
  blocking collectives: 59.9 us -> 167 us
  local copies, waits for them, and re-layouts: 40.6 us -> 3.15 us
  matrix products: 37 us -> 1.59 us
  Pallas kernels: 0 us -> 31.3 us
  starting transfers between devices: 0.29 us -> 14 us
  between operations: 14.9 us -> 1.45 us
    reduce_scatter x4 -> x0, waiting for transfers between devices: 424 us -> none  [the longest x1 153 us: on_device(): lax.psum_scatter(part_four.astype(jnp.bfloat16), 'row', scatter_dimension...]
    all_gather x2 -> x0, waiting for transfers between devices: 290 us -> none  [the longest x1 152 us: on_device(): grad_rows = lax.all_gather(grad_two, 'row', axis=0, tiled=True)]
    psum x1 -> x0, waiting for transfers between devices: 263 us -> none  [on_device(): sum_one, sum_two = lax.psum((weight_one, weight_two), ('row', 'col'))]
    all_to_all x0 -> x3, blocking collectives: none -> 137 us  [exchange(): return lax.all_to_all(blocks, axis, 0, 0, tiled=True)]
    all_to_all x0 -> x1, waiting for transfers between devices: none -> 49.1 us  [exchange(): return lax.all_to_all(blocks, axis, 0, 0, tiled=True)]
    dot_general x13 -> x5, matrix products: 36.2 us -> 1.4 us  [the longest x1 0.75 us: on_device(): output = f32(sums[:, :feat], weight2).astype(jnp.bfloat16)]
    pallas_call x0 -> x2, Pallas kernels: none -> 31.3 us  [tile_products(): pl.pallas_call(functools.partial(tile_kernel, transposed), out_shape=jax....]
    all_gather x2 -> x1, blocking collectives: 59.9 us -> 30.3 us  [on_device(): lax.all_gather(terms * (1.0 / math.sqrt(node_total)), 'col', axis=0, tile...]
  transfers between devices with their start and end apart: 7 -> 1, of which waited for: 7 -> 1; matrix products, arithmetic and copies ran while one was open for 5% -> 0% of each run, Pallas kernels for 0% -> 0%
where the time goes in v1:
time: 272 us; the launch traced here: 271 us
  blocking collectives  167 us (61%)
  waiting for transfers between devices  49.1 us (18%)
  Pallas kernels  31.3 us (12%)
  starting transfers between devices  14 us (5%)
  local copies, waits for them, and re-layouts  3.15 us (1%)
  other arithmetic  2.8 us (1%)
    all_to_all x3, blocking collectives, exchange(): return lax.all_to_all(blocks, axis, 0, 0, tiled=True)  137 us
    all_to_all x1, waiting for transfers between devices, exchange(): return lax.all_to_all(blocks, axis, 0, 0, tiled=True)  49.1 us
    pallas_call x2, Pallas kernels, tile_products(): pl.pallas_call(functools.partial(tile_kernel, transposed), out_shape=jax....  31.3 us
    all_gather x1, blocking collectives, on_device(): lax.all_gather(terms * (1.0 / math.sqrt(node_total)), 'col', axis=0, tile...  30.3 us
    all_to_all x1, starting transfers between devices, exchange(): return lax.all_to_all(blocks, axis, 0, 0, tiled=True)  14 us
  transfers between devices with their start and end apart: 1, of which 1 were waited for; matrix products, arithmetic and copies ran while one was open for 0% of the time, Pallas kernels for 0%

profile of v1, /device:TPU:56, one launch (start us, length us, event | category | flops | bytes accessed | tf_op | source)
XLA Modules:
  0.0 270.9 jit_solution(14931522459860510917)
XLA Ops:
  0.6 0.0 copy-start
  0.6 0.8 pad_maximum_fusion.3
  1.4 1.5 broadcast_in_dim.12
  3.0 0.0 copy-start.1
  3.0 0.0 copy-start.2
  3.0 14.0 %all-to-all-start = ((bf16[32,128,256]{2,1,0:T(8,128)(2,1)}), bf16[32,128,256]{2,1,0:T(8,128)(2,1)}, u32[]{:S(2)}, u32[]{:S(2)}) async-start(bf16[32,128,256]{2,1,0:T(8,128)(2,1)} %broadcast_in_dim.12), calls=%async_computation | async-start | bytes 4194304 | tf_op jit(solution)/shard_map/all_to_all | solution.py:52
  17.7 49.1 %all-to-all-done.panel_ref = bf16[32,128,256]{2,1,0:T(8,128)(2,1)} async-done(((bf16[32,128,256]{2,1,0:T(8,128)(2,1)}), bf16[32,128,256]{2,1,0:T(8,128)(2,1)}, u32[]{:S(2)}, u32[]{:S(2)}) %all-to-all-start) | async-done | bytes 2097184 | tf_op jit(solution)/shard_map/all_to_all | solution.py:52
  66.8 0.0 copy-done.1
  66.8 0.0 copy-done.2
  66.8 14.1 %shard_map.102 = bf16[16,128,256]{2,1,0:T(8,128)(2,1)S(1)} custom-call(s32[2,96]{1,0:T(2,128)S(1)} %bitcast.24, s32[1]{0:T(128)} %bitcast.20.count_ref, bf16[96,128,128]{2,1,0:T(8,128)(2,1)S(1)} %bitcast.22, bf16[32,128,256]{2,1,0:T(8,128)(2,1)} %all-to-all-done.panel_ref), custom_call_target="tpu_custom_call" | custom-call | flops 805306368 | bytes 6291456 | tf_op jit(solution)/shard_map/pallas_call | solution.py:36
  80.9 0.0 copy-start.3
  80.9 25.2 %all_to_all.20 = bf16[16,128,256]{2,1,0:T(8,128)(2,1)} all-to-all(bf16[16,128,256]{2,1,0:T(8,128)(2,1)S(1)} %shard_map.102), channel_id=1, replica_groups=mesh['row'=32,'col'=16] {'col'}, dimensions={0} | all-to-all | bytes 2097152 | tf_op jit(solution)/shard_map/all_to_all | solution.py:52
  106.2 1.4 reduce.1
  107.5 0.0 copy-done
  107.5 0.2 multiply_convert_fusion
  107.8 0.0 copy-done.3
  107.8 0.1 fusion
  107.9 0.1 convolution_convert_fusion
  108.1 0.2 convolution_bitcast_fusion.1
  108.3 0.1 convolution_bitcast_fusion
  108.4 0.1 copy.12
  108.6 0.1 broadcast_in_dim.13
  108.7 0.1 pad_maximum_fusion.1
  108.8 33.9 %all_to_all.21 = bf16[16,144,256]{2,1,0:T(8,128)(2,1)S(1)} all-to-all(bf16[16,144,256]{2,1,0:T(8,128)(2,1)S(1)} %pad_maximum_fusion.1), channel_id=1, replica_groups=mesh['row'=32,'col'=16] {'col'}, dimensions={0} | all-to-all | bytes 2359296 | tf_op jit(solution)/shard_map/all_to_all | solution.py:52
  142.7 0.1 slice.52.panel_ref
  142.8 17.2 %shard_map.103 = bf16[32,128,256]{2,1,0:T(8,128)(2,1)S(1)} custom-call(s32[2,96]{1,0:T(2,128)S(1)} %bitcast.25, s32[1]{0:T(128)} %bitcast.21.count_ref, bf16[96,128,128]{2,1,0:T(8,128)(2,1)S(1)} %bitcast.23, bf16[16,128,256]{2,1,0:T(8,128)(2,1)S(1)} %slice.52.panel_ref), custom_call_target="tpu_custom_call" | custom-call | flops 805306368 | bytes 6291456 | tf_op jit(solution)/shard_map/pallas_call | solution.py:36
  160.0 0.2 pad_maximum_fusion
  160.2 78.0 %all_to_all.22 = bf16[32,144,256]{2,1,0:T(8,128)(2,1)S(1)} all-to-all(bf16[32,144,256]{2,1,0:T(8,128)(2,1)S(1)} %pad_maximum_fusion), channel_id=1, replica_groups=mesh['row'=32,'col'=16] {'row'}, dimensions={0} | all-to-all | bytes 4718592 | tf_op jit(solution)/shard_map/all_to_all | solution.py:52
  238.2 0.3 slice_reduce_fusion
  238.5 0.6 slice_bitcast_fusion
  239.1 0.8 fusion.1
  239.9 30.3 %all_gather.3 = f32[128,256]{1,0:T(8,128)S(1)} all-gather(f32[8,256]{1,0:T(8,128)S(1)} %add_multiply_fusion), channel_id=1, replica_groups=mesh['row'=32,'col'=16] {'col'}, dimensions={0}, use_global_device_ids=true | all-gather | bytes 139264 | tf_op jit(solution)/shard_map/all_gather | solution.py:109
  270.3 0.7 fusion.10
  (8 shorter events, 0.1 us)
Async XLA Ops:
  0.6 106.9 %copy-start = (bf16[128,128]{1,0:T(8,128)(2,1)S(1)}, bf16[128,128]{1,0:T(8,128)(2,1)}, u32[]{:S(2)}) copy-start(bf16[128,128]{1,0:T(8,128)(2,1)} %param.8) | copy-start | bytes 98308
  3.0 63.8 %copy-start.1 = (bf16[1,1,96,128,128]{4,3,2,1,0:T(8,128)(2,1)S(1)}, bf16[1,1,96,128,128]{4,3,2,1,0:T(8,128)(2,1)}, u32[]{:S(2)}) copy-start(bf16[1,1,96,128,128]{4,3,2,1,0:T(8,128)(2,1)} %param.10) | copy-start | bytes 9437188
  3.0 63.8 %copy-start.2 = (s32[1,1,2,96]{3,2,1,0:T(2,128)S(1)}, s32[1,1,2,96]{3,2,1,0:T(2,128)}, u32[]{:S(2)}) copy-start(s32[1,1,2,96]{3,2,1,0:T(2,128)} %param.11) | copy-start | bytes 2308
  3.0 63.8 %all-to-all-start = ((bf16[32,128,256]{2,1,0:T(8,128)(2,1)}), bf16[32,128,256]{2,1,0:T(8,128)(2,1)}, u32[]{:S(2)}, u32[]{:S(2)}) async-start(bf16[32,128,256]{2,1,0:T(8,128)(2,1)} %broadcast_in_dim.12), calls=%async_computation | async-start | bytes 4194304 | tf_op jit(solution)/shard_map/all_to_all | solution.py:52
  80.9 26.9 %copy-start.3 = (bf16[128,128]{1,0:T(8,128)(2,1)S(1)}, bf16[128,128]{1,0:T(8,128)(2,1)}, u32[]{:S(2)}) copy-start(bf16[128,128]{1,0:T(8,128)(2,1)} %param.9) | copy-start | bytes 98308

commit v2 on v1

v2 whole, which is shorter than its diff:
```python
import functools
import math

import jax
import jax.numpy as jnp
from jax import lax
from jax.experimental import pallas as pl
from jax.experimental.pallas import tpu as pltpu
from jax.sharding import Mesh, PartitionSpec as P

ROW = ("z", "yl")
COL = ("yh", "x", "c")
PLANE = ("yh", "x")
UNROLL = 16


def add_tiles(transposed, source_ref, target_ref, count_ref, tiles_ref, panel_ref, acc_ref):
    acc_ref[...] = jnp.zeros_like(acc_ref)
    spare = acc_ref.shape[0] - 1
    slots = tiles_ref.shape[0]
    unroll = math.gcd(slots, UNROLL)
    contract = (((0,), (0,)), ((), ())) if transposed else (((1,), (0,)), ((), ()))
    count = count_ref[0]

    def group(step, carry):
        for k in range(unroll):
            slot = step * unroll + k
            product = lax.dot_general(
                tiles_ref[slot],
                panel_ref[source_ref[slot]],
                contract,
                preferred_element_type=jnp.float32,
            )
            acc_ref[jnp.where(slot < count, target_ref[slot], spare)] += product
        return carry

    lax.fori_loop(0, (count + unroll - 1) // unroll, group, 0)


def forward_kernel(source_ref, target_ref, count_ref, tiles_ref, *refs):
    pieces, (keep_ref, send_ref, panel_ref, acc_ref) = refs[:-4], refs[-4:]
    n = pieces[0].shape[0]
    for i, piece in enumerate(pieces):
        panel_ref[i * n : (i + 1) * n] = piece[...]
    add_tiles(False, source_ref, target_ref, count_ref, tiles_ref, panel_ref, acc_ref)
    half = keep_ref.shape[0]
    keep_ref[...] = acc_ref[:half].astype(keep_ref.dtype)
    send_ref[...] = acc_ref[half : 2 * half].astype(send_ref.dtype)


def transposed_kernel(
    core_ref, source_ref, target_ref, count_ref, tiles_ref, mine_ref, theirs_ref, out_ref,
    panel_ref, acc_ref, term_ref,
):
    half, side = mine_ref.shape[0], tiles_ref.shape[1]
    panel_ref[:half] = mine_ref[:, :side]
    panel_ref[half:] = theirs_ref[:, :side]
    add_tiles(True, source_ref, target_ref, count_ref, tiles_ref, panel_ref, acc_ref)
    blocks = out_ref.shape[0]
    out_ref[:, :side] = acc_ref[:blocks].astype(out_ref.dtype)
    term_ref[...] = jnp.sum(mine_ref[:, side:].astype(jnp.float32), axis=0) + jnp.sum(
        theirs_ref[:, side:].astype(jnp.float32), axis=0
    )
    rows = term_ref.shape[0] // 2
    own = term_ref[pl.ds(pl.multiple_of(core_ref[0] * rows, rows), rows), :]
    out_ref[:, side:] = jnp.broadcast_to(own[None], (blocks,) + own.shape).astype(out_ref.dtype)


VMEM = pl.BlockSpec(memory_space=pltpu.VMEM)
SMEM = pl.BlockSpec(memory_space=pltpu.SMEM)
PARAMS = pltpu.CompilerParams(vmem_limit_bytes=40 << 20)


def cost(tiles, width, moved):
    return pl.CostEstimate(
        flops=2 * tiles.size * width, transcendentals=0, bytes_accessed=2 * (tiles.size + moved)
    )


def exchange(blocks, axes):
    return lax.all_to_all(blocks, axes, 0, 0, tiled=True)


def swap_cores(value):
    return lax.ppermute(value, "c", [(0, 1), (1, 0)])


def on_device(features, weight1, weight2, tile_values, tile_coords, tile_count, out_grad):
    tiles = tile_values[0, 0]
    block_rows, block_cols = tile_coords[0, 0, 0], tile_coords[0, 0, 1]
    count = tile_count[0]
    side, feat = features.shape[1], features.shape[2]
    z_n, yl_n = lax.axis_size("z"), lax.axis_size("yl")
    rows_n, cols_n = z_n * yl_n, lax.axis_size(COL)
    plane_n = cols_n // 2
    core = lax.axis_index("c").astype(jnp.int32)
    z = lax.axis_index("z").astype(jnp.int32)
    width = 2 * feat
    node_total = side * rows_n * cols_n
    dot = functools.partial(jnp.dot, preferred_element_type=jnp.float32)
    contract = (((0,), (0,)), ((), ()))

    both = jnp.concatenate([features[0], out_grad[0]], axis=1)
    own = lax.all_gather(both, "yl", axis=0, tiled=True).reshape(yl_n, side, width)
    up = [(i, (i + 1) % z_n) for i in range(z_n)]
    down = [(i, (i - 1) % z_n) for i in range(z_n)]
    behind, ahead = [own], [own]
    for step in range(z_n // 2):
        behind.append(lax.ppermute(behind[-1], "z", up))
        if step < z_n // 2 - 1:
            ahead.append(lax.ppermute(ahead[-1], "z", down))
    pieces = ahead + behind[:0:-1]

    source = ((block_cols // yl_n - z) % z_n) * yl_n + block_cols % yl_n
    row_place = ((block_rows % 2) ^ core) * plane_n + block_rows // 2
    half = jax.ShapeDtypeStruct((plane_n, side, width), jnp.bfloat16)
    keep, send = pl.pallas_call(
        forward_kernel,
        out_shape=(half, half),
        in_specs=[SMEM] * 3 + [VMEM] * (1 + len(pieces)),
        out_specs=(VMEM, VMEM),
        scratch_shapes=[
            pltpu.VMEM((rows_n, side, width), jnp.bfloat16),
            pltpu.VMEM((cols_n + 1, side, width), jnp.float32),
        ],
        compiler_params=PARAMS,
        cost_estimate=cost(tiles, width, (rows_n + cols_n) * side * width),
    )(source, row_place, count, tiles, *pieces)

    pair = keep.astype(jnp.float32) + swap_cores(send).astype(jnp.float32)
    got = exchange(pair.astype(jnp.bfloat16), PLANE)
    sums = jnp.sum(got.astype(jnp.float32), axis=0)
    agg_one = sums[:, :feat].astype(jnp.bfloat16)
    agg_grad = sums[:, feat:].astype(jnp.bfloat16)
    pre_one = dot(agg_one, weight1)
    sigmoid = jax.nn.sigmoid(pre_one)
    hidden = (pre_one * sigmoid).astype(jnp.bfloat16)
    grad_hidden = dot(agg_grad, weight2.T)
    grad_pre = (grad_hidden * (sigmoid * (1.0 + pre_one * (1.0 - sigmoid)))).astype(jnp.bfloat16)
    grad_one = dot(grad_pre, weight1.T).astype(jnp.bfloat16)
    term_one = lax.dot_general(agg_one, grad_pre, contract, preferred_element_type=jnp.float32)
    term_two = lax.dot_general(hidden, agg_grad, contract, preferred_element_type=jnp.float32)

    both = jnp.concatenate([hidden, grad_one], axis=1)
    slices = jnp.concatenate([term_one, term_two], axis=1).astype(jnp.bfloat16)
    slices = slices.reshape(plane_n, feat // plane_n, width)
    sent = jnp.concatenate(
        [jnp.broadcast_to(both[None], (plane_n, side, width)), slices], axis=1
    )
    mine = exchange(sent, PLANE)
    theirs = swap_cores(mine)
    slice_rows = feat // cols_n
    parts = pl.pallas_call(
        transposed_kernel,
        out_shape=jax.ShapeDtypeStruct((rows_n, side + slice_rows, width), jnp.bfloat16),
        in_specs=[SMEM] * 4 + [VMEM] * 3,
        out_specs=VMEM,
        scratch_shapes=[
            pltpu.VMEM((cols_n, side, width), jnp.bfloat16),
            pltpu.VMEM((rows_n + 1, side, width), jnp.float32),
            pltpu.VMEM((2 * slice_rows, width), jnp.float32),
        ],
        compiler_params=PARAMS,
        cost_estimate=cost(tiles, width, (rows_n + cols_n) * side * width),
    )(core.reshape(1), row_place, block_cols, count, tiles, mine, theirs)

    got = exchange(parts, ROW)
    sums = jnp.sum(got[:, :side].astype(jnp.float32), axis=0).astype(jnp.bfloat16)
    terms = jnp.sum(got[:, side:].astype(jnp.float32), axis=0)
    output = dot(sums[:, :feat], weight2).astype(jnp.bfloat16)
    grad_features = sums[:, feat:]
    terms = terms * (1.0 / math.sqrt(node_total))
    weights = exchange(jnp.broadcast_to(terms[None], (cols_n,) + terms.shape), COL)
    weights = weights.reshape(feat, width)
    return (output[None], grad_features[None], weights[:, :feat], weights[:, feat:])


def solution(mesh):
    fine = Mesh(mesh.devices.reshape(8, 4, 2, 4, 2), ("z", "yl", "yh", "x", "c"))
    placed = (
        P(COL, ROW, None),
        P(),
        P(),
        P(ROW, COL, None, None, None),
        P(ROW, COL, None, None),
        P(ROW, COL),
        P(COL, ROW, None),
    )
    return jax.shard_map(
        on_device,
        mesh=fine,
        in_specs=placed,
        out_specs=(P(COL, ROW, None), P(COL, ROW, None), P(), P()),
        check_vma=False,
    )
```

time: 272 us -> 205 us (0.75)
  the two profiles are of different devices: /device:TPU:56 before, /device:TPU:1 now
where the time goes in v2:
time: 205 us; the launch traced here: 204 us
  blocking collectives  117 us (57%)
  starting transfers between devices  49.9 us (24%)
  waiting for transfers between devices  22.6 us (11%)
  Pallas kernels  4.82 us (2%)
  local copies, waits for them, and re-layouts  3.98 us (2%)
  other arithmetic  2.17 us (1%)
    all_to_all x3, blocking collectives, exchange(): return lax.all_to_all(blocks, axes, 0, 0, tiled=True)  105 us
    ppermute x2, starting transfers between devices, swap_cores(): return lax.ppermute(value, 'c', [(0, 1), (1, 0)])  17.8 us
    ppermute x3, starting transfers between devices, on_device(): ahead.append(lax.ppermute(ahead[-1], 'z', down))  17.7 us
    all_gather x1, blocking collectives, on_device(): lax.all_gather(both, 'yl', axis=0, tiled=True).reshape(yl_n, side, width)  12.1 us
    ppermute x4, starting transfers between devices, on_device(): behind.append(lax.ppermute(behind[-1], 'z', up))  11 us
    ppermute x4, waiting for transfers between devices, on_device(): behind.append(lax.ppermute(behind[-1], 'z', up))  10.9 us
    all_to_all x1, waiting for transfers between devices, exchange(): return lax.all_to_all(blocks, axes, 0, 0, tiled=True)  8.6 us
  transfers between devices with their start and end apart: 10, of which 7 were waited for; matrix products, arithmetic and copies ran while one was open for 1% of the time, Pallas kernels for 0%

profile of v2, /device:TPU:1, one launch (start us, length us, event | category | flops | bytes accessed | tf_op | source)
XLA Modules:
  0.0 203.9 jit_solution(16553951632932236188)
XLA Ops:
  0.6 0.0 copy-start
  0.6 0.8 pad_maximum_fusion
  1.4 12.1 %all_gather.3 = bf16[512,256]{1,0:T(8,128)(2,1)S(1)} all-gather(bf16[128,256]{1,0:T(8,128)(2,1)S(1)} %pad_maximum_fusion), channel_id=1, replica_groups=mesh['z'=8,'yl'=4,'yh'=2,'x'=4,'c'=2] {'yl'}, dimensions={0}, use_global_device_ids=true | all-gather | bytes 327680 | tf_op jit(solution)/shard_map/all_gather | solution.py:104
  13.5 5.2 %collective-permute-start.3 = (bf16[4,128,256]{2,1,0:T(8,128)(2,1)S(1)}, bf16[4,128,256]{2,1,0:T(8,128)(2,1)S(1)}, u32[]{:S(2)}, u32[]{:S(2)}) collective-permute-start(bf16[4,128,256]{2,1,0:T(8,128)(2,1)S(1)} %bitcast.41), channel_id=1, source_target_pairs={{0,64},{64,128},{128,192},{192,256},{256,320},{320,384},{384,448},... | collective-permute-start | bytes 786440 | tf_op jit(solution)/shard_map/ppermute | solution.py:109
  18.7 8.6 %collective-permute-start = (bf16[4,128,256]{2,1,0:T(8,128)(2,1)S(1)}, bf16[4,128,256]{2,1,0:T(8,128)(2,1)S(1)}, u32[]{:S(2)}, u32[]{:S(2)}) collective-permute-start(bf16[4,128,256]{2,1,0:T(8,128)(2,1)S(1)} %bitcast.42), channel_id=1, source_target_pairs={{0,448},{64,0},{128,64},{192,128},{256,192},{320,256},{384,320},{4... | collective-permute-start | bytes 786440 | tf_op jit(solution)/shard_map/ppermute | solution.py:111
  27.3 2.3 %collective-permute-done.3.refs_7_ = bf16[4,128,256]{2,1,0:T(8,128)(2,1)S(1)} collective-permute-done((bf16[4,128,256]{2,1,0:T(8,128)(2,1)S(1)}, bf16[4,128,256]{2,1,0:T(8,128)(2,1)S(1)}, u32[]{:S(2)}, u32[]{:S(2)}) %collective-permute-start.3) | collective-permute-done | bytes 262176 | tf_op jit(solution)/shard_map/ppermute | solution.py:109
  29.6 1.9 collective-permute-start.4
  31.6 0.0 collective-permute-done.refs_1_
  31.6 4.6 %collective-permute-start.1 = (bf16[4,128,256]{2,1,0:T(8,128)(2,1)S(1)}, bf16[4,128,256]{2,1,0:T(8,128)(2,1)S(1)}, u32[]{:S(2)}, u32[]{:S(2)}) collective-permute-start(bf16[4,128,256]{2,1,0:T(8,128)(2,1)S(1)} %collective-permute-done.refs_1_), channel_id=1, source_target_pairs={{0,448},{64,0},{128,64},{192,128},{256,192},{320,256},{384,320},{4... | collective-permute-start | bytes 786440 | tf_op jit(solution)/shard_map/ppermute | solution.py:111
  36.1 1.8 collective-permute-done.4.refs_6_
  38.0 1.9 collective-permute-start.5
  39.9 0.0 collective-permute-done.1.refs_2_
  39.9 4.6 %collective-permute-start.2 = (bf16[4,128,256]{2,1,0:T(8,128)(2,1)S(1)}, bf16[4,128,256]{2,1,0:T(8,128)(2,1)S(1)}, u32[]{:S(2)}, u32[]{:S(2)}) collective-permute-start(bf16[4,128,256]{2,1,0:T(8,128)(2,1)S(1)} %collective-permute-done.1.refs_2_), channel_id=1, source_target_pairs={{0,448},{64,0},{128,64},{192,128},{256,192},{320,256},{384,320},{4... | collective-permute-start | bytes 786440 | tf_op jit(solution)/shard_map/ppermute | solution.py:111
  44.5 1.8 collective-permute-done.5.refs_5_
  46.3 1.9 collective-permute-start.6
  48.8 0.8 fusion.8
  49.6 0.0 collective-permute-done.2.refs_3_
  49.6 5.0 %collective-permute-done.6.refs_4_ = bf16[4,128,256]{2,1,0:T(8,128)(2,1)S(1)} collective-permute-done((bf16[4,128,256]{2,1,0:T(8,128)(2,1)S(1)}, bf16[4,128,256]{2,1,0:T(8,128)(2,1)S(1)}, u32[]{:S(2)}, u32[]{:S(2)}) %collective-permute-start.6) | collective-permute-done | bytes 262176 | tf_op jit(solution)/shard_map/ppermute | solution.py:109
  54.6 0.0 copy-start.1
  54.6 1.9 copy-done.1
  56.5 2.3 %shard_map.102 = (bf16[8,128,256]{2,1,0:T(8,128)(2,1)S(1)}, bf16[8,128,256]{2,1,0:T(8,128)(2,1)S(1)}) custom-call(s32[96]{0:T(128)S(1)} %get-tuple-element.10.source_ref, s32[96]{0:T(128)S(1)} %get-tuple-element.11.target_ref.source_ref, s32[1]{0:T(128)} %bitcast.37.count_ref, bf16[96,128,128]{2,1,0:T(8,128)(2,1)S(1)} %bitcast.39, ...), custom_call_target="tpu_custom_call" | custom-call | flops 805306368 | bytes 6291456 | tf_op jit(solution)/shard_map/pallas_call | solution.py:117
  58.8 0.0 copy-start.3
  58.8 8.4 %collective-permute-start.7 = (bf16[8,128,256]{2,1,0:T(8,128)(2,1)S(1)}, bf16[8,128,256]{2,1,0:T(8,128)(2,1)S(1)}, u32[]{:S(2)}, u32[]{:S(2)}) collective-permute-start(bf16[8,128,256]{2,1,0:T(8,128)(2,1)S(1)} %get-tuple-element.7), channel_id=1, source_target_pairs={{0,1},{1,0},{2,3},{3,2},{4,5},{5,4},{6,7},{7,6},{8,9},{9,8},{10,11... | collective-permute-start | bytes 1572872 | tf_op jit(solution)/shard_map/ppermute | solution.py:85
  67.2 1.5 collective-permute-done.7
  68.7 0.1 add_convert_fusion
  68.8 24.7 %all_to_all.20 = bf16[8,128,256]{2,1,0:T(8,128)(2,1)S(1)} all-to-all(bf16[8,128,256]{2,1,0:T(8,128)(2,1)S(1)} %add_convert_fusion), channel_id=1, replica_groups=mesh['z'=8,'yl'=4,'yh'=2,'x'=4,'c'=2] {'yh','x'}, dimensions={0} | all-to-all | bytes 1048576 | tf_op jit(solution)/shard_map/all_to_all | solution.py:81
  93.5 0.1 reduce.1
  93.6 0.0 copy-done
  93.6 0.0 copy-start.4
  93.6 0.0 copy-start.2
  93.6 0.2 multiply_convert_fusion
  93.8 0.0 copy-done.3
  93.8 0.1 fusion
  94.0 0.2 convolution_convert_fusion.3
  94.2 0.1 convolution_convert_fusion
  94.3 0.1 convolution_convert_fusion.2
  94.5 0.1 copy.12
  94.7 14.9 %all_to_all.21.mine_ref = bf16[8,144,256]{2,1,0:T(8,128)(2,1)S(1)} all-to-all(bf16[8,144,256]{2,1,0:T(8,128)(2,1)S(1)} %maximum_maximum_fusion), channel_id=1, replica_groups=mesh['z'=8,'yl'=4,'yh'=2,'x'=4,'c'=2] {'yh','x'}, dimensions={0} | all-to-all | bytes 1179648 | tf_op jit(solution)/shard_map/all_to_all | solution.py:81
  109.6 9.4 %collective-permute-start.8 = (bf16[8,144,256]{2,1,0:T(8,128)(2,1)S(1)}, bf16[8,144,256]{2,1,0:T(8,128)(2,1)S(1)}, u32[]{:S(2)}, u32[]{:S(2)}) collective-permute-start(bf16[8,144,256]{2,1,0:T(8,128)(2,1)S(1)} %all_to_all.21.mine_ref), channel_id=1, source_target_pairs={{0,1},{1,0},{2,3},{3,2},{4,5},{5,4},{6,7},{7,6},{8,9},{9,8},{10,11... | collective-permute-start | bytes 1769480 | tf_op jit(solution)/shard_map/ppermute | solution.py:85
  119.0 0.0 copy-done.4
  119.0 1.6 collective-permute-done.8.theirs_ref
  120.6 0.0 copy-done.2
  120.6 2.5 %shard_map.103 = bf16[32,136,256]{2,1,0:T(8,128)(2,1)S(1)} custom-call(s32[1]{0:T(128)} %bitcast.core_ref, s32[96]{0:T(128)S(1)} %get-tuple-element.11.target_ref.source_ref, s32[96]{0:T(128)S(1)} %slice_bitcast_fusion.1.target_ref, s32[1]{0:T(128)} %bitcast.38.count_ref, bf16[96,128,128]{2,1,0:T(8,128)(2,1)S(1)} %bitcast.40, ...), custom_call_target="tpu_custom_call" | custom-call | flops 805306368 | bytes 6291456 | tf_op jit(solution)/shard_map/pallas_call | solution.py:153
  123.2 65.7 %all_to_all.22 = bf16[32,136,256]{2,1,0:T(8,128)(2,1)S(1)} all-to-all(bf16[32,136,256]{2,1,0:T(8,128)(2,1)S(1)} %shard_map.103), channel_id=1, replica_groups=mesh['z'=8,'yl'=4,'yh'=2,'x'=4,'c'=2] {'z','yl'}, dimensions={0} | all-to-all | bytes 4456448 | tf_op jit(solution)/shard_map/all_to_all | solution.py:81
  189.0 0.6 broadcast_in_dim.21
  189.6 3.4 %all-to-all-start.3 = ((f32[16,8,256]{2,1,0:T(8,128)}), f32[16,8,256]{2,1,0:T(8,128)S(1)}, u32[]{:S(2)}, u32[]{:S(2)}) async-start(f32[16,8,256]{2,1,0:T(8,128)} %broadcast_in_dim.21), calls=%async_computation.3 | async-start | bytes 262144 | tf_op jit(solution)/shard_map/all_to_all | solution.py:81
  193.0 0.3 slice_reduce_fusion
  193.3 0.8 fusion.1
  194.1 0.6 slice_bitcast_fusion
  194.7 8.6 %all-to-all-done.3 = f32[16,8,256]{2,1,0:T(8,128)S(1)} async-done(((f32[16,8,256]{2,1,0:T(8,128)}), f32[16,8,256]{2,1,0:T(8,128)S(1)}, u32[]{:S(2)}, u32[]{:S(2)}) %all-to-all-start.3) | async-done | bytes 131104 | tf_op jit(solution)/shard_map/all_to_all | solution.py:81
  203.3 0.7 fusion.14
  (6 shorter events, 0.1 us)
Async XLA Ops:
  0.6 92.9 %copy-start = (bf16[128,128]{1,0:T(8,128)(2,1)S(1)}, bf16[128,128]{1,0:T(8,128)(2,1)}, u32[]{:S(2)}) copy-start(bf16[128,128]{1,0:T(8,128)(2,1)} %param.8) | copy-start | bytes 98308
  13.5 16.1 %collective-permute-start.3 = (bf16[4,128,256]{2,1,0:T(8,128)(2,1)S(1)}, bf16[4,128,256]{2,1,0:T(8,128)(2,1)S(1)}, u32[]{:S(2)}, u32[]{:S(2)}) collective-permute-start(bf16[4,128,256]{2,1,0:T(8,128)(2,1)S(1)} %bitcast.41), channel_id=1, source_target_pairs={{0,64},{64,128},{128,192},{192,256},{256,320},{320,384},{384,448},... | collective-permute-start | bytes 786440 | tf_op jit(solution)/shard_map/ppermute | solution.py:109
  18.7 12.8 %collective-permute-start = (bf16[4,128,256]{2,1,0:T(8,128)(2,1)S(1)}, bf16[4,128,256]{2,1,0:T(8,128)(2,1)S(1)}, u32[]{:S(2)}, u32[]{:S(2)}) collective-permute-start(bf16[4,128,256]{2,1,0:T(8,128)(2,1)S(1)} %bitcast.42), channel_id=1, source_target_pairs={{0,448},{64,0},{128,64},{192,128},{256,192},{320,256},{384,320},{4... | collective-permute-start | bytes 786440 | tf_op jit(solution)/shard_map/ppermute | solution.py:111
  29.6 8.3 %collective-permute-start.4 = (bf16[4,128,256]{2,1,0:T(8,128)(2,1)S(1)}, bf16[4,128,256]{2,1,0:T(8,128)(2,1)S(1)}, u32[]{:S(2)}, u32[]{:S(2)}) collective-permute-start(bf16[4,128,256]{2,1,0:T(8,128)(2,1)S(1)} %collective-permute-done.3.refs_7_), channel_id=1, source_target_pairs={{0,64},{64,128},{128,192},{192,256},{256,320},{320,384},{384,448},... | collective-permute-start | bytes 786440 | tf_op jit(solution)/shard_map/ppermute | solution.py:109
  31.6 8.3 %collective-permute-start.1 = (bf16[4,128,256]{2,1,0:T(8,128)(2,1)S(1)}, bf16[4,128,256]{2,1,0:T(8,128)(2,1)S(1)}, u32[]{:S(2)}, u32[]{:S(2)}) collective-permute-start(bf16[4,128,256]{2,1,0:T(8,128)(2,1)S(1)} %collective-permute-done.refs_1_), channel_id=1, source_target_pairs={{0,448},{64,0},{128,64},{192,128},{256,192},{320,256},{384,320},{4... | collective-permute-start | bytes 786440 | tf_op jit(solution)/shard_map/ppermute | solution.py:111
  38.0 8.3 %collective-permute-start.5 = (bf16[4,128,256]{2,1,0:T(8,128)(2,1)S(1)}, bf16[4,128,256]{2,1,0:T(8,128)(2,1)S(1)}, u32[]{:S(2)}, u32[]{:S(2)}) collective-permute-start(bf16[4,128,256]{2,1,0:T(8,128)(2,1)S(1)} %collective-permute-done.4.refs_6_), channel_id=1, source_target_pairs={{0,64},{64,128},{128,192},{192,256},{256,320},{320,384},{384,448},... | collective-permute-start | bytes 786440 | tf_op jit(solution)/shard_map/ppermute | solution.py:109
  39.9 9.7 %collective-permute-start.2 = (bf16[4,128,256]{2,1,0:T(8,128)(2,1)S(1)}, bf16[4,128,256]{2,1,0:T(8,128)(2,1)S(1)}, u32[]{:S(2)}, u32[]{:S(2)}) collective-permute-start(bf16[4,128,256]{2,1,0:T(8,128)(2,1)S(1)} %collective-permute-done.1.refs_2_), channel_id=1, source_target_pairs={{0,448},{64,0},{128,64},{192,128},{256,192},{320,256},{384,320},{4... | collective-permute-start | bytes 786440 | tf_op jit(solution)/shard_map/ppermute | solution.py:111
  46.3 8.3 %collective-permute-start.6 = (bf16[4,128,256]{2,1,0:T(8,128)(2,1)S(1)}, bf16[4,128,256]{2,1,0:T(8,128)(2,1)S(1)}, u32[]{:S(2)}, u32[]{:S(2)}) collective-permute-start(bf16[4,128,256]{2,1,0:T(8,128)(2,1)S(1)} %collective-permute-done.5.refs_5_), channel_id=1, source_target_pairs={{0,64},{64,128},{128,192},{192,256},{256,320},{320,384},{384,448},... | collective-permute-start | bytes 786440 | tf_op jit(solution)/shard_map/ppermute | solution.py:109
  54.6 1.9 copy-start.1
  58.8 35.1 %copy-start.3 = (bf16[128,128]{1,0:T(8,128)(2,1)S(1)}, bf16[128,128]{1,0:T(8,128)(2,1)}, u32[]{:S(2)}) copy-start(bf16[128,128]{1,0:T(8,128)(2,1)} %param.9) | copy-start | bytes 98308
  58.8 9.9 %collective-permute-start.7 = (bf16[8,128,256]{2,1,0:T(8,128)(2,1)S(1)}, bf16[8,128,256]{2,1,0:T(8,128)(2,1)S(1)}, u32[]{:S(2)}, u32[]{:S(2)}) collective-permute-start(bf16[8,128,256]{2,1,0:T(8,128)(2,1)S(1)} %get-tuple-element.7), channel_id=1, source_target_pairs={{0,1},{1,0},{2,3},{3,2},{4,5},{5,4},{6,7},{7,6},{8,9},{9,8},{10,11... | collective-permute-start | bytes 1572872 | tf_op jit(solution)/shard_map/ppermute | solution.py:85
  93.6 25.4 %copy-start.4 = (s32[1,1,2,96]{3,2,1,0:T(2,128)S(1)}, s32[1,1,2,96]{3,2,1,0:T(2,128)}, u32[]{:S(2)}) copy-start(s32[1,1,2,96]{3,2,1,0:T(2,128)} %param.11) | copy-start | bytes 2308
  93.6 27.0 %copy-start.2 = (bf16[1,1,96,128,128]{4,3,2,1,0:T(8,128)(2,1)S(1)}, bf16[1,1,96,128,128]{4,3,2,1,0:T(8,128)(2,1)}, u32[]{:S(2)}) copy-start(bf16[1,1,96,128,128]{4,3,2,1,0:T(8,128)(2,1)} %param.10) | copy-start | bytes 9437188
  109.6 11.0 %collective-permute-start.8 = (bf16[8,144,256]{2,1,0:T(8,128)(2,1)S(1)}, bf16[8,144,256]{2,1,0:T(8,128)(2,1)S(1)}, u32[]{:S(2)}, u32[]{:S(2)}) collective-permute-start(bf16[8,144,256]{2,1,0:T(8,128)(2,1)S(1)} %all_to_all.21.mine_ref), channel_id=1, source_target_pairs={{0,1},{1,0},{2,3},{3,2},{4,5},{5,4},{6,7},{7,6},{8,9},{9,8},{10,11... | collective-permute-start | bytes 1769480 | tf_op jit(solution)/shard_map/ppermute | solution.py:85
  189.6 13.7 %all-to-all-start.3 = ((f32[16,8,256]{2,1,0:T(8,128)}), f32[16,8,256]{2,1,0:T(8,128)S(1)}, u32[]{:S(2)}, u32[]{:S(2)}) async-start(f32[16,8,256]{2,1,0:T(8,128)} %broadcast_in_dim.21), calls=%async_computation.3 | async-start | bytes 262144 | tf_op jit(solution)/shard_map/all_to_all | solution.py:81

commit v3 on v2

v3 whole, which is shorter than its diff:
```python
import functools
import math

import jax
import jax.numpy as jnp
from jax import lax
from jax.experimental import pallas as pl
from jax.experimental.pallas import tpu as pltpu
from jax.sharding import Mesh, PartitionSpec as P

ROW = ("z", "yl")
COL = ("yh", "x", "c")
SLICES = ("x", "yh", "c")
UNROLL = 16


def add_tiles(transposed, first, count, source_ref, target_ref, tiles_ref, panel_ref, acc_ref):
    spare = acc_ref.shape[0] - 1
    contract = (((0,), (0,)), ((), ())) if transposed else (((1,), (0,)), ((), ()))
    for k in range(tiles_ref.shape[0]):
        slot = first + k
        product = lax.dot_general(
            tiles_ref[k],
            panel_ref[source_ref[slot]],
            contract,
            preferred_element_type=jnp.float32,
        )
        acc_ref[jnp.where(slot < count, target_ref[slot], spare)] += product


def forward_kernel(source_ref, target_ref, count_ref, tiles_ref, *refs):
    pieces, (keep_ref, send_ref, held_ref, panel_ref, acc_ref, sems) = refs[:-6], refs[-6:]
    steps = sems.shape[0]
    group = held_ref.shape[0] // steps
    copies = [
        pltpu.make_async_copy(
            tiles_ref.at[pl.ds(i * group, group)], held_ref.at[pl.ds(i * group, group)], sems.at[i]
        )
        for i in range(steps)
    ]
    for copy in copies:
        copy.start()
    acc_ref[...] = jnp.zeros_like(acc_ref)
    n = pieces[0].shape[0]
    for i, piece in enumerate(pieces):
        panel_ref[i * n : (i + 1) * n] = piece[...]
    count = count_ref[0]
    for i, copy in enumerate(copies):
        copy.wait()

        @pl.when(i * group < count)
        def _():
            tiles = held_ref.at[pl.ds(i * group, group)]
            add_tiles(False, i * group, count, source_ref, target_ref, tiles, panel_ref, acc_ref)

    half = keep_ref.shape[0]
    keep_ref[...] = acc_ref[:half].astype(keep_ref.dtype)
    send_ref[...] = acc_ref[half : 2 * half].astype(send_ref.dtype)


def transposed_kernel(
    part_ref, source_ref, target_ref, count_ref, tiles_ref, mine_ref, theirs_ref,
    out_ref, terms_ref, panel_ref, acc_ref, sum_ref, rounded_ref, sems,
):
    side = tiles_ref.shape[1]
    acc_ref[...] = jnp.zeros_like(acc_ref)
    places = mine_ref.shape[0]
    held = panel_ref.shape[0] // (2 * places)
    for i, ref in enumerate((mine_ref, theirs_ref)):
        for k in range(held):
            for place in range(places):
                panel_ref[(i * places + place) * held + k] = ref[place, k * side : (k + 1) * side]
    rest = held * side
    sum_ref[...] = jnp.sum(mine_ref[:, rest:].astype(jnp.float32), axis=0) + jnp.sum(
        theirs_ref[:, rest:].astype(jnp.float32), axis=0
    )
    rows = terms_ref.shape[1]
    own = sum_ref[pl.ds(pl.multiple_of(part_ref[0] * rows, rows), rows), :]
    terms_ref[...] = jnp.broadcast_to(own[None], terms_ref.shape)

    count = count_ref[0]
    slots = tiles_ref.shape[0]
    group = math.gcd(slots, UNROLL)
    for first in range(0, slots, group):

        @pl.when(first < count)
        def _():
            tiles = tiles_ref.at[pl.ds(first, group)]
            add_tiles(True, first, count, source_ref, target_ref, tiles, panel_ref, acc_ref)

    steps = sems.shape[0]
    blocks = rounded_ref.shape[0] // steps
    copies = []
    for i in range(steps):
        window = pl.ds(i * blocks, blocks)
        rounded_ref[window] = acc_ref[window].astype(rounded_ref.dtype)
        copies.append(
            pltpu.make_async_copy(rounded_ref.at[window], out_ref.at[window], sems.at[i])
        )
        copies[-1].start()
    for copy in copies:
        copy.wait()


VMEM = pl.BlockSpec(memory_space=pltpu.VMEM)
SMEM = pl.BlockSpec(memory_space=pltpu.SMEM)
HBM = pl.BlockSpec(memory_space=pltpu.HBM)
PARAMS = pltpu.CompilerParams(vmem_limit_bytes=40 << 20)


def cost(tiles, width, moved):
    return pl.CostEstimate(
        flops=2 * tiles.size * width, transcendentals=0, bytes_accessed=2 * (tiles.size + moved)
    )


def exchange(blocks, axes):
    return lax.all_to_all(blocks, axes, 0, 0, tiled=True)


def swap_cores(value):
    return lax.ppermute(value, "c", [(0, 1), (1, 0)])


def on_device(features, weight1, weight2, tile_values, tile_coords, tile_count, out_grad):
    tiles = tile_values[0, 0]
    block_rows, block_cols = tile_coords[0, 0, 0], tile_coords[0, 0, 1]
    count = tile_count[0]
    side, feat = features.shape[1], features.shape[2]
    z_n, yl_n = lax.axis_size("z"), lax.axis_size("yl")
    rows_n, cols_n = z_n * yl_n, lax.axis_size(COL)
    x_n, yh_n = lax.axis_size("x"), lax.axis_size("yh")
    half_n = cols_n // 2
    core = lax.axis_index("c").astype(jnp.int32)
    z = lax.axis_index("z").astype(jnp.int32)
    width = 2 * feat
    node_total = side * rows_n * cols_n
    dot = functools.partial(jnp.dot, preferred_element_type=jnp.float32)
    contract = (((0,), (0,)), ((), ()))

    both = jnp.concatenate([features[0], out_grad[0]], axis=1)
    own = lax.all_gather(both, "yl", axis=0, tiled=True).reshape(yl_n, side, width)
    up = [(i, (i + 1) % z_n) for i in range(z_n)]
    down = [(i, (i - 1) % z_n) for i in range(z_n)]
    behind, ahead = [own], [own]
    for step in range(z_n // 2):
        behind.append(lax.ppermute(behind[-1], "z", up))
        if step < z_n // 2 - 1:
            ahead.append(lax.ppermute(ahead[-1], "z", down))
    pieces = ahead + behind[:0:-1]

    source = ((block_cols // yl_n - z) % z_n) * yl_n + block_cols % yl_n
    row_place = (
        ((block_rows % 2) ^ core) * half_n
        + (block_rows // 2 % x_n) * yh_n
        + block_rows // (2 * x_n)
    )
    half = jax.ShapeDtypeStruct((half_n, side, width), jnp.bfloat16)
    keep, send = pl.pallas_call(
        forward_kernel,
        out_shape=(half, half),
        in_specs=[SMEM] * 3 + [HBM] + [VMEM] * len(pieces),
        out_specs=(VMEM, VMEM),
        scratch_shapes=[
            pltpu.VMEM(tiles.shape, jnp.bfloat16),
            pltpu.VMEM((rows_n, side, width), jnp.bfloat16),
            pltpu.VMEM((cols_n + 1, side, width), jnp.float32),
            pltpu.SemaphoreType.DMA((tiles.shape[0] // math.gcd(tiles.shape[0], UNROLL),)),
        ],
        compiler_params=PARAMS,
        cost_estimate=cost(tiles, width, (rows_n + cols_n) * side * width),
    )(source, row_place, count, pltpu.with_memory_space_constraint(tiles, pltpu.HBM), *pieces)

    pair = keep.astype(jnp.float32) + swap_cores(send).astype(jnp.float32)
    got = exchange(pair.astype(jnp.bfloat16), "x").reshape(x_n, yh_n * side, width)
    sums = jnp.sum(got.astype(jnp.float32), axis=0).astype(jnp.bfloat16)
    swapped = lax.ppermute(sums, "yh", [(0, 1), (1, 0)])
    sums = sums.astype(jnp.float32) + swapped.astype(jnp.float32)
    agg_one = sums[:, :feat].astype(jnp.bfloat16)
    agg_grad = sums[:, feat:].astype(jnp.bfloat16)
    pre_one = dot(agg_one, weight1)
    sigmoid = jax.nn.sigmoid(pre_one)
    hidden = (pre_one * sigmoid).astype(jnp.bfloat16)
    grad_hidden = dot(agg_grad, weight2.T)
    grad_pre = (grad_hidden * (sigmoid * (1.0 + pre_one * (1.0 - sigmoid)))).astype(jnp.bfloat16)
    grad_one = dot(grad_pre, weight1.T).astype(jnp.bfloat16)
    term_one = lax.dot_general(agg_one, grad_pre, contract, preferred_element_type=jnp.float32)
    term_two = lax.dot_general(hidden, agg_grad, contract, preferred_element_type=jnp.float32)

    both = jnp.concatenate([hidden, grad_one], axis=1)
    slices = jnp.concatenate([term_one, term_two], axis=1).astype(jnp.bfloat16)
    slices = slices.reshape(x_n, feat // x_n, width)
    sent = jnp.concatenate(
        [jnp.broadcast_to(both[None], (x_n,) + both.shape), slices], axis=1
    )
    mine = exchange(sent, "x")
    theirs = swap_cores(mine)
    part = lax.axis_index("yh").astype(jnp.int32) * 2 + core
    parts, terms = pl.pallas_call(
        transposed_kernel,
        out_shape=(
            pltpu.HBM((rows_n, side, width), jnp.bfloat16),
            jax.ShapeDtypeStruct((rows_n, feat // cols_n, width), jnp.float32),
        ),
        in_specs=[SMEM] * 4 + [VMEM] * 3,
        out_specs=(HBM, VMEM),
        scratch_shapes=[
            pltpu.VMEM((cols_n, side, width), jnp.bfloat16),
            pltpu.VMEM((rows_n + 1, side, width), jnp.float32),
            pltpu.VMEM((feat // x_n, width), jnp.float32),
            pltpu.VMEM((rows_n, side, width), jnp.bfloat16),
            pltpu.SemaphoreType.DMA((z_n,)),
        ],
        compiler_params=PARAMS,
        cost_estimate=cost(tiles, width, (rows_n + cols_n) * side * width),
    )(part.reshape(1), row_place, block_cols, count, tiles, mine, theirs)

    sums = lax.psum_scatter(parts, "z", scatter_dimension=0, tiled=True)
    terms = jnp.sum(exchange(terms, ROW), axis=0) * (1.0 / math.sqrt(node_total))
    weights = exchange(jnp.broadcast_to(terms[None], (cols_n,) + terms.shape), SLICES)
    sums = jnp.sum(exchange(sums, "yl").astype(jnp.float32), axis=0).astype(jnp.bfloat16)
    output = dot(sums[:, :feat], weight2).astype(jnp.bfloat16)
    grad_features = sums[:, feat:]
    weights = weights.reshape(feat, width)
    return (output[None], grad_features[None], weights[:, :feat], weights[:, feat:])


def solution(mesh):
    fine = Mesh(mesh.devices.reshape(8, 4, 2, 4, 2), ("z", "yl", "yh", "x", "c"))
    placed = (
        P(COL, ROW, None),
        P(),
        P(),
        P(ROW, COL, None, None, None),
        P(ROW, COL, None, None),
        P(ROW, COL),
        P(COL, ROW, None),
    )
    return jax.shard_map(
        on_device,
        mesh=fine,
        in_specs=placed,
        out_specs=(P(COL, ROW, None), P(COL, ROW, None), P(), P()),
        check_vma=False,
    )
```

time: 205 us -> 188 us (0.917)
  the two profiles are of different devices: /device:TPU:1 before, /device:TPU:56 now
where the time goes in v3:
time: 188 us; the launch traced here: 185 us
  blocking collectives  71.7 us (38%)
  starting transfers between devices  43.7 us (23%)
  waiting for transfers between devices  39.7 us (21%)
  between operations  15 us (8%)
  Pallas kernels  10.3 us (5%)
  other arithmetic  1.94 us (1%)
    all_to_all x4, blocking collectives, exchange(): return lax.all_to_all(blocks, axes, 0, 0, tiled=True)  57.8 us
    ppermute x3, starting transfers between devices, on_device(): ahead.append(lax.ppermute(ahead[-1], 'z', down))  18.9 us
    all_gather x1, blocking collectives, on_device(): lax.all_gather(both, 'yl', axis=0, tiled=True).reshape(yl_n, side, width)  14 us
    ppermute x4, waiting for transfers between devices, on_device(): behind.append(lax.ppermute(behind[-1], 'z', up))  13.4 us
    reduce_scatter x1, waiting for transfers between devices, on_device(): sums = lax.psum_scatter(parts, 'z', scatter_dimension=0, tiled=True)  10.7 us
    ppermute x4, starting transfers between devices, on_device(): behind.append(lax.ppermute(behind[-1], 'z', up))  10 us
    ppermute x1, waiting for transfers between devices, on_device(): swapped = lax.ppermute(sums, 'yh', [(0, 1), (1, 0)])  7 us
    pallas_call x1, Pallas kernels, on_device(): pl.pallas_call(transposed_kernel, out_shape=(pltpu.HBM((rows_n, side, wid...  5.92 us
  transfers between devices with their start and end apart: 12, of which 9 were waited for; matrix products, arithmetic and copies ran while one was open for 1% of the time, Pallas kernels for 0%

profile of v3, /device:TPU:56, one launch (start us, length us, event | category | flops | bytes accessed | tf_op | source)
XLA Modules:
  0.0 185.5 jit_solution(1967544513462907508)
XLA Ops:
  7.2 0.0 copy-start
  7.2 0.0 reduce-scatter.2.cloned.1.call-start
  7.2 0.8 pad_maximum_fusion.1
  8.0 14.0 %all_gather.3 = bf16[512,256]{1,0:T(8,128)(2,1)S(1)} all-gather(bf16[128,256]{1,0:T(8,128)(2,1)S(1)} %pad_maximum_fusion.1), channel_id=1, replica_groups=mesh['z'=8,'yl'=4,'yh'=2,'x'=4,'c'=2] {'yl'}, dimensions={0}, use_global_device_ids=true | all-gather | bytes 327680 | tf_op jit(solution)/shard_map/all_gather | solution.py:142
  22.0 4.3 %collective-permute-start.3 = (bf16[4,128,256]{2,1,0:T(8,128)(2,1)S(1)}, bf16[4,128,256]{2,1,0:T(8,128)(2,1)S(1)}, u32[]{:S(2)}, u32[]{:S(2)}) collective-permute-start(bf16[4,128,256]{2,1,0:T(8,128)(2,1)S(1)} %bitcast.47), channel_id=1, source_target_pairs={{0,64},{64,128},{128,192},{192,256},{256,320},{320,384},{384,448},... | collective-permute-start | bytes 786440 | tf_op jit(solution)/shard_map/ppermute | solution.py:147
  26.3 8.6 %collective-permute-start = (bf16[4,128,256]{2,1,0:T(8,128)(2,1)S(1)}, bf16[4,128,256]{2,1,0:T(8,128)(2,1)S(1)}, u32[]{:S(2)}, u32[]{:S(2)}) collective-permute-start(bf16[4,128,256]{2,1,0:T(8,128)(2,1)S(1)} %bitcast.48), channel_id=1, source_target_pairs={{0,448},{64,0},{128,64},{192,128},{256,192},{320,256},{384,320},{4... | collective-permute-start | bytes 786440 | tf_op jit(solution)/shard_map/ppermute | solution.py:149
  34.9 2.5 %collective-permute-done.3.refs_7_ = bf16[4,128,256]{2,1,0:T(8,128)(2,1)S(1)} collective-permute-done((bf16[4,128,256]{2,1,0:T(8,128)(2,1)S(1)}, bf16[4,128,256]{2,1,0:T(8,128)(2,1)S(1)}, u32[]{:S(2)}, u32[]{:S(2)}) %collective-permute-start.3) | collective-permute-done | bytes 262176 | tf_op jit(solution)/shard_map/ppermute | solution.py:147
  37.4 1.9 %collective-permute-start.4 = (bf16[4,128,256]{2,1,0:T(8,128)(2,1)S(1)}, bf16[4,128,256]{2,1,0:T(8,128)(2,1)S(1)}, u32[]{:S(2)}, u32[]{:S(2)}) collective-permute-start(bf16[4,128,256]{2,1,0:T(8,128)(2,1)S(1)} %collective-permute-done.3.refs_7_), channel_id=1, source_target_pairs={{0,64},{64,128},{128,192},{192,256},{256,320},{320,384},{384,448},... | collective-permute-start | bytes 786440 | tf_op jit(solution)/shard_map/ppermute | solution.py:147
  39.3 0.0 collective-permute-done.refs_1_
  39.3 5.1 %collective-permute-start.1 = (bf16[4,128,256]{2,1,0:T(8,128)(2,1)S(1)}, bf16[4,128,256]{2,1,0:T(8,128)(2,1)S(1)}, u32[]{:S(2)}, u32[]{:S(2)}) collective-permute-start(bf16[4,128,256]{2,1,0:T(8,128)(2,1)S(1)} %collective-permute-done.refs_1_), channel_id=1, source_target_pairs={{0,448},{64,0},{128,64},{192,128},{256,192},{320,256},{384,320},{4... | collective-permute-start | bytes 786440 | tf_op jit(solution)/shard_map/ppermute | solution.py:149
  44.4 2.4 %collective-permute-done.4.refs_6_ = bf16[4,128,256]{2,1,0:T(8,128)(2,1)S(1)} collective-permute-done((bf16[4,128,256]{2,1,0:T(8,128)(2,1)S(1)}, bf16[4,128,256]{2,1,0:T(8,128)(2,1)S(1)}, u32[]{:S(2)}, u32[]{:S(2)}) %collective-permute-start.4) | collective-permute-done | bytes 262176 | tf_op jit(solution)/shard_map/ppermute | solution.py:147
  46.8 1.9 %collective-permute-start.5 = (bf16[4,128,256]{2,1,0:T(8,128)(2,1)S(1)}, bf16[4,128,256]{2,1,0:T(8,128)(2,1)S(1)}, u32[]{:S(2)}, u32[]{:S(2)}) collective-permute-start(bf16[4,128,256]{2,1,0:T(8,128)(2,1)S(1)} %collective-permute-done.4.refs_6_), channel_id=1, source_target_pairs={{0,64},{64,128},{128,192},{192,256},{256,320},{320,384},{384,448},... | collective-permute-start | bytes 786440 | tf_op jit(solution)/shard_map/ppermute | solution.py:147
  48.8 0.0 collective-permute-done.1.refs_2_
  48.8 5.1 %collective-permute-start.2 = (bf16[4,128,256]{2,1,0:T(8,128)(2,1)S(1)}, bf16[4,128,256]{2,1,0:T(8,128)(2,1)S(1)}, u32[]{:S(2)}, u32[]{:S(2)}) collective-permute-start(bf16[4,128,256]{2,1,0:T(8,128)(2,1)S(1)} %collective-permute-done.1.refs_2_), channel_id=1, source_target_pairs={{0,448},{64,0},{128,64},{192,128},{256,192},{320,256},{384,320},{4... | collective-permute-start | bytes 786440 | tf_op jit(solution)/shard_map/ppermute | solution.py:149
  53.9 2.4 %collective-permute-done.5.refs_5_ = bf16[4,128,256]{2,1,0:T(8,128)(2,1)S(1)} collective-permute-done((bf16[4,128,256]{2,1,0:T(8,128)(2,1)S(1)}, bf16[4,128,256]{2,1,0:T(8,128)(2,1)S(1)}, u32[]{:S(2)}, u32[]{:S(2)}) %collective-permute-start.5) | collective-permute-done | bytes 262176 | tf_op jit(solution)/shard_map/ppermute | solution.py:147
  56.3 1.9 %collective-permute-start.6 = (bf16[4,128,256]{2,1,0:T(8,128)(2,1)S(1)}, bf16[4,128,256]{2,1,0:T(8,128)(2,1)S(1)}, u32[]{:S(2)}, u32[]{:S(2)}) collective-permute-start(bf16[4,128,256]{2,1,0:T(8,128)(2,1)S(1)} %collective-permute-done.5.refs_5_), channel_id=1, source_target_pairs={{0,64},{64,128},{128,192},{192,256},{256,320},{320,384},{384,448},... | collective-permute-start | bytes 786440 | tf_op jit(solution)/shard_map/ppermute | solution.py:147
  58.9 0.8 fusion.8
  59.7 0.0 collective-permute-done.2.refs_3_
  59.7 6.1 %collective-permute-done.6.refs_4_ = bf16[4,128,256]{2,1,0:T(8,128)(2,1)S(1)} collective-permute-done((bf16[4,128,256]{2,1,0:T(8,128)(2,1)S(1)}, bf16[4,128,256]{2,1,0:T(8,128)(2,1)S(1)}, u32[]{:S(2)}, u32[]{:S(2)}) %collective-permute-start.6) | collective-permute-done | bytes 262176 | tf_op jit(solution)/shard_map/ppermute | solution.py:147
  65.8 4.4 %shard_map.102 = (bf16[8,128,256]{2,1,0:T(8,128)(2,1)S(1)}, bf16[8,128,256]{2,1,0:T(8,128)(2,1)S(1)}) custom-call(s32[96]{0:T(128)S(1)} %get-tuple-element.14.source_ref, s32[96]{0:T(128)S(1)} %get-tuple-element.15.target_ref.source_ref, s32[1]{0:T(128)} %bitcast.43.count_ref, bf16[96,128,128]{2,1,0:T(8,128)(2,1)} %bitcast.45, ...), custom_call_target="tpu_custom_call" | custom-call | flops 805306368 | bytes 6291456 | tf_op jit(solution)/shard_map/pallas_call | solution.py:159
  70.1 1.9 %collective-permute-start.7 = (bf16[8,128,256]{2,1,0:T(8,128)(2,1)S(1)}, bf16[8,128,256]{2,1,0:T(8,128)(2,1)S(1)}, u32[]{:S(2)}, u32[]{:S(2)}) collective-permute-start(bf16[8,128,256]{2,1,0:T(8,128)(2,1)S(1)} %get-tuple-element.9), channel_id=1, source_target_pairs={{0,1},{1,0},{2,3},{3,2},{4,5},{5,4},{6,7},{7,6},{8,9},{9,8},{10,11... | collective-permute-start | bytes 1572872 | tf_op jit(solution)/shard_map/ppermute | solution.py:122
  72.1 1.9 %collective-permute-done.7 = bf16[8,128,256]{2,1,0:T(8,128)(2,1)S(1)} collective-permute-done((bf16[8,128,256]{2,1,0:T(8,128)(2,1)S(1)}, bf16[8,128,256]{2,1,0:T(8,128)(2,1)S(1)}, u32[]{:S(2)}, u32[]{:S(2)}) %collective-permute-start.7) | collective-permute-done | bytes 524320 | tf_op jit(solution)/shard_map/ppermute | solution.py:122
  73.9 0.1 add_convert_fusion
  74.1 0.0 copy-start.2
  74.1 13.9 %all_to_all.25 = bf16[8,128,256]{2,1,0:T(8,128)(2,1)S(1)} all-to-all(bf16[8,128,256]{2,1,0:T(8,128)(2,1)S(1)} %add_convert_fusion), channel_id=1, replica_groups=mesh['z'=8,'yl'=4,'yh'=2,'x'=4,'c'=2] {'x'}, dimensions={0} | all-to-all | bytes 1048576 | tf_op jit(solution)/shard_map/all_to_all | solution.py:118
  88.0 0.1 bitcast_reduce_fusion
  88.0 5.7 %collective-permute-start.8 = (bf16[256,256]{1,0:T(8,128)(2,1)S(1)}, bf16[256,256]{1,0:T(8,128)(2,1)S(1)}, u32[]{:S(2)}, u32[]{:S(2)}) collective-permute-start(bf16[256,256]{1,0:T(8,128)(2,1)S(1)} %bitcast_reduce_fusion), channel_id=1, source_target_pairs={{0,8},{8,0},{1,9},{9,1},{2,10},{10,2},{3,11},{11,3},{4,12},{12,4},... | collective-permute-start | bytes 393224 | tf_op jit(solution)/shard_map/ppermute | solution.py:177
  93.8 7.0 %collective-permute-done.8 = bf16[256,256]{1,0:T(8,128)(2,1)S(1)} collective-permute-done((bf16[256,256]{1,0:T(8,128)(2,1)S(1)}, bf16[256,256]{1,0:T(8,128)(2,1)S(1)}, u32[]{:S(2)}, u32[]{:S(2)}) %collective-permute-start.8) | collective-permute-done | bytes 131104 | tf_op jit(solution)/shard_map/ppermute | solution.py:177
  100.8 0.0 copy-done
  100.8 0.2 multiply_convert_fusion
  101.0 0.0 copy-done.2
  101.1 0.2 fusion
  101.2 0.2 convolution_convert_fusion.3
  101.4 0.2 convolution_convert_fusion
  101.6 0.1 convolution_convert_fusion.2
  101.7 0.0 copy-start.1
  101.8 0.1 copy.12
  101.9 0.0 copy-start.3
  102.0 13.0 %all_to_all.26.mine_ref = bf16[4,288,256]{2,1,0:T(8,128)(2,1)} all-to-all(bf16[4,288,256]{2,1,0:T(8,128)(2,1)S(1)} %maximum_maximum_fusion), channel_id=1, replica_groups=mesh['z'=8,'yl'=4,'yh'=2,'x'=4,'c'=2] {'x'}, dimensions={0} | all-to-all | bytes 1179648 | tf_op jit(solution)/shard_map/all_to_all | solution.py:118
  115.0 1.9 %collective-permute-start.9 = (bf16[4,288,256]{2,1,0:T(8,128)(2,1)}, bf16[4,288,256]{2,1,0:T(8,128)(2,1)}, u32[]{:S(2)}, u32[]{:S(2)}) collective-permute-start(bf16[4,288,256]{2,1,0:T(8,128)(2,1)} %all_to_all.26.mine_ref), channel_id=1, source_target_pairs={{0,1},{1,0},{2,3},{3,2},{4,5},{5,4},{6,7},{7,6},{8,9},{9,8},{10,11... | collective-permute-start | bytes 1769480 | tf_op jit(solution)/shard_map/ppermute | solution.py:122
  116.9 0.0 copy-done.3
  116.9 2.3 %collective-permute-done.9.theirs_ref = bf16[4,288,256]{2,1,0:T(8,128)(2,1)} collective-permute-done((bf16[4,288,256]{2,1,0:T(8,128)(2,1)}, bf16[4,288,256]{2,1,0:T(8,128)(2,1)}, u32[]{:S(2)}, u32[]{:S(2)}) %collective-permute-start.9) | collective-permute-done | bytes 589856 | tf_op jit(solution)/shard_map/ppermute | solution.py:122
  119.2 0.0 copy-done.1
  119.2 5.9 %shard_map.103 = (bf16[32,128,256]{2,1,0:T(8,128)(2,1)}, f32[32,8,256]{2,1,0:T(8,128)S(1)}) custom-call(s32[1]{0:T(128)} %bitcast.part_ref, s32[96]{0:T(128)S(1)} %get-tuple-element.15.target_ref.source_ref, s32[96]{0:T(128)S(1)} %slice_bitcast_fusion.1.target_ref, s32[1]{0:T(128)} %bitcast.44.count_ref, bf16[96,128,128]{2,1,0:T(8,128)(2,1)S(1)} %bitcast.46, ...), custom_call_target="tpu_custom_call" | custom-call | flops 805306368 | bytes 6291456 | tf_op jit(solution)/shard_map/pallas_call | solution.py:199
  125.1 0.0 reduce-scatter.2.cloned.1.call-update
  125.2 17.7 %all_to_all.27 = f32[32,8,256]{2,1,0:T(8,128)S(1)} all-to-all(f32[32,8,256]{2,1,0:T(8,128)S(1)} %get-tuple-element.11), channel_id=1, replica_groups=mesh['z'=8,'yl'=4,'yh'=2,'x'=4,'c'=2] {'z','yl'}, dimensions={0} | all-to-all | bytes 524288 | tf_op jit(solution)/shard_map/all_to_all | solution.py:118
  142.9 13.2 %all_to_all.28 = f32[16,8,256]{2,1,0:T(8,128)S(1)} all-to-all(f32[16,8,256]{2,1,0:T(8,128)S(1)} %broadcast_in_dim.21), channel_id=1, replica_groups=mesh['z'=8,'yl'=4,'yh'=2,'x'=4,'c'=2] {'x','yh','c'}, dimensions={0} | all-to-all | bytes 262144 | tf_op jit(solution)/shard_map/all_to_all | solution.py:118
  156.1 10.7 %reduce-scatter.2.cloned.1.call-done = bf16[4,128,256]{2,1,0:T(8,128)(2,1)} async-done(((bf16[32,128,256]{2,1,0:T(8,128)(2,1)}), bf16[4,128,256]{2,1,0:T(8,128)(2,1)}) %reduce-scatter.2.cloned.1.call-update) | async-done | bytes 262160 | tf_op jit(solution)/shard_map/reduce_scatter | solution.py:218
  166.8 5.3 %all-to-all-start.2 = ((bf16[4,128,256]{2,1,0:T(8,128)(2,1)}), bf16[4,128,256]{2,1,0:T(8,128)(2,1)S(1)}, u32[]{:S(2)}, u32[]{:S(2)}) async-start(bf16[4,128,256]{2,1,0:T(8,128)(2,1)} %reduce-scatter.2.cloned.1.call-done), calls=%async_computation.3 | async-start | bytes 524288 | tf_op jit(solution)/shard_map/all_to_all | solution.py:118
  172.1 0.7 fusion.17
  172.7 4.5 %all-to-all-done.2 = bf16[4,128,256]{2,1,0:T(8,128)(2,1)S(1)} async-done(((bf16[4,128,256]{2,1,0:T(8,128)(2,1)}), bf16[4,128,256]{2,1,0:T(8,128)(2,1)S(1)}, u32[]{:S(2)}, u32[]{:S(2)}) %all-to-all-start.2) | async-done | bytes 262176 | tf_op jit(solution)/shard_map/all_to_all | solution.py:118
  177.2 0.6 slice_bitcast_fusion
  177.9 0.8 fusion.1
  (9 shorter events, 0.2 us)
Async XLA Ops:
  7.2 93.6 %copy-start = (bf16[128,128]{1,0:T(8,128)(2,1)S(1)}, bf16[128,128]{1,0:T(8,128)(2,1)}, u32[]{:S(2)}) copy-start(bf16[128,128]{1,0:T(8,128)(2,1)} %param.8) | copy-start | bytes 98308
  7.2 159.6 %reduce-scatter.2.cloned.1.call-start = ((), (), s32[]{:S(2)}) async-start(), calls=%async_computation.6 | async-start | bytes 2359296 | tf_op jit(solution)/shard_map/reduce_scatter | solution.py:218
  22.0 15.4 %collective-permute-start.3 = (bf16[4,128,256]{2,1,0:T(8,128)(2,1)S(1)}, bf16[4,128,256]{2,1,0:T(8,128)(2,1)S(1)}, u32[]{:S(2)}, u32[]{:S(2)}) collective-permute-start(bf16[4,128,256]{2,1,0:T(8,128)(2,1)S(1)} %bitcast.47), channel_id=1, source_target_pairs={{0,64},{64,128},{128,192},{192,256},{256,320},{320,384},{384,448},... | collective-permute-start | bytes 786440 | tf_op jit(solution)/shard_map/ppermute | solution.py:147
  26.3 13.0 %collective-permute-start = (bf16[4,128,256]{2,1,0:T(8,128)(2,1)S(1)}, bf16[4,128,256]{2,1,0:T(8,128)(2,1)S(1)}, u32[]{:S(2)}, u32[]{:S(2)}) collective-permute-start(bf16[4,128,256]{2,1,0:T(8,128)(2,1)S(1)} %bitcast.48), channel_id=1, source_target_pairs={{0,448},{64,0},{128,64},{192,128},{256,192},{320,256},{384,320},{4... | collective-permute-start | bytes 786440 | tf_op jit(solution)/shard_map/ppermute | solution.py:149
  37.4 9.5 %collective-permute-start.4 = (bf16[4,128,256]{2,1,0:T(8,128)(2,1)S(1)}, bf16[4,128,256]{2,1,0:T(8,128)(2,1)S(1)}, u32[]{:S(2)}, u32[]{:S(2)}) collective-permute-start(bf16[4,128,256]{2,1,0:T(8,128)(2,1)S(1)} %collective-permute-done.3.refs_7_), channel_id=1, source_target_pairs={{0,64},{64,128},{128,192},{192,256},{256,320},{320,384},{384,448},... | collective-permute-start | bytes 786440 | tf_op jit(solution)/shard_map/ppermute | solution.py:147
  39.3 9.5 %collective-permute-start.1 = (bf16[4,128,256]{2,1,0:T(8,128)(2,1)S(1)}, bf16[4,128,256]{2,1,0:T(8,128)(2,1)S(1)}, u32[]{:S(2)}, u32[]{:S(2)}) collective-permute-start(bf16[4,128,256]{2,1,0:T(8,128)(2,1)S(1)} %collective-permute-done.refs_1_), channel_id=1, source_target_pairs={{0,448},{64,0},{128,64},{192,128},{256,192},{320,256},{384,320},{4... | collective-permute-start | bytes 786440 | tf_op jit(solution)/shard_map/ppermute | solution.py:149
  46.8 9.5 %collective-permute-start.5 = (bf16[4,128,256]{2,1,0:T(8,128)(2,1)S(1)}, bf16[4,128,256]{2,1,0:T(8,128)(2,1)S(1)}, u32[]{:S(2)}, u32[]{:S(2)}) collective-permute-start(bf16[4,128,256]{2,1,0:T(8,128)(2,1)S(1)} %collective-permute-done.4.refs_6_), channel_id=1, source_target_pairs={{0,64},{64,128},{128,192},{192,256},{256,320},{320,384},{384,448},... | collective-permute-start | bytes 786440 | tf_op jit(solution)/shard_map/ppermute | solution.py:147
  48.8 10.9 %collective-permute-start.2 = (bf16[4,128,256]{2,1,0:T(8,128)(2,1)S(1)}, bf16[4,128,256]{2,1,0:T(8,128)(2,1)S(1)}, u32[]{:S(2)}, u32[]{:S(2)}) collective-permute-start(bf16[4,128,256]{2,1,0:T(8,128)(2,1)S(1)} %collective-permute-done.1.refs_2_), channel_id=1, source_target_pairs={{0,448},{64,0},{128,64},{192,128},{256,192},{320,256},{384,320},{4... | collective-permute-start | bytes 786440 | tf_op jit(solution)/shard_map/ppermute | solution.py:149
  56.3 9.5 %collective-permute-start.6 = (bf16[4,128,256]{2,1,0:T(8,128)(2,1)S(1)}, bf16[4,128,256]{2,1,0:T(8,128)(2,1)S(1)}, u32[]{:S(2)}, u32[]{:S(2)}) collective-permute-start(bf16[4,128,256]{2,1,0:T(8,128)(2,1)S(1)} %collective-permute-done.5.refs_5_), channel_id=1, source_target_pairs={{0,64},{64,128},{128,192},{192,256},{256,320},{320,384},{384,448},... | collective-permute-start | bytes 786440 | tf_op jit(solution)/shard_map/ppermute | solution.py:147
  70.1 3.8 %collective-permute-start.7 = (bf16[8,128,256]{2,1,0:T(8,128)(2,1)S(1)}, bf16[8,128,256]{2,1,0:T(8,128)(2,1)S(1)}, u32[]{:S(2)}, u32[]{:S(2)}) collective-permute-start(bf16[8,128,256]{2,1,0:T(8,128)(2,1)S(1)} %get-tuple-element.9), channel_id=1, source_target_pairs={{0,1},{1,0},{2,3},{3,2},{4,5},{5,4},{6,7},{7,6},{8,9},{9,8},{10,11... | collective-permute-start | bytes 1572872 | tf_op jit(solution)/shard_map/ppermute | solution.py:122
  74.1 27.0 %copy-start.2 = (bf16[128,128]{1,0:T(8,128)(2,1)S(1)}, bf16[128,128]{1,0:T(8,128)(2,1)}, u32[]{:S(2)}) copy-start(bf16[128,128]{1,0:T(8,128)(2,1)} %param.9) | copy-start | bytes 98308
  88.0 12.7 %collective-permute-start.8 = (bf16[256,256]{1,0:T(8,128)(2,1)S(1)}, bf16[256,256]{1,0:T(8,128)(2,1)S(1)}, u32[]{:S(2)}, u32[]{:S(2)}) collective-permute-start(bf16[256,256]{1,0:T(8,128)(2,1)S(1)} %bitcast_reduce_fusion), channel_id=1, source_target_pairs={{0,8},{8,0},{1,9},{9,1},{2,10},{10,2},{3,11},{11,3},{4,12},{12,4},... | collective-permute-start | bytes 393224 | tf_op jit(solution)/shard_map/ppermute | solution.py:177
  101.7 17.5 %copy-start.1 = (bf16[1,1,96,128,128]{4,3,2,1,0:T(8,128)(2,1)S(1)}, bf16[1,1,96,128,128]{4,3,2,1,0:T(8,128)(2,1)}, u32[]{:S(2)}) copy-start(bf16[1,1,96,128,128]{4,3,2,1,0:T(8,128)(2,1)} %param.10) | copy-start | bytes 9437188
  101.9 15.0 %copy-start.3 = (s32[1,1,2,96]{3,2,1,0:T(2,128)S(1)}, s32[1,1,2,96]{3,2,1,0:T(2,128)}, u32[]{:S(2)}) copy-start(s32[1,1,2,96]{3,2,1,0:T(2,128)} %param.11) | copy-start | bytes 2308
  115.0 4.2 %collective-permute-start.9 = (bf16[4,288,256]{2,1,0:T(8,128)(2,1)}, bf16[4,288,256]{2,1,0:T(8,128)(2,1)}, u32[]{:S(2)}, u32[]{:S(2)}) collective-permute-start(bf16[4,288,256]{2,1,0:T(8,128)(2,1)} %all_to_all.26.mine_ref), channel_id=1, source_target_pairs={{0,1},{1,0},{2,3},{3,2},{4,5},{5,4},{6,7},{7,6},{8,9},{9,8},{10,11... | collective-permute-start | bytes 1769480 | tf_op jit(solution)/shard_map/ppermute | solution.py:122
  166.8 10.4 %all-to-all-start.2 = ((bf16[4,128,256]{2,1,0:T(8,128)(2,1)}), bf16[4,128,256]{2,1,0:T(8,128)(2,1)S(1)}, u32[]{:S(2)}, u32[]{:S(2)}) async-start(bf16[4,128,256]{2,1,0:T(8,128)(2,1)} %reduce-scatter.2.cloned.1.call-done), calls=%async_computation.3 | async-start | bytes 524288 | tf_op jit(solution)/shard_map/all_to_all | solution.py:118
Sparse Core Ops, SparseCore 0:
  125.3 41.4 reduce-scatter.1

commit v4 on v3

--- a/solution.py
+++ b/solution.py
@@ -10,7 +10,6 @@
 
 ROW = ("z", "yl")
 COL = ("yh", "x", "c")
-SLICES = ("x", "yh", "c")
 UNROLL = 16
 
 
@@ -59,9 +58,9 @@
 
 
 def transposed_kernel(
-    part_ref, source_ref, target_ref, count_ref, tiles_ref, mine_ref, theirs_ref,
-    out_ref, terms_ref, panel_ref, acc_ref, sum_ref, rounded_ref, sems,
+    source_ref, target_ref, count_ref, tiles_ref, mine_ref, theirs_ref, *refs
 ):
+    outs, (term_ref, panel_ref, acc_ref) = refs[:-3], refs[-3:]
     side = tiles_ref.shape[1]
     acc_ref[...] = jnp.zeros_like(acc_ref)
     places = mine_ref.shape[0]
@@ -71,12 +70,10 @@
             for place in range(places):
                 panel_ref[(i * places + place) * held + k] = ref[place, k * side : (k + 1) * side]
     rest = held * side
-    sum_ref[...] = jnp.sum(mine_ref[:, rest:].astype(jnp.float32), axis=0) + jnp.sum(
+    terms = jnp.sum(mine_ref[:, rest:].astype(jnp.float32), axis=0) + jnp.sum(
         theirs_ref[:, rest:].astype(jnp.float32), axis=0
     )
-    rows = terms_ref.shape[1]
-    own = sum_ref[pl.ds(pl.multiple_of(part_ref[0] * rows, rows), rows), :]
-    terms_ref[...] = jnp.broadcast_to(own[None], terms_ref.shape)
+    term_ref[...] = terms.astype(term_ref.dtype)
 
     count = count_ref[0]
     slots = tiles_ref.shape[0]
@@ -88,18 +85,33 @@
             tiles = tiles_ref.at[pl.ds(first, group)]
             add_tiles(True, first, count, source_ref, target_ref, tiles, panel_ref, acc_ref)
 
-    steps = sems.shape[0]
-    blocks = rounded_ref.shape[0] // steps
-    copies = []
-    for i in range(steps):
-        window = pl.ds(i * blocks, blocks)
-        rounded_ref[window] = acc_ref[window].astype(rounded_ref.dtype)
-        copies.append(
-            pltpu.make_async_copy(rounded_ref.at[window], out_ref.at[window], sems.at[i])
-        )
-        copies[-1].start()
-    for copy in copies:
-        copy.wait()
+    blocks = (acc_ref.shape[0] - 1) // len(outs)
+    rest = blocks * side
+    firsts = (len(outs) // 2 - 1, len(outs) // 2)
+    for k, out_ref in enumerate(outs):
+        for i in range(blocks):
+            out_ref[i * side : (i + 1) * side] = acc_ref[k * blocks + i].astype(out_ref.dtype)
+        if k in firsts:
+            out_ref[rest:] = term_ref[...]
+        elif k:
+            out_ref[rest:] = jnp.zeros_like(term_ref)
+
+
+def ring_sum_kernel(z_ref, own_ref, term_ref, *refs):
+    got, (out_ref, held_ref) = refs[:-2], refs[-2:]
+    blocks, side = out_ref.shape[0], own_ref.shape[0] // out_ref.shape[0]
+    places = len(got) + 1
+    rest = own_ref.shape[0]
+    held_ref[z_ref[0]] = term_ref[...]
+    for k, ref in enumerate(got):
+        held_ref[lax.rem(z_ref[0] + k + 1, places)] = ref[rest:]
+    terms = jnp.sum(held_ref[...].astype(jnp.float32), axis=0).astype(out_ref.dtype)
+    ahead, behind = got[places // 2 - 1], got[places // 2]
+    for i in range(blocks):
+        rows = pl.ds(i * side, side)
+        total = own_ref[rows].astype(jnp.float32) + ahead[rows].astype(jnp.float32)
+        out_ref[i, :side] = (total + behind[rows].astype(jnp.float32)).astype(out_ref.dtype)
+        out_ref[i, side:] = terms
 
 
 VMEM = pl.BlockSpec(memory_space=pltpu.VMEM)
@@ -116,6 +128,10 @@
 
 def exchange(blocks, axes):
     return lax.all_to_all(blocks, axes, 0, 0, tiled=True)
+
+
+def add(left, right):
+    return (left.astype(jnp.float32) + right.astype(jnp.float32)).astype(jnp.bfloat16)
 
 
 def swap_cores(value):
@@ -195,30 +211,47 @@
     )
     mine = exchange(sent, "x")
     theirs = swap_cores(mine)
-    part = lax.axis_index("yh").astype(jnp.int32) * 2 + core
-    parts, terms = pl.pallas_call(
+    term_rows = feat // x_n
+    message = jax.ShapeDtypeStruct((yl_n * side + term_rows, width), jnp.bfloat16)
+    *chunks, terms = pl.pallas_call(
         transposed_kernel,
         out_shape=(
-            pltpu.HBM((rows_n, side, width), jnp.bfloat16),
-            jax.ShapeDtypeStruct((rows_n, feat // cols_n, width), jnp.float32),
+            jax.ShapeDtypeStruct((yl_n * side, width), jnp.bfloat16),
+            *[message] * (z_n - 1),
+            jax.ShapeDtypeStruct((term_rows, width), jnp.bfloat16),
         ),
-        in_specs=[SMEM] * 4 + [VMEM] * 3,
-        out_specs=(HBM, VMEM),
+        in_specs=[SMEM] * 3 + [VMEM] * 3,
+        out_specs=(VMEM,) * (z_n + 1),
         scratch_shapes=[
             pltpu.VMEM((cols_n, side, width), jnp.bfloat16),
             pltpu.VMEM((rows_n + 1, side, width), jnp.float32),
-            pltpu.VMEM((feat // x_n, width), jnp.float32),
-            pltpu.VMEM((rows_n, side, width), jnp.bfloat16),
-            pltpu.SemaphoreType.DMA((z_n,)),
         ],
         compiler_params=PARAMS,
         cost_estimate=cost(tiles, width, (rows_n + cols_n) * side * width),
-    )(part.reshape(1), row_place, block_cols, count, tiles, mine, theirs)
-
-    sums = lax.psum_scatter(parts, "z", scatter_dimension=0, tiled=True)
-    terms = jnp.sum(exchange(terms, ROW), axis=0) * (1.0 / math.sqrt(node_total))
-    weights = exchange(jnp.broadcast_to(terms[None], (cols_n,) + terms.shape), SLICES)
-    sums = jnp.sum(exchange(sums, "yl").astype(jnp.float32), axis=0).astype(jnp.bfloat16)
+    )(row_place, source, count, tiles, mine, theirs)
+
+    middle = z_n // 2
+    ahead, behind = [], []
+    down_sum, up_sum = chunks[middle], chunks[middle - 1]
+    for step in range(middle):
+        ahead.append(lax.ppermute(down_sum, "z", down))
+        if step < middle - 1:
+            behind.append(lax.ppermute(up_sum, "z", up))
+            down_sum = add(ahead[-1], chunks[middle + 1 + step])
+        if step < middle - 2:
+            up_sum = add(behind[-1], chunks[middle - 2 - step])
+    sent = pl.pallas_call(
+        ring_sum_kernel,
+        out_shape=jax.ShapeDtypeStruct((yl_n, side + term_rows, width), jnp.bfloat16),
+        in_specs=[SMEM] + [VMEM] * (z_n + 1),
+        out_specs=VMEM,
+        scratch_shapes=[pltpu.VMEM((z_n, term_rows, width), jnp.bfloat16)],
+        compiler_params=PARAMS,
+    )(z.reshape(1), chunks[0], terms, *ahead, *behind[::-1])
+    got = exchange(sent, "yl")
+    terms = jnp.sum(got[:, side:].astype(jnp.float32), axis=0) * (1.0 / math.sqrt(node_total))
+    weights = exchange(jnp.broadcast_to(terms[None], (x_n,) + terms.shape), "x")
+    sums = jnp.sum(got[:, :side].astype(jnp.float32), axis=0).astype(jnp.bfloat16)
     output = dot(sums[:, :feat], weight2).astype(jnp.bfloat16)
     grad_features = sums[:, feat:]
     weights = weights.reshape(feat, width)

time: 188 us -> 180 us (0.957)
  starting transfers between devices: 43.7 us -> 64.9 us
  blocking collectives: 71.7 us -> 52.9 us
  between operations: 15 us -> 1.64 us
  waiting for transfers between devices: 39.7 us -> 48.5 us
  Pallas kernels: 10.3 us -> 4.83 us
    ppermute x0 -> x7, starting transfers between devices: none -> 22.7 us  [the longest x4 14 us: on_device(): ahead.append(lax.ppermute(down_sum, 'z', down))]
    ppermute x0 -> x7, waiting for transfers between devices: none -> 19.5 us  [the longest x4 19.3 us: on_device(): ahead.append(lax.ppermute(down_sum, 'z', down))]
    all_to_all x4 -> x3, blocking collectives: 57.8 us -> 38.9 us  [exchange(): return lax.all_to_all(blocks, axes, 0, 0, tiled=True)]
    reduce_scatter x1 -> x0, waiting for transfers between devices: 10.7 us -> none  [on_device(): sums = lax.psum_scatter(parts, 'z', scatter_dimension=0, tiled=True)]
    pallas_call x1 -> x2, Pallas kernels: 5.92 us -> 2.2 us  [the longest x1 2.07 us: on_device(): pl.pallas_call(transposed_kernel, out_shape=(jax.ShapeDtypeStruct((yl_n *...]
    all_to_all x1, starting transfers between devices: 5.3 us -> 3.32 us  [exchange(): return lax.all_to_all(blocks, axes, 0, 0, tiled=True)]
  transfers between devices with their start and end apart: 12 -> 18, of which waited for: 9 -> 13; matrix products, arithmetic and copies ran while one was open for 1% -> 1% of each run, Pallas kernels for 0% -> 0%
where the time goes in v4:
time: 180 us; the launch traced here: 179 us
  starting transfers between devices  64.9 us (36%)
  blocking collectives  52.9 us (29%)
  waiting for transfers between devices  48.5 us (27%)
  Pallas kernels  4.83 us (3%)
  other arithmetic  2.31 us (1%)
  local copies, waits for them, and re-layouts  2.11 us (1%)
    all_to_all x3, blocking collectives, exchange(): return lax.all_to_all(blocks, axes, 0, 0, tiled=True)  38.9 us
    ppermute x4, waiting for transfers between devices, on_device(): ahead.append(lax.ppermute(down_sum, 'z', down))  19.3 us
    ppermute x3, starting transfers between devices, on_device(): ahead.append(lax.ppermute(ahead[-1], 'z', down))  18.9 us
    all_gather x1, blocking collectives, on_device(): lax.all_gather(both, 'yl', axis=0, tiled=True).reshape(yl_n, side, width)  14 us
    ppermute x4, starting transfers between devices, on_device(): ahead.append(lax.ppermute(down_sum, 'z', down))  14 us
    ppermute x4, waiting for transfers between devices, on_device(): behind.append(lax.ppermute(behind[-1], 'z', up))  13.4 us
    ppermute x4, starting transfers between devices, on_device(): behind.append(lax.ppermute(behind[-1], 'z', up))  10 us
    ppermute x3, starting transfers between devices, on_device(): behind.append(lax.ppermute(up_sum, 'z', up))  8.77 us
  transfers between devices with their start and end apart: 18, of which 13 were waited for; matrix products, arithmetic and copies ran while one was open for 1% of the time, Pallas kernels for 0%

profile of v4, /device:TPU:56, one launch (start us, length us, event | category | flops | bytes accessed | tf_op | source)
XLA Modules:
  0.0 178.8 jit_solution(9749611002455096643)
XLA Ops:
  0.6 0.0 copy-start
  0.6 0.8 pad_maximum_fusion.1
  1.4 14.0 %all_gather.3 = bf16[512,256]{1,0:T(8,128)(2,1)S(1)} all-gather(bf16[128,256]{1,0:T(8,128)(2,1)S(1)} %pad_maximum_fusion.1), channel_id=1, replica_groups=mesh['z'=8,'yl'=4,'yh'=2,'x'=4,'c'=2] {'yl'}, dimensions={0}, use_global_device_ids=true | all-gather | bytes 327680 | tf_op jit(solution)/shard_map/all_gather | solution.py:158
  15.4 4.3 %collective-permute-start.3 = (bf16[4,128,256]{2,1,0:T(8,128)(2,1)S(1)}, bf16[4,128,256]{2,1,0:T(8,128)(2,1)S(1)}, u32[]{:S(2)}, u32[]{:S(2)}) collective-permute-start(bf16[4,128,256]{2,1,0:T(8,128)(2,1)S(1)} %bitcast.56), channel_id=1, source_target_pairs={{0,64},{64,128},{128,192},{192,256},{256,320},{320,384},{384,448},... | collective-permute-start | bytes 786440 | tf_op jit(solution)/shard_map/ppermute | solution.py:163
  19.7 8.6 %collective-permute-start = (bf16[4,128,256]{2,1,0:T(8,128)(2,1)S(1)}, bf16[4,128,256]{2,1,0:T(8,128)(2,1)S(1)}, u32[]{:S(2)}, u32[]{:S(2)}) collective-permute-start(bf16[4,128,256]{2,1,0:T(8,128)(2,1)S(1)} %bitcast.57), channel_id=1, source_target_pairs={{0,448},{64,0},{128,64},{192,128},{256,192},{320,256},{384,320},{4... | collective-permute-start | bytes 786440 | tf_op jit(solution)/shard_map/ppermute | solution.py:165
  28.3 2.5 %collective-permute-done.3.refs_7_ = bf16[4,128,256]{2,1,0:T(8,128)(2,1)S(1)} collective-permute-done((bf16[4,128,256]{2,1,0:T(8,128)(2,1)S(1)}, bf16[4,128,256]{2,1,0:T(8,128)(2,1)S(1)}, u32[]{:S(2)}, u32[]{:S(2)}) %collective-permute-start.3) | collective-permute-done | bytes 262176 | tf_op jit(solution)/shard_map/ppermute | solution.py:163
  30.8 1.9 %collective-permute-start.4 = (bf16[4,128,256]{2,1,0:T(8,128)(2,1)S(1)}, bf16[4,128,256]{2,1,0:T(8,128)(2,1)S(1)}, u32[]{:S(2)}, u32[]{:S(2)}) collective-permute-start(bf16[4,128,256]{2,1,0:T(8,128)(2,1)S(1)} %collective-permute-done.3.refs_7_), channel_id=1, source_target_pairs={{0,64},{64,128},{128,192},{192,256},{256,320},{320,384},{384,448},... | collective-permute-start | bytes 786440 | tf_op jit(solution)/shard_map/ppermute | solution.py:163
  32.7 0.0 collective-permute-done.refs_1_
  32.7 5.1 %collective-permute-start.1 = (bf16[4,128,256]{2,1,0:T(8,128)(2,1)S(1)}, bf16[4,128,256]{2,1,0:T(8,128)(2,1)S(1)}, u32[]{:S(2)}, u32[]{:S(2)}) collective-permute-start(bf16[4,128,256]{2,1,0:T(8,128)(2,1)S(1)} %collective-permute-done.refs_1_), channel_id=1, source_target_pairs={{0,448},{64,0},{128,64},{192,128},{256,192},{320,256},{384,320},{4... | collective-permute-start | bytes 786440 | tf_op jit(solution)/shard_map/ppermute | solution.py:165
  37.9 2.4 %collective-permute-done.4.refs_6_ = bf16[4,128,256]{2,1,0:T(8,128)(2,1)S(1)} collective-permute-done((bf16[4,128,256]{2,1,0:T(8,128)(2,1)S(1)}, bf16[4,128,256]{2,1,0:T(8,128)(2,1)S(1)}, u32[]{:S(2)}, u32[]{:S(2)}) %collective-permute-start.4) | collective-permute-done | bytes 262176 | tf_op jit(solution)/shard_map/ppermute | solution.py:163
  40.3 1.9 %collective-permute-start.5 = (bf16[4,128,256]{2,1,0:T(8,128)(2,1)S(1)}, bf16[4,128,256]{2,1,0:T(8,128)(2,1)S(1)}, u32[]{:S(2)}, u32[]{:S(2)}) collective-permute-start(bf16[4,128,256]{2,1,0:T(8,128)(2,1)S(1)} %collective-permute-done.4.refs_6_), channel_id=1, source_target_pairs={{0,64},{64,128},{128,192},{192,256},{256,320},{320,384},{384,448},... | collective-permute-start | bytes 786440 | tf_op jit(solution)/shard_map/ppermute | solution.py:163
  42.2 5.1 %collective-permute-start.2 = (bf16[4,128,256]{2,1,0:T(8,128)(2,1)S(1)}, bf16[4,128,256]{2,1,0:T(8,128)(2,1)S(1)}, u32[]{:S(2)}, u32[]{:S(2)}) collective-permute-start(bf16[4,128,256]{2,1,0:T(8,128)(2,1)S(1)} %collective-permute-done.1.refs_2_), channel_id=1, source_target_pairs={{0,448},{64,0},{128,64},{192,128},{256,192},{320,256},{384,320},{4... | collective-permute-start | bytes 786440 | tf_op jit(solution)/shard_map/ppermute | solution.py:165
  47.3 2.4 %collective-permute-done.5.refs_5_ = bf16[4,128,256]{2,1,0:T(8,128)(2,1)S(1)} collective-permute-done((bf16[4,128,256]{2,1,0:T(8,128)(2,1)S(1)}, bf16[4,128,256]{2,1,0:T(8,128)(2,1)S(1)}, u32[]{:S(2)}, u32[]{:S(2)}) %collective-permute-start.5) | collective-permute-done | bytes 262176 | tf_op jit(solution)/shard_map/ppermute | solution.py:163
  49.7 1.9 %collective-permute-start.6 = (bf16[4,128,256]{2,1,0:T(8,128)(2,1)S(1)}, bf16[4,128,256]{2,1,0:T(8,128)(2,1)S(1)}, u32[]{:S(2)}, u32[]{:S(2)}) collective-permute-start(bf16[4,128,256]{2,1,0:T(8,128)(2,1)S(1)} %collective-permute-done.5.refs_5_), channel_id=1, source_target_pairs={{0,64},{64,128},{128,192},{192,256},{256,320},{320,384},{384,448},... | collective-permute-start | bytes 786440 | tf_op jit(solution)/shard_map/ppermute | solution.py:163
  52.3 0.8 fusion.8
  53.1 0.0 collective-permute-done.2.refs_3_
  53.1 6.1 %collective-permute-done.6.refs_4_ = bf16[4,128,256]{2,1,0:T(8,128)(2,1)S(1)} collective-permute-done((bf16[4,128,256]{2,1,0:T(8,128)(2,1)S(1)}, bf16[4,128,256]{2,1,0:T(8,128)(2,1)S(1)}, u32[]{:S(2)}, u32[]{:S(2)}) %collective-permute-start.6) | collective-permute-done | bytes 262176 | tf_op jit(solution)/shard_map/ppermute | solution.py:163
  59.2 2.6 %shard_map.102 = (bf16[8,128,256]{2,1,0:T(8,128)(2,1)S(1)}, bf16[8,128,256]{2,1,0:T(8,128)(2,1)S(1)}) custom-call(s32[96]{0:T(128)S(1)} %get-tuple-element.28.source_ref.target_ref, s32[96]{0:T(128)S(1)} %get-tuple-element.29.target_ref.source_ref, s32[1]{0:T(128)} %bitcast.52.count_ref, bf16[96,128,128]{2,1,0:T(8,128)(2,1)} %bitcast.54, ...), custom_call_target="tpu_custom_call" | custom-call | flops 805306368 | bytes 6291456 | tf_op jit(solution)/shard_map/pallas_call | solution.py:175
  61.8 1.9 %collective-permute-start.7 = (bf16[8,128,256]{2,1,0:T(8,128)(2,1)S(1)}, bf16[8,128,256]{2,1,0:T(8,128)(2,1)S(1)}, u32[]{:S(2)}, u32[]{:S(2)}) collective-permute-start(bf16[8,128,256]{2,1,0:T(8,128)(2,1)S(1)} %get-tuple-element.16), channel_id=1, source_target_pairs={{0,1},{1,0},{2,3},{3,2},{4,5},{5,4},{6,7},{7,6},{8,9},{9,8},{10,11... | collective-permute-start | bytes 1572872 | tf_op jit(solution)/shard_map/ppermute | solution.py:138
  63.8 1.9 %collective-permute-done.7 = bf16[8,128,256]{2,1,0:T(8,128)(2,1)S(1)} collective-permute-done((bf16[8,128,256]{2,1,0:T(8,128)(2,1)S(1)}, bf16[8,128,256]{2,1,0:T(8,128)(2,1)S(1)}, u32[]{:S(2)}, u32[]{:S(2)}) %collective-permute-start.7) | collective-permute-done | bytes 524320 | tf_op jit(solution)/shard_map/ppermute | solution.py:138
  65.6 0.1 add_convert_fusion
  65.8 0.0 copy-start.2
  65.8 15.6 %all_to_all.20 = bf16[8,128,256]{2,1,0:T(8,128)(2,1)S(1)} all-to-all(bf16[8,128,256]{2,1,0:T(8,128)(2,1)S(1)} %add_convert_fusion), channel_id=1, replica_groups=mesh['z'=8,'yl'=4,'yh'=2,'x'=4,'c'=2] {'x'}, dimensions={0} | all-to-all | bytes 1048576 | tf_op jit(solution)/shard_map/all_to_all | solution.py:130
  81.4 0.1 bitcast_reduce_fusion
  81.5 6.1 %collective-permute-start.8 = (bf16[256,256]{1,0:T(8,128)(2,1)S(1)}, bf16[256,256]{1,0:T(8,128)(2,1)S(1)}, u32[]{:S(2)}, u32[]{:S(2)}) collective-permute-start(bf16[256,256]{1,0:T(8,128)(2,1)S(1)} %bitcast_reduce_fusion), channel_id=1, source_target_pairs={{0,8},{8,0},{1,9},{9,1},{2,10},{10,2},{3,11},{11,3},{4,12},{12,4},... | collective-permute-start | bytes 393224 | tf_op jit(solution)/shard_map/ppermute | solution.py:193
  87.6 6.6 %collective-permute-done.8 = bf16[256,256]{1,0:T(8,128)(2,1)S(1)} collective-permute-done((bf16[256,256]{1,0:T(8,128)(2,1)S(1)}, bf16[256,256]{1,0:T(8,128)(2,1)S(1)}, u32[]{:S(2)}, u32[]{:S(2)}) %collective-permute-start.8) | collective-permute-done | bytes 131104 | tf_op jit(solution)/shard_map/ppermute | solution.py:193
  94.2 0.2 multiply_convert_fusion
  94.5 0.2 fusion
  94.6 0.2 convolution_convert_fusion.3
  94.8 0.1 convolution_convert_fusion
  95.0 0.1 convolution_convert_fusion.2
  95.2 0.0 copy-start.1
  95.2 0.1 copy.12
  95.4 12.3 %all_to_all.21.mine_ref = bf16[4,288,256]{2,1,0:T(8,128)(2,1)S(1)} all-to-all(bf16[4,288,256]{2,1,0:T(8,128)(2,1)S(1)} %maximum_maximum_fusion), channel_id=1, replica_groups=mesh['z'=8,'yl'=4,'yh'=2,'x'=4,'c'=2] {'x'}, dimensions={0} | all-to-all | bytes 1179648 | tf_op jit(solution)/shard_map/all_to_all | solution.py:130
  107.7 1.9 %collective-permute-start.9 = (bf16[4,288,256]{2,1,0:T(8,128)(2,1)S(1)}, bf16[4,288,256]{2,1,0:T(8,128)(2,1)S(1)}, u32[]{:S(2)}, u32[]{:S(2)}) collective-permute-start(bf16[4,288,256]{2,1,0:T(8,128)(2,1)S(1)} %all_to_all.21.mine_ref), channel_id=1, source_target_pairs={{0,1},{1,0},{2,3},{3,2},{4,5},{5,4},{6,7},{7,6},{8,9},{9,8},{10,11... | collective-permute-start | bytes 1769480 | tf_op jit(solution)/shard_map/ppermute | solution.py:138
  109.6 2.0 %collective-permute-done.9.theirs_ref = bf16[4,288,256]{2,1,0:T(8,128)(2,1)S(1)} collective-permute-done((bf16[4,288,256]{2,1,0:T(8,128)(2,1)S(1)}, bf16[4,288,256]{2,1,0:T(8,128)(2,1)S(1)}, u32[]{:S(2)}, u32[]{:S(2)}) %collective-permute-start.9) | collective-permute-done | bytes 589856 | tf_op jit(solution)/shard_map/ppermute | solution.py:138
  111.6 2.1 %shard_map.103 = (bf16[512,256]{1,0:T(8,128)(2,1)S(1)}, bf16[544,256]{1,0:T(8,128)(2,1)S(1)}, bf16[544,256]{1,0:T(8,128)(2,1)S(1)}, bf16[544,256]{1,0:T(8,128)(2...) custom-call(s32[96]{0:T(128)S(1)} %get-tuple-element.29.target_ref.s, ...), custom_call_target="tpu_custom_call" | custom-call | flops 805306368 | bytes 6291456 | tf_op jit(solution)/shard_map/pallas_call | solution.py:216
  113.7 1.9 %collective-permute-start.10 = (bf16[544,256]{1,0:T(8,128)(2,1)S(1)}, bf16[544,256]{1,0:T(8,128)(2,1)S(1)}, u32[]{:S(2)}, u32[]{:S(2)}) collective-permute-start(bf16[544,256]{1,0:T(8,128)(2,1)S(1)} %get-tuple-element.19), channel_id=1, source_target_pairs={{0,448},{64,0},{128,64},{192,128},{256,192},{320,256},{384,320},{4... | collective-permute-start | bytes 835592 | tf_op jit(solution)/shard_map/ppermute | solution.py:237
  115.6 3.9 %collective-permute-start.14 = (bf16[544,256]{1,0:T(8,128)(2,1)S(1)}, bf16[544,256]{1,0:T(8,128)(2,1)S(1)}, u32[]{:S(2)}, u32[]{:S(2)}) collective-permute-start(bf16[544,256]{1,0:T(8,128)(2,1)S(1)} %get-tuple-element.23), channel_id=1, source_target_pairs={{0,64},{64,128},{128,192},{192,256},{256,320},{320,384},{384,448},... | collective-permute-start | bytes 835592 | tf_op jit(solution)/shard_map/ppermute | solution.py:239
  119.5 5.1 %collective-permute-done.10.refs_0_ = bf16[544,256]{1,0:T(8,128)(2,1)S(1)} collective-permute-done((bf16[544,256]{1,0:T(8,128)(2,1)S(1)}, bf16[544,256]{1,0:T(8,128)(2,1)S(1)}, u32[]{:S(2)}, u32[]{:S(2)}) %collective-permute-start.10) | collective-permute-done | bytes 278560 | tf_op jit(solution)/shard_map/ppermute | solution.py:237
  124.6 0.1 add_convert_fusion.5
  124.7 2.8 %collective-permute-start.11 = (bf16[544,256]{1,0:T(8,128)(2,1)S(1)}, bf16[544,256]{1,0:T(8,128)(2,1)S(1)}, u32[]{:S(2)}, u32[]{:S(2)}) collective-permute-start(bf16[544,256]{1,0:T(8,128)(2,1)S(1)} %add_convert_fusion.5), channel_id=1, source_target_pairs={{0,448},{64,0},{128,64},{192,128},{256,192},{320,256},{384,320},{4... | collective-permute-start | bytes 835592 | tf_op jit(solution)/shard_map/ppermute | solution.py:237
  127.5 0.2 collective-permute-done.14.refs_6_
  127.7 0.1 add_convert_fusion.2
  127.8 2.9 %collective-permute-start.15 = (bf16[544,256]{1,0:T(8,128)(2,1)S(1)}, bf16[544,256]{1,0:T(8,128)(2,1)S(1)}, u32[]{:S(2)}, u32[]{:S(2)}) collective-permute-start(bf16[544,256]{1,0:T(8,128)(2,1)S(1)} %add_convert_fusion.2), channel_id=1, source_target_pairs={{0,64},{64,128},{128,192},{192,256},{256,320},{320,384},{384,448},... | collective-permute-start | bytes 835592 | tf_op jit(solution)/shard_map/ppermute | solution.py:239
  130.7 5.0 %collective-permute-done.11.refs_1_ = bf16[544,256]{1,0:T(8,128)(2,1)S(1)} collective-permute-done((bf16[544,256]{1,0:T(8,128)(2,1)S(1)}, bf16[544,256]{1,0:T(8,128)(2,1)S(1)}, u32[]{:S(2)}, u32[]{:S(2)}) %collective-permute-start.11) | collective-permute-done | bytes 278560 | tf_op jit(solution)/shard_map/ppermute | solution.py:237
  135.7 0.1 add_convert_fusion.4
  135.8 4.0 %collective-permute-start.12 = (bf16[544,256]{1,0:T(8,128)(2,1)S(1)}, bf16[544,256]{1,0:T(8,128)(2,1)S(1)}, u32[]{:S(2)}, u32[]{:S(2)}) collective-permute-start(bf16[544,256]{1,0:T(8,128)(2,1)S(1)} %add_convert_fusion.4), channel_id=1, source_target_pairs={{0,448},{64,0},{128,64},{192,128},{256,192},{320,256},{384,320},{4... | collective-permute-start | bytes 835592 | tf_op jit(solution)/shard_map/ppermute | solution.py:237
  139.9 0.0 collective-permute-done.15.refs_5_
  139.9 0.1 add_convert_fusion.1
  140.0 1.9 %collective-permute-start.16 = (bf16[544,256]{1,0:T(8,128)(2,1)S(1)}, bf16[544,256]{1,0:T(8,128)(2,1)S(1)}, u32[]{:S(2)}, u32[]{:S(2)}) collective-permute-start(bf16[544,256]{1,0:T(8,128)(2,1)S(1)} %add_convert_fusion.1), channel_id=1, source_target_pairs={{0,64},{64,128},{128,192},{192,256},{256,320},{320,384},{384,448},... | collective-permute-start | bytes 835592 | tf_op jit(solution)/shard_map/ppermute | solution.py:239
  141.9 4.2 %collective-permute-done.12.refs_2_ = bf16[544,256]{1,0:T(8,128)(2,1)S(1)} collective-permute-done((bf16[544,256]{1,0:T(8,128)(2,1)S(1)}, bf16[544,256]{1,0:T(8,128)(2,1)S(1)}, u32[]{:S(2)}, u32[]{:S(2)}) %collective-permute-start.12) | collective-permute-done | bytes 278560 | tf_op jit(solution)/shard_map/ppermute | solution.py:237
  146.1 0.1 add_convert_fusion.3
  146.2 5.2 %collective-permute-start.13 = (bf16[544,256]{1,0:T(8,128)(2,1)S(1)}, bf16[544,256]{1,0:T(8,128)(2,1)S(1)}, u32[]{:S(2)}, u32[]{:S(2)}) collective-permute-start(bf16[544,256]{1,0:T(8,128)(2,1)S(1)} %add_convert_fusion.3), channel_id=1, source_target_pairs={{0,448},{64,0},{128,64},{192,128},{256,192},{320,256},{384,320},{4... | collective-permute-start | bytes 835592 | tf_op jit(solution)/shard_map/ppermute | solution.py:237
  151.4 0.0 collective-permute-done.16.refs_4_
  151.4 5.0 %collective-permute-done.13.refs_3_ = bf16[544,256]{1,0:T(8,128)(2,1)S(1)} collective-permute-done((bf16[544,256]{1,0:T(8,128)(2,1)S(1)}, bf16[544,256]{1,0:T(8,128)(2,1)S(1)}, u32[]{:S(2)}, u32[]{:S(2)}) %collective-permute-start.13) | collective-permute-done | bytes 278560 | tf_op jit(solution)/shard_map/ppermute | solution.py:237
  156.4 0.1 shard_map.104
  156.5 11.0 %all_to_all.22 = bf16[4,160,256]{2,1,0:T(8,128)(2,1)S(1)} all-to-all(bf16[4,160,256]{2,1,0:T(8,128)(2,1)S(1)} %shard_map.104), channel_id=1, replica_groups=mesh['z'=8,'yl'=4,'yh'=2,'x'=4,'c'=2] {'yl'}, dimensions={0} | all-to-all | bytes 655360 | tf_op jit(solution)/shard_map/all_to_all | solution.py:130
  167.5 0.6 slice_bitcast_fusion
  168.2 0.7 broadcast_in_dim.21
  168.8 3.3 %all-to-all-start.3 = ((f32[4,32,256]{2,1,0:T(8,128)}), f32[4,32,256]{2,1,0:T(8,128)S(1)}, u32[]{:S(2)}, u32[]{:S(2)}) async-start(f32[4,32,256]{2,1,0:T(8,128)} %broadcast_in_dim.21), calls=%async_computation.3 | async-start | bytes 262144 | tf_op jit(solution)/shard_map/all_to_all | solution.py:130
  172.2 0.8 fusion.1
  172.9 5.2 %all-to-all-done.3 = f32[4,32,256]{2,1,0:T(8,128)S(1)} async-done(((f32[4,32,256]{2,1,0:T(8,128)}), f32[4,32,256]{2,1,0:T(8,128)S(1)}, u32[]{:S(2)}, u32[]{:S(2)}) %all-to-all-start.3) | async-done | bytes 131104 | tf_op jit(solution)/shard_map/all_to_all | solution.py:130
  178.1 0.7 fusion.17
  (11 shorter events, 0.2 us)
Async XLA Ops:
  0.6 93.6 %copy-start = (bf16[128,128]{1,0:T(8,128)(2,1)S(1)}, bf16[128,128]{1,0:T(8,128)(2,1)}, u32[]{:S(2)}) copy-start(bf16[128,128]{1,0:T(8,128)(2,1)} %param.8) | copy-start | bytes 98308
  15.4 15.4 %collective-permute-start.3 = (bf16[4,128,256]{2,1,0:T(8,128)(2,1)S(1)}, bf16[4,128,256]{2,1,0:T(8,128)(2,1)S(1)}, u32[]{:S(2)}, u32[]{:S(2)}) collective-permute-start(bf16[4,128,256]{2,1,0:T(8,128)(2,1)S(1)} %bitcast.56), channel_id=1, source_target_pairs={{0,64},{64,128},{128,192},{192,256},{256,320},{320,384},{384,448},... | collective-permute-start | bytes 786440 | tf_op jit(solution)/shard_map/ppermute | solution.py:163
  19.7 13.0 %collective-permute-start = (bf16[4,128,256]{2,1,0:T(8,128)(2,1)S(1)}, bf16[4,128,256]{2,1,0:T(8,128)(2,1)S(1)}, u32[]{:S(2)}, u32[]{:S(2)}) collective-permute-start(bf16[4,128,256]{2,1,0:T(8,128)(2,1)S(1)} %bitcast.57), channel_id=1, source_target_pairs={{0,448},{64,0},{128,64},{192,128},{256,192},{320,256},{384,320},{4... | collective-permute-start | bytes 786440 | tf_op jit(solution)/shard_map/ppermute | solution.py:165
  30.8 9.5 %collective-permute-start.4 = (bf16[4,128,256]{2,1,0:T(8,128)(2,1)S(1)}, bf16[4,128,256]{2,1,0:T(8,128)(2,1)S(1)}, u32[]{:S(2)}, u32[]{:S(2)}) collective-permute-start(bf16[4,128,256]{2,1,0:T(8,128)(2,1)S(1)} %collective-permute-done.3.refs_7_), channel_id=1, source_target_pairs={{0,64},{64,128},{128,192},{192,256},{256,320},{320,384},{384,448},... | collective-permute-start | bytes 786440 | tf_op jit(solution)/shard_map/ppermute | solution.py:163
  32.7 9.5 %collective-permute-start.1 = (bf16[4,128,256]{2,1,0:T(8,128)(2,1)S(1)}, bf16[4,128,256]{2,1,0:T(8,128)(2,1)S(1)}, u32[]{:S(2)}, u32[]{:S(2)}) collective-permute-start(bf16[4,128,256]{2,1,0:T(8,128)(2,1)S(1)} %collective-permute-done.refs_1_), channel_id=1, source_target_pairs={{0,448},{64,0},{128,64},{192,128},{256,192},{320,256},{384,320},{4... | collective-permute-start | bytes 786440 | tf_op jit(solution)/shard_map/ppermute | solution.py:165
  40.3 9.5 %collective-permute-start.5 = (bf16[4,128,256]{2,1,0:T(8,128)(2,1)S(1)}, bf16[4,128,256]{2,1,0:T(8,128)(2,1)S(1)}, u32[]{:S(2)}, u32[]{:S(2)}) collective-permute-start(bf16[4,128,256]{2,1,0:T(8,128)(2,1)S(1)} %collective-permute-done.4.refs_6_), channel_id=1, source_target_pairs={{0,64},{64,128},{128,192},{192,256},{256,320},{320,384},{384,448},... | collective-permute-start | bytes 786440 | tf_op jit(solution)/shard_map/ppermute | solution.py:163
  42.2 10.9 %collective-permute-start.2 = (bf16[4,128,256]{2,1,0:T(8,128)(2,1)S(1)}, bf16[4,128,256]{2,1,0:T(8,128)(2,1)S(1)}, u32[]{:S(2)}, u32[]{:S(2)}) collective-permute-start(bf16[4,128,256]{2,1,0:T(8,128)(2,1)S(1)} %collective-permute-done.1.refs_2_), channel_id=1, source_target_pairs={{0,448},{64,0},{128,64},{192,128},{256,192},{320,256},{384,320},{4... | collective-permute-start | bytes 786440 | tf_op jit(solution)/shard_map/ppermute | solution.py:165
  49.7 9.5 %collective-permute-start.6 = (bf16[4,128,256]{2,1,0:T(8,128)(2,1)S(1)}, bf16[4,128,256]{2,1,0:T(8,128)(2,1)S(1)}, u32[]{:S(2)}, u32[]{:S(2)}) collective-permute-start(bf16[4,128,256]{2,1,0:T(8,128)(2,1)S(1)} %collective-permute-done.5.refs_5_), channel_id=1, source_target_pairs={{0,64},{64,128},{128,192},{192,256},{256,320},{320,384},{384,448},... | collective-permute-start | bytes 786440 | tf_op jit(solution)/shard_map/ppermute | solution.py:163
  61.8 3.8 %collective-permute-start.7 = (bf16[8,128,256]{2,1,0:T(8,128)(2,1)S(1)}, bf16[8,128,256]{2,1,0:T(8,128)(2,1)S(1)}, u32[]{:S(2)}, u32[]{:S(2)}) collective-permute-start(bf16[8,128,256]{2,1,0:T(8,128)(2,1)S(1)} %get-tuple-element.16), channel_id=1, source_target_pairs={{0,1},{1,0},{2,3},{3,2},{4,5},{5,4},{6,7},{7,6},{8,9},{9,8},{10,11... | collective-permute-start | bytes 1572872 | tf_op jit(solution)/shard_map/ppermute | solution.py:138
  65.8 28.7 %copy-start.2 = (bf16[128,128]{1,0:T(8,128)(2,1)S(1)}, bf16[128,128]{1,0:T(8,128)(2,1)}, u32[]{:S(2)}) copy-start(bf16[128,128]{1,0:T(8,128)(2,1)} %param.9) | copy-start | bytes 98308
  81.5 12.7 %collective-permute-start.8 = (bf16[256,256]{1,0:T(8,128)(2,1)S(1)}, bf16[256,256]{1,0:T(8,128)(2,1)S(1)}, u32[]{:S(2)}, u32[]{:S(2)}) collective-permute-start(bf16[256,256]{1,0:T(8,128)(2,1)S(1)} %bitcast_reduce_fusion), channel_id=1, source_target_pairs={{0,8},{8,0},{1,9},{9,1},{2,10},{10,2},{3,11},{11,3},{4,12},{12,4},... | collective-permute-start | bytes 393224 | tf_op jit(solution)/shard_map/ppermute | solution.py:193
  95.2 16.4 %copy-start.1 = (bf16[1,1,96,128,128]{4,3,2,1,0:T(8,128)(2,1)S(1)}, bf16[1,1,96,128,128]{4,3,2,1,0:T(8,128)(2,1)}, u32[]{:S(2)}) copy-start(bf16[1,1,96,128,128]{4,3,2,1,0:T(8,128)(2,1)} %param.10) | copy-start | bytes 9437188
  107.7 3.9 %collective-permute-start.9 = (bf16[4,288,256]{2,1,0:T(8,128)(2,1)S(1)}, bf16[4,288,256]{2,1,0:T(8,128)(2,1)S(1)}, u32[]{:S(2)}, u32[]{:S(2)}) collective-permute-start(bf16[4,288,256]{2,1,0:T(8,128)(2,1)S(1)} %all_to_all.21.mine_ref), channel_id=1, source_target_pairs={{0,1},{1,0},{2,3},{3,2},{4,5},{5,4},{6,7},{7,6},{8,9},{9,8},{10,11... | collective-permute-start | bytes 1769480 | tf_op jit(solution)/shard_map/ppermute | solution.py:138
  113.7 10.9 %collective-permute-start.10 = (bf16[544,256]{1,0:T(8,128)(2,1)S(1)}, bf16[544,256]{1,0:T(8,128)(2,1)S(1)}, u32[]{:S(2)}, u32[]{:S(2)}) collective-permute-start(bf16[544,256]{1,0:T(8,128)(2,1)S(1)} %get-tuple-element.19), channel_id=1, source_target_pairs={{0,448},{64,0},{128,64},{192,128},{256,192},{320,256},{384,320},{4... | collective-permute-start | bytes 835592 | tf_op jit(solution)/shard_map/ppermute | solution.py:237
  115.6 12.1 %collective-permute-start.14 = (bf16[544,256]{1,0:T(8,128)(2,1)S(1)}, bf16[544,256]{1,0:T(8,128)(2,1)S(1)}, u32[]{:S(2)}, u32[]{:S(2)}) collective-permute-start(bf16[544,256]{1,0:T(8,128)(2,1)S(1)} %get-tuple-element.23), channel_id=1, source_target_pairs={{0,64},{64,128},{128,192},{192,256},{256,320},{320,384},{384,448},... | collective-permute-start | bytes 835592 | tf_op jit(solution)/shard_map/ppermute | solution.py:239
  124.7 11.1 %collective-permute-start.11 = (bf16[544,256]{1,0:T(8,128)(2,1)S(1)}, bf16[544,256]{1,0:T(8,128)(2,1)S(1)}, u32[]{:S(2)}, u32[]{:S(2)}) collective-permute-start(bf16[544,256]{1,0:T(8,128)(2,1)S(1)} %add_convert_fusion.5), channel_id=1, source_target_pairs={{0,448},{64,0},{128,64},{192,128},{256,192},{320,256},{384,320},{4... | collective-permute-start | bytes 835592 | tf_op jit(solution)/shard_map/ppermute | solution.py:237
  127.8 12.1 %collective-permute-start.15 = (bf16[544,256]{1,0:T(8,128)(2,1)S(1)}, bf16[544,256]{1,0:T(8,128)(2,1)S(1)}, u32[]{:S(2)}, u32[]{:S(2)}) collective-permute-start(bf16[544,256]{1,0:T(8,128)(2,1)S(1)} %add_convert_fusion.2), channel_id=1, source_target_pairs={{0,64},{64,128},{128,192},{192,256},{256,320},{320,384},{384,448},... | collective-permute-start | bytes 835592 | tf_op jit(solution)/shard_map/ppermute | solution.py:239
  135.8 10.3 %collective-permute-start.12 = (bf16[544,256]{1,0:T(8,128)(2,1)S(1)}, bf16[544,256]{1,0:T(8,128)(2,1)S(1)}, u32[]{:S(2)}, u32[]{:S(2)}) collective-permute-start(bf16[544,256]{1,0:T(8,128)(2,1)S(1)} %add_convert_fusion.4), channel_id=1, source_target_pairs={{0,448},{64,0},{128,64},{192,128},{256,192},{320,256},{384,320},{4... | collective-permute-start | bytes 835592 | tf_op jit(solution)/shard_map/ppermute | solution.py:237
  140.0 11.4 %collective-permute-start.16 = (bf16[544,256]{1,0:T(8,128)(2,1)S(1)}, bf16[544,256]{1,0:T(8,128)(2,1)S(1)}, u32[]{:S(2)}, u32[]{:S(2)}) collective-permute-start(bf16[544,256]{1,0:T(8,128)(2,1)S(1)} %add_convert_fusion.1), channel_id=1, source_target_pairs={{0,64},{64,128},{128,192},{192,256},{256,320},{320,384},{384,448},... | collective-permute-start | bytes 835592 | tf_op jit(solution)/shard_map/ppermute | solution.py:239
  146.2 10.2 %collective-permute-start.13 = (bf16[544,256]{1,0:T(8,128)(2,1)S(1)}, bf16[544,256]{1,0:T(8,128)(2,1)S(1)}, u32[]{:S(2)}, u32[]{:S(2)}) collective-permute-start(bf16[544,256]{1,0:T(8,128)(2,1)S(1)} %add_convert_fusion.3), channel_id=1, source_target_pairs={{0,448},{64,0},{128,64},{192,128},{256,192},{320,256},{384,320},{4... | collective-permute-start | bytes 835592 | tf_op jit(solution)/shard_map/ppermute | solution.py:237
  168.8 9.3 %all-to-all-start.3 = ((f32[4,32,256]{2,1,0:T(8,128)}), f32[4,32,256]{2,1,0:T(8,128)S(1)}, u32[]{:S(2)}, u32[]{:S(2)}) async-start(f32[4,32,256]{2,1,0:T(8,128)} %broadcast_in_dim.21), calls=%async_computation.3 | async-start | bytes 262144 | tf_op jit(solution)/shard_map/all_to_all | solution.py:130

commit v5 on v4

v5 whole, which is shorter than its diff:
```python
import functools
import math

import jax
import jax.numpy as jnp
from jax import lax
from jax.experimental import pallas as pl
from jax.experimental.pallas import tpu as pltpu
from jax.sharding import Mesh, PartitionSpec as P

ROW = ("z", "yl")
COL = ("yh", "x", "c")
UNROLL = 16
MINE, FIRST, REST = range(3)


def add_slots(first, count, source_ref, target_ref, tiles_ref, panel_ref, acc_ref):
    spare = acc_ref.shape[0] - 1
    for k in range(tiles_ref.shape[0]):
        slot = first + k
        product = jnp.dot(
            tiles_ref[k], panel_ref[source_ref[slot]], preferred_element_type=jnp.float32
        )
        acc_ref[jnp.where(slot < count, target_ref[slot], spare)] += product


def forward_kernel(source_ref, target_ref, count_ref, tiles_ref, *refs):
    pieces, (keep_ref, send_ref, held_ref, panel_ref, acc_ref, sems) = refs[:-6], refs[-6:]
    steps = sems.shape[0]
    group = held_ref.shape[0] // steps
    copies = [
        pltpu.make_async_copy(
            tiles_ref.at[pl.ds(i * group, group)], held_ref.at[pl.ds(i * group, group)], sems.at[i]
        )
        for i in range(steps)
    ]
    for copy in copies:
        copy.start()
    acc_ref[...] = jnp.zeros_like(acc_ref)
    n = pieces[0].shape[0]
    for i, piece in enumerate(pieces):
        panel_ref[i * n : (i + 1) * n] = piece[...]
    count = count_ref[0]
    for i, copy in enumerate(copies):
        copy.wait()

        @pl.when(i * group < count)
        def _():
            tiles = held_ref.at[pl.ds(i * group, group)]
            add_slots(i * group, count, source_ref, target_ref, tiles, panel_ref, acc_ref)

    half = keep_ref.shape[0]
    keep_ref[...] = acc_ref[:half].astype(keep_ref.dtype)
    send_ref[...] = acc_ref[half : 2 * half].astype(send_ref.dtype)


def shift(value, n):
    return lax.shift_right_logical(value, jnp.int32(n.bit_length() - 1))


def plan_kernel(sizes, coords_ref, count_ref, list_ref, size_ref):
    z_n, yl_n, yh_n, x_n = sizes
    middle = z_n // 2
    slots, groups = coords_ref.shape[0], size_ref.shape[0]
    unroll = math.gcd(slots, 4)
    z, core, count = (coords_ref[0] >> 16) & 255, coords_ref[0] >> 24, count_ref[0]

    def step(first, ends):
        ends = list(ends)
        for k in range(unroll):
            slot = first * unroll + k
            row, col = coords_ref[slot] & 255, (coords_ref[slot] >> 8) & 255
            turn = (shift(col, yl_n) - z) & (z_n - 1)
            place = (shift(row, 2) & (x_n - 1)) * yh_n + shift(row, 2 * x_n)
            block = turn * yl_n + (col & (yl_n - 1))
            mine = (row & 1) == core
            chunks = (turn == middle) | (turn == middle - 1)
            group = jnp.where(mine, MINE, jnp.where(chunks, FIRST, REST))
            target = jnp.where(~mine & chunks, block - (middle - 1) * yl_n, block)
            at = jnp.int32(groups * slots)
            for g in range(groups):
                chosen = (slot < count) & (group == g)
                at = jnp.where(chosen, g * slots + ends[g], at)
                ends[g] = ends[g] + chosen.astype(jnp.int32)
            list_ref[at] = slot + (place << 8) + (target << 16)
        return tuple(ends)

    ends = lax.fori_loop(0, (count + unroll - 1) // unroll, step, (jnp.int32(0),) * groups)
    for group in range(groups):
        size_ref[group] = ends[group]


def add_tiles(unroll, group, list_ref, size_ref, tiles_ref, read, acc_ref):
    spare, slots = acc_ref.shape[0] - 1, tiles_ref.shape[0]
    contract = (((0,), (0,)), ((), ()))
    size = size_ref[group]

    def step(first, carry):
        for k in range(unroll):
            at = first * unroll + k
            live = at < size
            entry = list_ref[slots * group + jnp.minimum(at, slots - 1)]
            entry = jnp.where(live, entry, spare << 16)
            slot, source, target = entry & 255, (entry >> 8) & 255, entry >> 16
            product = lax.dot_general(
                tiles_ref[slot], read(source), contract, preferred_element_type=jnp.float32
            )
            acc_ref[target] += product
        return carry

    lax.fori_loop(0, (size + unroll - 1) // unroll, step, 0)


def reader(ref, side, held):
    def read(source):
        start = pl.multiple_of(lax.rem(source, held) * side, side)
        return ref[source // held, pl.ds(start, side), :]

    return read


def mine_kernel(held, list_ref, size_ref, tiles_ref, mine_ref, acc_ref):
    acc_ref[...] = jnp.zeros_like(acc_ref)
    read = reader(mine_ref, tiles_ref.shape[1], held)
    add_tiles(16, MINE, list_ref, size_ref, tiles_ref, read, acc_ref)


def first_kernel(
    held, begin, list_ref, size_ref, tiles_ref, mine_ref, theirs_ref, begun_ref,
    up_ref, down_ref, term_ref, acc_ref,
):
    side = tiles_ref.shape[1]
    blocks = acc_ref.shape[0] - 1
    acc_ref[:blocks] = begun_ref[begin : begin + blocks]
    acc_ref[blocks] = jnp.zeros_like(acc_ref[blocks])
    read = reader(theirs_ref, side, held)
    add_tiles(8, FIRST, list_ref, size_ref, tiles_ref, read, acc_ref)
    terms = jnp.sum(mine_ref[:, held * side :].astype(jnp.float32), axis=0) + jnp.sum(
        theirs_ref[:, held * side :].astype(jnp.float32), axis=0
    )
    terms = terms.astype(term_ref.dtype)
    term_ref[...] = terms
    for i in range(blocks // 2):
        rows = pl.ds(i * side, side)
        up_ref[rows] = acc_ref[i].astype(up_ref.dtype)
        down_ref[rows] = acc_ref[blocks // 2 + i].astype(down_ref.dtype)
    rest = blocks // 2 * side
    up_ref[rest:] = terms
    down_ref[rest:] = terms


def rest_kernel(held, turns, list_ref, size_ref, tiles_ref, theirs_ref, begun_ref, *refs):
    outs, acc_ref = refs[:-1], refs[-1]
    side = tiles_ref.shape[1]
    n = outs[0].shape[0] // side
    spare = acc_ref.shape[0] - 1
    acc_ref[spare] = jnp.zeros_like(acc_ref[spare])
    for turn in turns:
        acc_ref[turn * n : (turn + 1) * n] = begun_ref[turn * n : (turn + 1) * n]
    read = reader(theirs_ref, side, held)
    add_tiles(16, REST, list_ref, size_ref, tiles_ref, read, acc_ref)
    for turn, out_ref in zip(turns, outs):
        for i in range(n):
            out_ref[i * side : (i + 1) * side] = acc_ref[turn * n + i].astype(out_ref.dtype)
        if turn:
            out_ref[n * side :] = jnp.zeros_like(out_ref[n * side :])


def ring_sum_kernel(coords_ref, own_ref, term_ref, *refs):
    got, (out_ref, held_ref) = refs[:-2], refs[-2:]
    blocks, side = out_ref.shape[0], own_ref.shape[0] // out_ref.shape[0]
    places = len(got) + 1
    rest = own_ref.shape[0]
    z = (coords_ref[0] >> 16) & 255
    held_ref[z] = term_ref[...]
    for k, ref in enumerate(got):
        held_ref[lax.rem(z + k + 1, places)] = ref[rest:]
    terms = jnp.sum(held_ref[...].astype(jnp.float32), axis=0).astype(out_ref.dtype)
    ahead, behind = got[places // 2 - 1], got[places // 2]
    for i in range(blocks):
        rows = pl.ds(i * side, side)
        total = own_ref[rows].astype(jnp.float32) + ahead[rows].astype(jnp.float32)
        out_ref[i, :side] = (total + behind[rows].astype(jnp.float32)).astype(out_ref.dtype)
        out_ref[i, side:] = terms


VMEM = pl.BlockSpec(memory_space=pltpu.VMEM)
SMEM = pl.BlockSpec(memory_space=pltpu.SMEM)
HBM = pl.BlockSpec(memory_space=pltpu.HBM)


def call(kernel, ins, outs, scratch, args, flops=0):
    return pl.pallas_call(
        kernel,
        out_shape=outs,
        in_specs=ins,
        out_specs=jax.tree.map(lambda _: VMEM, outs),
        scratch_shapes=scratch,
        compiler_params=pltpu.CompilerParams(vmem_limit_bytes=24 << 20),
        cost_estimate=pl.CostEstimate(
            flops=flops, transcendentals=0, bytes_accessed=4 * math.prod(outs[0].shape)
        ),
    )(*args)


def exchange(blocks, axes):
    return lax.all_to_all(blocks, axes, 0, 0, tiled=True)


def add(left, right):
    return (left.astype(jnp.float32) + right.astype(jnp.float32)).astype(jnp.bfloat16)


def swap_cores(value):
    return lax.ppermute(value, "c", [(0, 1), (1, 0)])


def on_device(features, weight1, weight2, tile_values, tile_coords, tile_count, out_grad):
    side, feat = features.shape[1], features.shape[2]
    z_n, yl_n = lax.axis_size("z"), lax.axis_size("yl")
    x_n, yh_n = lax.axis_size("x"), lax.axis_size("yh")
    rows_n, cols_n = z_n * yl_n, lax.axis_size(COL)
    half_n, middle = cols_n // 2, z_n // 2
    width = 2 * feat
    node_total = side * rows_n * cols_n
    slots = tile_values.shape[2]
    coords = (
        tile_coords[0, 0, 0]
        + (tile_coords[0, 0, 1] << 8)
        + (lax.axis_index("z").astype(jnp.int32) << 16)
        + (lax.axis_index("c").astype(jnp.int32) << 24)
    )
    dot = functools.partial(jnp.dot, preferred_element_type=jnp.float32)
    contract = (((0,), (0,)), ((), ()))
    bf16 = functools.partial(jax.ShapeDtypeStruct, dtype=jnp.bfloat16)
    f32 = functools.partial(jax.ShapeDtypeStruct, dtype=jnp.float32)
    tile_flops = 2 * side * side * width

    both = jnp.concatenate([features[0], out_grad[0]], axis=1)
    own = lax.all_gather(both, "yl", axis=0, tiled=True).reshape(yl_n, side, width)
    up = [(i, (i + 1) % z_n) for i in range(z_n)]
    down = [(i, (i - 1) % z_n) for i in range(z_n)]
    pieces = {0: own}
    for step in range(1, middle):
        pieces[-step % z_n] = lax.ppermute(pieces[(1 - step) % z_n], "z", up)
        pieces[step] = lax.ppermute(pieces[step - 1], "z", down)
    pieces[middle] = lax.ppermute(pieces[middle + 1], "z", up)
    block_rows, block_cols = tile_coords[0, 0, 0], tile_coords[0, 0, 1]
    z, core = (lax.axis_index(name).astype(jnp.int32) for name in ("z", "c"))
    source = ((block_cols // yl_n - z) % z_n) * yl_n + block_cols % yl_n
    row_place = (
        ((block_rows % 2) ^ core) * half_n
        + (block_rows // 2 % x_n) * yh_n
        + block_rows // (2 * x_n)
    )
    half = bf16((half_n, side, width))
    keep, send = pl.pallas_call(
        forward_kernel,
        out_shape=(half, half),
        in_specs=[SMEM] * 3 + [HBM] + [VMEM] * len(pieces),
        out_specs=(VMEM, VMEM),
        scratch_shapes=[
            pltpu.VMEM((slots, side, side), jnp.bfloat16),
            pltpu.VMEM((rows_n, side, width), jnp.bfloat16),
            pltpu.VMEM((cols_n + 1, side, width), jnp.float32),
            pltpu.SemaphoreType.DMA((slots // math.gcd(slots, UNROLL),)),
        ],
        compiler_params=pltpu.CompilerParams(vmem_limit_bytes=24 << 20),
        cost_estimate=pl.CostEstimate(
            flops=tile_flops * slots, transcendentals=0, bytes_accessed=2 * slots * side * side
        ),
    )(
        source,
        row_place,
        tile_count[0],
        pltpu.with_memory_space_constraint(tile_values[0, 0], pltpu.HBM),
        *(pieces[turn] for turn in range(z_n)),
    )

    pair = add(keep, swap_cores(send))
    got = exchange(pair, "x").reshape(x_n, yh_n * side, width)
    sums = jnp.sum(got.astype(jnp.float32), axis=0).astype(jnp.bfloat16)
    sums, coords = lax.optimization_barrier((sums, coords))
    swapped = lax.ppermute(sums, "yh", [(0, 1), (1, 0)])
    lists, list_sizes = pl.pallas_call(
        functools.partial(plan_kernel, (z_n, yl_n, yh_n, x_n)),
        out_shape=(
            jax.ShapeDtypeStruct((3 * slots + 1,), jnp.int32),
            jax.ShapeDtypeStruct((3,), jnp.int32),
        ),
        in_specs=[SMEM] * 2,
        out_specs=(SMEM, SMEM),
        compiler_params=pltpu.CompilerParams(vmem_limit_bytes=4 << 20),
        cost_estimate=pl.CostEstimate(flops=0, transcendentals=0, bytes_accessed=1 << 20),
    )(coords, tile_count[0])
    swapped, lists, list_sizes = lax.optimization_barrier((swapped, lists, list_sizes))
    plan = (lists, list_sizes, tile_values[0, 0])
    specs = [SMEM, SMEM, VMEM]
    sums = sums.astype(jnp.float32) + swapped.astype(jnp.float32)
    agg_one = sums[:, :feat].astype(jnp.bfloat16)
    agg_grad = sums[:, feat:].astype(jnp.bfloat16)
    pre_one = dot(agg_one, weight1)
    sigmoid = jax.nn.sigmoid(pre_one)
    hidden = (pre_one * sigmoid).astype(jnp.bfloat16)
    grad_hidden = dot(agg_grad, weight2.T)
    grad_pre = (grad_hidden * (sigmoid * (1.0 + pre_one * (1.0 - sigmoid)))).astype(jnp.bfloat16)
    grad_one = dot(grad_pre, weight1.T).astype(jnp.bfloat16)
    term_one = lax.dot_general(agg_one, grad_pre, contract, preferred_element_type=jnp.float32)
    term_two = lax.dot_general(hidden, agg_grad, contract, preferred_element_type=jnp.float32)

    both = jnp.concatenate([hidden, grad_one], axis=1)
    slices = jnp.concatenate([term_one, term_two], axis=1).astype(jnp.bfloat16)
    term_rows = feat // x_n
    slices = slices.reshape(x_n, term_rows, width)
    sent = jnp.concatenate(
        [jnp.broadcast_to(both[None], (x_n,) + both.shape), slices], axis=1
    )
    mine = exchange(sent, "x")
    theirs = swap_cores(mine)
    (begun,) = call(
        functools.partial(mine_kernel, yh_n),
        specs + [VMEM],
        (f32((rows_n + 1, side, width)),),
        [],
        (*plan, mine),
        tile_flops * slots // 2,
    )
    message = bf16((yl_n * side + term_rows, width))
    chunks = {}
    chunks[middle - 1], chunks[middle], terms = call(
        functools.partial(first_kernel, yh_n, (middle - 1) * yl_n),
        specs + [VMEM] * 3,
        (message, message, bf16((term_rows, width))),
        [pltpu.VMEM((2 * yl_n + 1, side, width), jnp.float32)],
        (*plan, mine, theirs, begun),
        tile_flops * slots // 8,
    )
    rest = tuple(k for k in range(z_n) if k not in chunks)
    outs = call(
        functools.partial(rest_kernel, yh_n, rest),
        specs + [VMEM] * 2,
        tuple(message if k else bf16((yl_n * side, width)) for k in rest),
        [pltpu.VMEM((rows_n + 1, side, width), jnp.float32)],
        (*plan, theirs, begun),
        tile_flops * slots // 2,
    )
    chunks.update(zip(rest, outs))

    ahead, behind = [], []
    down_sum, up_sum = chunks[middle], chunks[middle - 1]
    for step in range(middle):
        ahead.append(lax.ppermute(down_sum, "z", down))
        if step < middle - 1:
            behind.append(lax.ppermute(up_sum, "z", up))
            down_sum = add(ahead[-1], chunks[middle + 1 + step])
        if step < middle - 2:
            up_sum = add(behind[-1], chunks[middle - 2 - step])
    (sent,) = call(
        ring_sum_kernel,
        [SMEM] + [VMEM] * (z_n + 1),
        (bf16((yl_n, side + term_rows, width)),),
        [pltpu.VMEM((z_n, term_rows, width), jnp.bfloat16)],
        (coords, chunks[0], terms, *ahead, *behind[::-1]),
    )
    got = exchange(sent, "yl")
    terms = jnp.sum(got[:, side:].astype(jnp.float32), axis=0) * (1.0 / math.sqrt(node_total))
    weights = exchange(jnp.broadcast_to(terms[None], (x_n,) + terms.shape), "x")
    sums = jnp.sum(got[:, :side].astype(jnp.float32), axis=0).astype(jnp.bfloat16)
    output = dot(sums[:, :feat], weight2).astype(jnp.bfloat16)
    grad_features = sums[:, feat:]
    weights = weights.reshape(feat, width)
    return (output[None], grad_features[None], weights[:, :feat], weights[:, feat:])


def solution(mesh):
    fine = Mesh(mesh.devices.reshape(8, 4, 2, 4, 2), ("z", "yl", "yh", "x", "c"))
    placed = (
        P(COL, ROW, None),
        P(),
        P(),
        P(ROW, COL, None, None, None),
        P(ROW, COL, None, None),
        P(ROW, COL),
        P(COL, ROW, None),
    )
    return jax.shard_map(
        on_device,
        mesh=fine,
        in_specs=placed,
        out_specs=(P(COL, ROW, None), P(COL, ROW, None), P(), P()),
        check_vma=False,
    )
```

time: 180 us -> 177 us (0.983)
  waiting for transfers between devices: 48.5 us -> 41.3 us
  Pallas kernels: 4.83 us -> 8.62 us
    ppermute x4, waiting for transfers between devices: 19.3 us -> 13.9 us  [on_device(): ahead.append(lax.ppermute(down_sum, 'z', down))]
    pallas_call x2 -> x5, Pallas kernels: 2.2 us -> 5.99 us  [the longest x4 4.47 us: call(): pl.pallas_call(kernel, out_shape=outs, in_specs=ins, out_specs=jax.tree.m...]
    ppermute x4, starting transfers between devices: 14 us -> 15.9 us  [on_device(): ahead.append(lax.ppermute(down_sum, 'z', down))]
  transfers between devices with their start and end apart: 18 -> 18, of which waited for: 13 -> 12; matrix products, arithmetic and copies ran while one was open for 1% -> 1% of each run, Pallas kernels for 0% -> 2%
where the time goes in v5:
time: 177 us; the launch traced here: 176 us
  starting transfers between devices  65 us (37%)
  blocking collectives  53.4 us (30%)
  waiting for transfers between devices  41.3 us (23%)
  Pallas kernels  8.62 us (5%)
  other arithmetic  2.32 us (1%)
  local copies, waits for them, and re-layouts  2.09 us (1%)
    all_to_all x3, blocking collectives, exchange(): return lax.all_to_all(blocks, axes, 0, 0, tiled=True)  39.5 us
    ppermute x3, starting transfers between devices, on_device(): pieces[step] = lax.ppermute(pieces[step - 1], 'z', down)  18.9 us
    ppermute x4, starting transfers between devices, on_device(): ahead.append(lax.ppermute(down_sum, 'z', down))  15.9 us
    all_gather x1, blocking collectives, on_device(): lax.all_gather(both, 'yl', axis=0, tiled=True).reshape(yl_n, side, width)  14 us
    ppermute x4, waiting for transfers between devices, on_device(): ahead.append(lax.ppermute(down_sum, 'z', down))  13.9 us
    ppermute x3, starting transfers between devices, on_device(): behind.append(lax.ppermute(up_sum, 'z', up))  8.27 us
    ppermute x3, starting transfers between devices, on_device(): pieces[-step % z_n] = lax.ppermute(pieces[(1 - step) % z_n], 'z', up)  8.09 us
    ppermute x3, waiting for transfers between devices, on_device(): pieces[-step % z_n] = lax.ppermute(pieces[(1 - step) % z_n], 'z', up)  7.31 us
  transfers between devices with their start and end apart: 18, of which 12 were waited for; matrix products, arithmetic and copies ran while one was open for 1% of the time, Pallas kernels for 2%

profile of v5, /device:TPU:56, one launch (start us, length us, event | category | flops | bytes accessed | tf_op | source)
XLA Modules:
  0.0 176.0 jit_solution(12060053306892813371)
XLA Ops:
  0.6 0.0 copy-start
  0.6 0.8 pad_maximum_fusion.1
  1.4 14.0 %all_gather.3 = bf16[512,256]{1,0:T(8,128)(2,1)S(1)} all-gather(bf16[128,256]{1,0:T(8,128)(2,1)S(1)} %pad_maximum_fusion.1), channel_id=1, replica_groups=mesh['z'=8,'yl'=4,'yh'=2,'x'=4,'c'=2] {'yl'}, dimensions={0}, use_global_device_ids=true | all-gather | bytes 327680 | tf_op jit(solution)/shard_map/all_gather | solution.py:240
  15.4 4.3 %collective-permute-start.3 = (bf16[4,128,256]{2,1,0:T(8,128)(2,1)S(1)}, bf16[4,128,256]{2,1,0:T(8,128)(2,1)S(1)}, u32[]{:S(2)}, u32[]{:S(2)}) collective-permute-start(bf16[4,128,256]{2,1,0:T(8,128)(2,1)S(1)} %bitcast.65), channel_id=1, source_target_pairs={{0,64},{64,128},{128,192},{192,256},{256,320},{320,384},{384,448},... | collective-permute-start | bytes 786440 | tf_op jit(solution)/shard_map/ppermute | solution.py:245
  19.7 8.6 %collective-permute-start = (bf16[4,128,256]{2,1,0:T(8,128)(2,1)S(1)}, bf16[4,128,256]{2,1,0:T(8,128)(2,1)S(1)}, u32[]{:S(2)}, u32[]{:S(2)}) collective-permute-start(bf16[4,128,256]{2,1,0:T(8,128)(2,1)S(1)} %bitcast.66), channel_id=1, source_target_pairs={{0,448},{64,0},{128,64},{192,128},{256,192},{320,256},{384,320},{4... | collective-permute-start | bytes 786440 | tf_op jit(solution)/shard_map/ppermute | solution.py:246
  28.3 2.5 %collective-permute-done.3.refs_7_ = bf16[4,128,256]{2,1,0:T(8,128)(2,1)S(1)} collective-permute-done((bf16[4,128,256]{2,1,0:T(8,128)(2,1)S(1)}, bf16[4,128,256]{2,1,0:T(8,128)(2,1)S(1)}, u32[]{:S(2)}, u32[]{:S(2)}) %collective-permute-start.3) | collective-permute-done | bytes 262176 | tf_op jit(solution)/shard_map/ppermute | solution.py:245
  30.8 1.9 %collective-permute-start.4 = (bf16[4,128,256]{2,1,0:T(8,128)(2,1)S(1)}, bf16[4,128,256]{2,1,0:T(8,128)(2,1)S(1)}, u32[]{:S(2)}, u32[]{:S(2)}) collective-permute-start(bf16[4,128,256]{2,1,0:T(8,128)(2,1)S(1)} %collective-permute-done.3.refs_7_), channel_id=1, source_target_pairs={{0,64},{64,128},{128,192},{192,256},{256,320},{320,384},{384,448},... | collective-permute-start | bytes 786440 | tf_op jit(solution)/shard_map/ppermute | solution.py:245
  32.7 0.0 collective-permute-done.refs_1_
  32.7 5.1 %collective-permute-start.1 = (bf16[4,128,256]{2,1,0:T(8,128)(2,1)S(1)}, bf16[4,128,256]{2,1,0:T(8,128)(2,1)S(1)}, u32[]{:S(2)}, u32[]{:S(2)}) collective-permute-start(bf16[4,128,256]{2,1,0:T(8,128)(2,1)S(1)} %collective-permute-done.refs_1_), channel_id=1, source_target_pairs={{0,448},{64,0},{128,64},{192,128},{256,192},{320,256},{384,320},{4... | collective-permute-start | bytes 786440 | tf_op jit(solution)/shard_map/ppermute | solution.py:246
  37.9 2.4 %collective-permute-done.4.refs_6_ = bf16[4,128,256]{2,1,0:T(8,128)(2,1)S(1)} collective-permute-done((bf16[4,128,256]{2,1,0:T(8,128)(2,1)S(1)}, bf16[4,128,256]{2,1,0:T(8,128)(2,1)S(1)}, u32[]{:S(2)}, u32[]{:S(2)}) %collective-permute-start.4) | collective-permute-done | bytes 262176 | tf_op jit(solution)/shard_map/ppermute | solution.py:245
  40.3 1.9 %collective-permute-start.5 = (bf16[4,128,256]{2,1,0:T(8,128)(2,1)S(1)}, bf16[4,128,256]{2,1,0:T(8,128)(2,1)S(1)}, u32[]{:S(2)}, u32[]{:S(2)}) collective-permute-start(bf16[4,128,256]{2,1,0:T(8,128)(2,1)S(1)} %collective-permute-done.4.refs_6_), channel_id=1, source_target_pairs={{0,64},{64,128},{128,192},{192,256},{256,320},{320,384},{384,448},... | collective-permute-start | bytes 786440 | tf_op jit(solution)/shard_map/ppermute | solution.py:245
  42.2 5.1 %collective-permute-start.2 = (bf16[4,128,256]{2,1,0:T(8,128)(2,1)S(1)}, bf16[4,128,256]{2,1,0:T(8,128)(2,1)S(1)}, u32[]{:S(2)}, u32[]{:S(2)}) collective-permute-start(bf16[4,128,256]{2,1,0:T(8,128)(2,1)S(1)} %collective-permute-done.1.refs_2_), channel_id=1, source_target_pairs={{0,448},{64,0},{128,64},{192,128},{256,192},{320,256},{384,320},{4... | collective-permute-start | bytes 786440 | tf_op jit(solution)/shard_map/ppermute | solution.py:246
  47.3 2.4 %collective-permute-done.5.refs_5_ = bf16[4,128,256]{2,1,0:T(8,128)(2,1)S(1)} collective-permute-done((bf16[4,128,256]{2,1,0:T(8,128)(2,1)S(1)}, bf16[4,128,256]{2,1,0:T(8,128)(2,1)S(1)}, u32[]{:S(2)}, u32[]{:S(2)}) %collective-permute-start.5) | collective-permute-done | bytes 262176 | tf_op jit(solution)/shard_map/ppermute | solution.py:245
  49.7 1.9 %collective-permute-start.6 = (bf16[4,128,256]{2,1,0:T(8,128)(2,1)S(1)}, bf16[4,128,256]{2,1,0:T(8,128)(2,1)S(1)}, u32[]{:S(2)}, u32[]{:S(2)}) collective-permute-start(bf16[4,128,256]{2,1,0:T(8,128)(2,1)S(1)} %collective-permute-done.5.refs_5_), channel_id=1, source_target_pairs={{0,64},{64,128},{128,192},{192,256},{256,320},{320,384},{384,448},... | collective-permute-start | bytes 786440 | tf_op jit(solution)/shard_map/ppermute | solution.py:247
  52.3 0.8 fusion.18
  53.1 6.1 %collective-permute-done.6.refs_4_ = bf16[4,128,256]{2,1,0:T(8,128)(2,1)S(1)} collective-permute-done((bf16[4,128,256]{2,1,0:T(8,128)(2,1)S(1)}, bf16[4,128,256]{2,1,0:T(8,128)(2,1)S(1)}, u32[]{:S(2)}, u32[]{:S(2)}) %collective-permute-start.6) | collective-permute-done | bytes 262176 | tf_op jit(solution)/shard_map/ppermute | solution.py:247
  59.2 2.6 %shard_map.102 = (bf16[8,128,256]{2,1,0:T(8,128)(2,1)S(1)}, bf16[8,128,256]{2,1,0:T(8,128)(2,1)S(1)}) custom-call(s32[96]{0:T(128)S(1)} %get-tuple-element.44.source_ref, s32[96]{0:T(128)S(1)} %get-tuple-element.43.target_ref, s32[1]{0:T(128)} %bitcast.59.count_ref, bf16[96,128,128]{2,1,0:T(8,128)(2,1)} %bitcast.61, bf16[4,128,256]{2,1,0:T(8,128)(2,1)S(1)} %bitcast.67, ...), custom_call_target="tpu_custom_call" | custom-call | flops 805306368 | bytes 3145728 | tf_op jit(solution)/shard_map/pallas_call | solution.py:257
  61.8 1.9 %collective-permute-start.7 = (bf16[8,128,256]{2,1,0:T(8,128)(2,1)S(1)}, bf16[8,128,256]{2,1,0:T(8,128)(2,1)S(1)}, u32[]{:S(2)}, u32[]{:S(2)}) collective-permute-start(bf16[8,128,256]{2,1,0:T(8,128)(2,1)S(1)} %get-tuple-element.23), channel_id=1, source_target_pairs={{0,1},{1,0},{2,3},{3,2},{4,5},{5,4},{6,7},{7,6},{8,9},{9,8},{10,11... | collective-permute-start | bytes 1572872 | tf_op jit(solution)/shard_map/ppermute | solution.py:215
  63.8 1.9 %collective-permute-done.7 = bf16[8,128,256]{2,1,0:T(8,128)(2,1)S(1)} collective-permute-done((bf16[8,128,256]{2,1,0:T(8,128)(2,1)S(1)}, bf16[8,128,256]{2,1,0:T(8,128)(2,1)S(1)}, u32[]{:S(2)}, u32[]{:S(2)}) %collective-permute-start.7) | collective-permute-done | bytes 524320 | tf_op jit(solution)/shard_map/ppermute | solution.py:215
  65.6 0.1 add_convert_fusion
  65.8 0.0 copy-start.2
  65.8 15.6 %all_to_all.20 = bf16[8,128,256]{2,1,0:T(8,128)(2,1)S(1)} all-to-all(bf16[8,128,256]{2,1,0:T(8,128)(2,1)S(1)} %add_convert_fusion), channel_id=1, replica_groups=mesh['z'=8,'yl'=4,'yh'=2,'x'=4,'c'=2] {'x'}, dimensions={0} | all-to-all | bytes 1048576 | tf_op jit(solution)/shard_map/all_to_all | solution.py:207
  81.4 0.1 bitcast_reduce_fusion
  81.5 4.8 %collective-permute-start.8 = (bf16[256,256]{1,0:T(8,128)(2,1)S(1)}, bf16[256,256]{1,0:T(8,128)(2,1)S(1)}, u32[]{:S(2)}, u32[]{:S(2)}) collective-permute-start(bf16[256,256]{1,0:T(8,128)(2,1)S(1)} %bitcast_reduce_fusion), channel_id=1, source_target_pairs={{0,8},{8,0},{1,9},{9,1},{2,10},{10,2},{3,11},{11,3},{4,12},{12,4},... | collective-permute-start | bytes 393224 | tf_op jit(solution)/shard_map/ppermute | solution.py:284
  86.3 1.5 shard_map.103
  87.8 6.2 %collective-permute-done.8 = bf16[256,256]{1,0:T(8,128)(2,1)S(1)} collective-permute-done((bf16[256,256]{1,0:T(8,128)(2,1)S(1)}, bf16[256,256]{1,0:T(8,128)(2,1)S(1)}, u32[]{:S(2)}, u32[]{:S(2)}) %collective-permute-start.8) | collective-permute-done | bytes 131104 | tf_op jit(solution)/shard_map/ppermute | solution.py:284
  94.1 0.2 multiply_convert_fusion
  94.4 0.2 fusion
  94.5 0.2 convolution_convert_fusion.3
  94.7 0.1 convolution_convert_fusion
  94.9 0.1 convolution_convert_fusion.2
  95.1 0.0 copy-start.1
  95.1 0.1 copy.12
  95.3 10.9 %all_to_all.21.mine_ref = bf16[4,288,256]{2,1,0:T(8,128)(2,1)S(1)} all-to-all(bf16[4,288,256]{2,1,0:T(8,128)(2,1)S(1)} %maximum_maximum_fusion), channel_id=1, replica_groups=mesh['z'=8,'yl'=4,'yh'=2,'x'=4,'c'=2] {'x'}, dimensions={0} | all-to-all | bytes 1179648 | tf_op jit(solution)/shard_map/all_to_all | solution.py:207
  106.2 1.9 %collective-permute-start.9 = (bf16[4,288,256]{2,1,0:T(8,128)(2,1)S(1)}, bf16[4,288,256]{2,1,0:T(8,128)(2,1)S(1)}, u32[]{:S(2)}, u32[]{:S(2)}) collective-permute-start(bf16[4,288,256]{2,1,0:T(8,128)(2,1)S(1)} %all_to_all.21.mine_ref), channel_id=1, source_target_pairs={{0,1},{1,0},{2,3},{3,2},{4,5},{5,4},{6,7},{7,6},{8,9},{9,8},{10,11... | collective-permute-start | bytes 1769480 | tf_op jit(solution)/shard_map/ppermute | solution.py:215
  108.2 1.3 shard_map.104.begun_ref
  109.5 0.6 collective-permute-done.9.theirs_ref
  110.1 1.0 shard_map.106
  111.2 1.9 %collective-permute-start.10 = (bf16[544,256]{1,0:T(8,128)(2,1)S(1)}, bf16[544,256]{1,0:T(8,128)(2,1)S(1)}, u32[]{:S(2)}, u32[]{:S(2)}) collective-permute-start(bf16[544,256]{1,0:T(8,128)(2,1)S(1)} %get-tuple-element.33), channel_id=1, source_target_pairs={{0,448},{64,0},{128,64},{192,128},{256,192},{320,256},{384,320},{4... | collective-permute-start | bytes 835592 | tf_op jit(solution)/shard_map/ppermute | solution.py:352
  113.1 3.9 %collective-permute-start.14 = (bf16[544,256]{1,0:T(8,128)(2,1)S(1)}, bf16[544,256]{1,0:T(8,128)(2,1)S(1)}, u32[]{:S(2)}, u32[]{:S(2)}) collective-permute-start(bf16[544,256]{1,0:T(8,128)(2,1)S(1)} %get-tuple-element.37), channel_id=1, source_target_pairs={{0,64},{64,128},{128,192},{192,256},{256,320},{320,384},{384,448},... | collective-permute-start | bytes 835592 | tf_op jit(solution)/shard_map/ppermute | solution.py:354
  117.0 1.4 shard_map.105
  118.5 3.3 %collective-permute-done.10.refs_0_ = bf16[544,256]{1,0:T(8,128)(2,1)S(1)} collective-permute-done((bf16[544,256]{1,0:T(8,128)(2,1)S(1)}, bf16[544,256]{1,0:T(8,128)(2,1)S(1)}, u32[]{:S(2)}, u32[]{:S(2)}) %collective-permute-start.10) | collective-permute-done | bytes 278560 | tf_op jit(solution)/shard_map/ppermute | solution.py:352
  121.8 0.1 add_convert_fusion.5
  121.8 3.4 %collective-permute-start.11 = (bf16[544,256]{1,0:T(8,128)(2,1)S(1)}, bf16[544,256]{1,0:T(8,128)(2,1)S(1)}, u32[]{:S(2)}, u32[]{:S(2)}) collective-permute-start(bf16[544,256]{1,0:T(8,128)(2,1)S(1)} %add_convert_fusion.5), channel_id=1, source_target_pairs={{0,448},{64,0},{128,64},{192,128},{256,192},{320,256},{384,320},{4... | collective-permute-start | bytes 835592 | tf_op jit(solution)/shard_map/ppermute | solution.py:352
  125.3 0.1 add_convert_fusion.2
  125.4 2.4 %collective-permute-start.15 = (bf16[544,256]{1,0:T(8,128)(2,1)S(1)}, bf16[544,256]{1,0:T(8,128)(2,1)S(1)}, u32[]{:S(2)}, u32[]{:S(2)}) collective-permute-start(bf16[544,256]{1,0:T(8,128)(2,1)S(1)} %add_convert_fusion.2), channel_id=1, source_target_pairs={{0,64},{64,128},{128,192},{192,256},{256,320},{320,384},{384,448},... | collective-permute-start | bytes 835592 | tf_op jit(solution)/shard_map/ppermute | solution.py:354
  127.8 3.8 %collective-permute-done.11.refs_1_ = bf16[544,256]{1,0:T(8,128)(2,1)S(1)} collective-permute-done((bf16[544,256]{1,0:T(8,128)(2,1)S(1)}, bf16[544,256]{1,0:T(8,128)(2,1)S(1)}, u32[]{:S(2)}, u32[]{:S(2)}) %collective-permute-start.11) | collective-permute-done | bytes 278560 | tf_op jit(solution)/shard_map/ppermute | solution.py:352
  131.6 0.1 add_convert_fusion.4
  131.7 4.9 %collective-permute-start.12 = (bf16[544,256]{1,0:T(8,128)(2,1)S(1)}, bf16[544,256]{1,0:T(8,128)(2,1)S(1)}, u32[]{:S(2)}, u32[]{:S(2)}) collective-permute-start(bf16[544,256]{1,0:T(8,128)(2,1)S(1)} %add_convert_fusion.4), channel_id=1, source_target_pairs={{0,448},{64,0},{128,64},{192,128},{256,192},{320,256},{384,320},{4... | collective-permute-start | bytes 835592 | tf_op jit(solution)/shard_map/ppermute | solution.py:352
  136.6 0.0 collective-permute-done.15.refs_5_
  136.7 0.1 add_convert_fusion.1
  136.7 1.9 %collective-permute-start.16 = (bf16[544,256]{1,0:T(8,128)(2,1)S(1)}, bf16[544,256]{1,0:T(8,128)(2,1)S(1)}, u32[]{:S(2)}, u32[]{:S(2)}) collective-permute-start(bf16[544,256]{1,0:T(8,128)(2,1)S(1)} %add_convert_fusion.1), channel_id=1, source_target_pairs={{0,64},{64,128},{128,192},{192,256},{256,320},{320,384},{384,448},... | collective-permute-start | bytes 835592 | tf_op jit(solution)/shard_map/ppermute | solution.py:354
  138.7 2.8 %collective-permute-done.12.refs_2_ = bf16[544,256]{1,0:T(8,128)(2,1)S(1)} collective-permute-done((bf16[544,256]{1,0:T(8,128)(2,1)S(1)}, bf16[544,256]{1,0:T(8,128)(2,1)S(1)}, u32[]{:S(2)}, u32[]{:S(2)}) %collective-permute-start.12) | collective-permute-done | bytes 278560 | tf_op jit(solution)/shard_map/ppermute | solution.py:352
  141.4 0.1 add_convert_fusion.3
  141.5 5.6 %collective-permute-start.13 = (bf16[544,256]{1,0:T(8,128)(2,1)S(1)}, bf16[544,256]{1,0:T(8,128)(2,1)S(1)}, u32[]{:S(2)}, u32[]{:S(2)}) collective-permute-start(bf16[544,256]{1,0:T(8,128)(2,1)S(1)} %add_convert_fusion.3), channel_id=1, source_target_pairs={{0,448},{64,0},{128,64},{192,128},{256,192},{320,256},{384,320},{4... | collective-permute-start | bytes 835592 | tf_op jit(solution)/shard_map/ppermute | solution.py:352
  147.1 4.0 %collective-permute-done.13.refs_3_ = bf16[544,256]{1,0:T(8,128)(2,1)S(1)} collective-permute-done((bf16[544,256]{1,0:T(8,128)(2,1)S(1)}, bf16[544,256]{1,0:T(8,128)(2,1)S(1)}, u32[]{:S(2)}, u32[]{:S(2)}) %collective-permute-start.13) | collective-permute-done | bytes 278560 | tf_op jit(solution)/shard_map/ppermute | solution.py:352
  151.2 0.7 shard_map.107
  151.8 12.9 %all_to_all.22 = bf16[4,160,256]{2,1,0:T(8,128)(2,1)S(1)} all-to-all(bf16[4,160,256]{2,1,0:T(8,128)(2,1)S(1)} %shard_map.107), channel_id=1, replica_groups=mesh['z'=8,'yl'=4,'yh'=2,'x'=4,'c'=2] {'yl'}, dimensions={0} | all-to-all | bytes 655360 | tf_op jit(solution)/shard_map/all_to_all | solution.py:207
  164.8 0.6 slice_bitcast_fusion
  165.4 0.7 broadcast_in_dim.21
  166.1 3.3 %all-to-all-start.3 = ((f32[4,32,256]{2,1,0:T(8,128)}), f32[4,32,256]{2,1,0:T(8,128)S(1)}, u32[]{:S(2)}, u32[]{:S(2)}) async-start(f32[4,32,256]{2,1,0:T(8,128)} %broadcast_in_dim.21), calls=%async_computation.3 | async-start | bytes 262144 | tf_op jit(solution)/shard_map/all_to_all | solution.py:207
  169.4 0.8 fusion.1
  170.2 5.2 %all-to-all-done.3 = f32[4,32,256]{2,1,0:T(8,128)S(1)} async-done(((f32[4,32,256]{2,1,0:T(8,128)}), f32[4,32,256]{2,1,0:T(8,128)S(1)}, u32[]{:S(2)}, u32[]{:S(2)}) %all-to-all-start.3) | async-done | bytes 131104 | tf_op jit(solution)/shard_map/all_to_all | solution.py:207
  175.4 0.7 fusion.19
  (14 shorter events, 0.2 us)
Async XLA Ops:
  0.6 93.5 %copy-start = (bf16[128,128]{1,0:T(8,128)(2,1)S(1)}, bf16[128,128]{1,0:T(8,128)(2,1)}, u32[]{:S(2)}) copy-start(bf16[128,128]{1,0:T(8,128)(2,1)} %param.8) | copy-start | bytes 98308
  15.4 15.4 %collective-permute-start.3 = (bf16[4,128,256]{2,1,0:T(8,128)(2,1)S(1)}, bf16[4,128,256]{2,1,0:T(8,128)(2,1)S(1)}, u32[]{:S(2)}, u32[]{:S(2)}) collective-permute-start(bf16[4,128,256]{2,1,0:T(8,128)(2,1)S(1)} %bitcast.65), channel_id=1, source_target_pairs={{0,64},{64,128},{128,192},{192,256},{256,320},{320,384},{384,448},... | collective-permute-start | bytes 786440 | tf_op jit(solution)/shard_map/ppermute | solution.py:245
  19.7 13.0 %collective-permute-start = (bf16[4,128,256]{2,1,0:T(8,128)(2,1)S(1)}, bf16[4,128,256]{2,1,0:T(8,128)(2,1)S(1)}, u32[]{:S(2)}, u32[]{:S(2)}) collective-permute-start(bf16[4,128,256]{2,1,0:T(8,128)(2,1)S(1)} %bitcast.66), channel_id=1, source_target_pairs={{0,448},{64,0},{128,64},{192,128},{256,192},{320,256},{384,320},{4... | collective-permute-start | bytes 786440 | tf_op jit(solution)/shard_map/ppermute | solution.py:246
  30.8 9.5 %collective-permute-start.4 = (bf16[4,128,256]{2,1,0:T(8,128)(2,1)S(1)}, bf16[4,128,256]{2,1,0:T(8,128)(2,1)S(1)}, u32[]{:S(2)}, u32[]{:S(2)}) collective-permute-start(bf16[4,128,256]{2,1,0:T(8,128)(2,1)S(1)} %collective-permute-done.3.refs_7_), channel_id=1, source_target_pairs={{0,64},{64,128},{128,192},{192,256},{256,320},{320,384},{384,448},... | collective-permute-start | bytes 786440 | tf_op jit(solution)/shard_map/ppermute | solution.py:245
  32.7 9.5 %collective-permute-start.1 = (bf16[4,128,256]{2,1,0:T(8,128)(2,1)S(1)}, bf16[4,128,256]{2,1,0:T(8,128)(2,1)S(1)}, u32[]{:S(2)}, u32[]{:S(2)}) collective-permute-start(bf16[4,128,256]{2,1,0:T(8,128)(2,1)S(1)} %collective-permute-done.refs_1_), channel_id=1, source_target_pairs={{0,448},{64,0},{128,64},{192,128},{256,192},{320,256},{384,320},{4... | collective-permute-start | bytes 786440 | tf_op jit(solution)/shard_map/ppermute | solution.py:246
  40.3 9.5 %collective-permute-start.5 = (bf16[4,128,256]{2,1,0:T(8,128)(2,1)S(1)}, bf16[4,128,256]{2,1,0:T(8,128)(2,1)S(1)}, u32[]{:S(2)}, u32[]{:S(2)}) collective-permute-start(bf16[4,128,256]{2,1,0:T(8,128)(2,1)S(1)} %collective-permute-done.4.refs_6_), channel_id=1, source_target_pairs={{0,64},{64,128},{128,192},{192,256},{256,320},{320,384},{384,448},... | collective-permute-start | bytes 786440 | tf_op jit(solution)/shard_map/ppermute | solution.py:245
  42.2 10.9 %collective-permute-start.2 = (bf16[4,128,256]{2,1,0:T(8,128)(2,1)S(1)}, bf16[4,128,256]{2,1,0:T(8,128)(2,1)S(1)}, u32[]{:S(2)}, u32[]{:S(2)}) collective-permute-start(bf16[4,128,256]{2,1,0:T(8,128)(2,1)S(1)} %collective-permute-done.1.refs_2_), channel_id=1, source_target_pairs={{0,448},{64,0},{128,64},{192,128},{256,192},{320,256},{384,320},{4... | collective-permute-start | bytes 786440 | tf_op jit(solution)/shard_map/ppermute | solution.py:246
  49.7 9.5 %collective-permute-start.6 = (bf16[4,128,256]{2,1,0:T(8,128)(2,1)S(1)}, bf16[4,128,256]{2,1,0:T(8,128)(2,1)S(1)}, u32[]{:S(2)}, u32[]{:S(2)}) collective-permute-start(bf16[4,128,256]{2,1,0:T(8,128)(2,1)S(1)} %collective-permute-done.5.refs_5_), channel_id=1, source_target_pairs={{0,64},{64,128},{128,192},{192,256},{256,320},{320,384},{384,448},... | collective-permute-start | bytes 786440 | tf_op jit(solution)/shard_map/ppermute | solution.py:247
  61.8 3.8 %collective-permute-start.7 = (bf16[8,128,256]{2,1,0:T(8,128)(2,1)S(1)}, bf16[8,128,256]{2,1,0:T(8,128)(2,1)S(1)}, u32[]{:S(2)}, u32[]{:S(2)}) collective-permute-start(bf16[8,128,256]{2,1,0:T(8,128)(2,1)S(1)} %get-tuple-element.23), channel_id=1, source_target_pairs={{0,1},{1,0},{2,3},{3,2},{4,5},{5,4},{6,7},{7,6},{8,9},{9,8},{10,11... | collective-permute-start | bytes 1572872 | tf_op jit(solution)/shard_map/ppermute | solution.py:215
  65.8 28.6 %copy-start.2 = (bf16[128,128]{1,0:T(8,128)(2,1)S(1)}, bf16[128,128]{1,0:T(8,128)(2,1)}, u32[]{:S(2)}) copy-start(bf16[128,128]{1,0:T(8,128)(2,1)} %param.9) | copy-start | bytes 98308
  81.5 12.6 %collective-permute-start.8 = (bf16[256,256]{1,0:T(8,128)(2,1)S(1)}, bf16[256,256]{1,0:T(8,128)(2,1)S(1)}, u32[]{:S(2)}, u32[]{:S(2)}) collective-permute-start(bf16[256,256]{1,0:T(8,128)(2,1)S(1)} %bitcast_reduce_fusion), channel_id=1, source_target_pairs={{0,8},{8,0},{1,9},{9,1},{2,10},{10,2},{3,11},{11,3},{4,12},{12,4},... | collective-permute-start | bytes 393224 | tf_op jit(solution)/shard_map/ppermute | solution.py:284
  95.1 13.1 %copy-start.1 = (bf16[1,1,96,128,128]{4,3,2,1,0:T(8,128)(2,1)S(1)}, bf16[1,1,96,128,128]{4,3,2,1,0:T(8,128)(2,1)}, u32[]{:S(2)}) copy-start(bf16[1,1,96,128,128]{4,3,2,1,0:T(8,128)(2,1)} %param.10) | copy-start | bytes 9437188
  106.2 3.9 %collective-permute-start.9 = (bf16[4,288,256]{2,1,0:T(8,128)(2,1)S(1)}, bf16[4,288,256]{2,1,0:T(8,128)(2,1)S(1)}, u32[]{:S(2)}, u32[]{:S(2)}) collective-permute-start(bf16[4,288,256]{2,1,0:T(8,128)(2,1)S(1)} %all_to_all.21.mine_ref), channel_id=1, source_target_pairs={{0,1},{1,0},{2,3},{3,2},{4,5},{5,4},{6,7},{7,6},{8,9},{9,8},{10,11... | collective-permute-start | bytes 1769480 | tf_op jit(solution)/shard_map/ppermute | solution.py:215
  111.2 10.6 %collective-permute-start.10 = (bf16[544,256]{1,0:T(8,128)(2,1)S(1)}, bf16[544,256]{1,0:T(8,128)(2,1)S(1)}, u32[]{:S(2)}, u32[]{:S(2)}) collective-permute-start(bf16[544,256]{1,0:T(8,128)(2,1)S(1)} %get-tuple-element.33), channel_id=1, source_target_pairs={{0,448},{64,0},{128,64},{192,128},{256,192},{320,256},{384,320},{4... | collective-permute-start | bytes 835592 | tf_op jit(solution)/shard_map/ppermute | solution.py:352
  113.1 12.2 %collective-permute-start.14 = (bf16[544,256]{1,0:T(8,128)(2,1)S(1)}, bf16[544,256]{1,0:T(8,128)(2,1)S(1)}, u32[]{:S(2)}, u32[]{:S(2)}) collective-permute-start(bf16[544,256]{1,0:T(8,128)(2,1)S(1)} %get-tuple-element.37), channel_id=1, source_target_pairs={{0,64},{64,128},{128,192},{192,256},{256,320},{320,384},{384,448},... | collective-permute-start | bytes 835592 | tf_op jit(solution)/shard_map/ppermute | solution.py:354
  121.8 9.8 %collective-permute-start.11 = (bf16[544,256]{1,0:T(8,128)(2,1)S(1)}, bf16[544,256]{1,0:T(8,128)(2,1)S(1)}, u32[]{:S(2)}, u32[]{:S(2)}) collective-permute-start(bf16[544,256]{1,0:T(8,128)(2,1)S(1)} %add_convert_fusion.5), channel_id=1, source_target_pairs={{0,448},{64,0},{128,64},{192,128},{256,192},{320,256},{384,320},{4... | collective-permute-start | bytes 835592 | tf_op jit(solution)/shard_map/ppermute | solution.py:352
  125.4 11.3 %collective-permute-start.15 = (bf16[544,256]{1,0:T(8,128)(2,1)S(1)}, bf16[544,256]{1,0:T(8,128)(2,1)S(1)}, u32[]{:S(2)}, u32[]{:S(2)}) collective-permute-start(bf16[544,256]{1,0:T(8,128)(2,1)S(1)} %add_convert_fusion.2), channel_id=1, source_target_pairs={{0,64},{64,128},{128,192},{192,256},{256,320},{320,384},{384,448},... | collective-permute-start | bytes 835592 | tf_op jit(solution)/shard_map/ppermute | solution.py:354
  131.7 9.7 %collective-permute-start.12 = (bf16[544,256]{1,0:T(8,128)(2,1)S(1)}, bf16[544,256]{1,0:T(8,128)(2,1)S(1)}, u32[]{:S(2)}, u32[]{:S(2)}) collective-permute-start(bf16[544,256]{1,0:T(8,128)(2,1)S(1)} %add_convert_fusion.4), channel_id=1, source_target_pairs={{0,448},{64,0},{128,64},{192,128},{256,192},{320,256},{384,320},{4... | collective-permute-start | bytes 835592 | tf_op jit(solution)/shard_map/ppermute | solution.py:352
  136.7 10.4 %collective-permute-start.16 = (bf16[544,256]{1,0:T(8,128)(2,1)S(1)}, bf16[544,256]{1,0:T(8,128)(2,1)S(1)}, u32[]{:S(2)}, u32[]{:S(2)}) collective-permute-start(bf16[544,256]{1,0:T(8,128)(2,1)S(1)} %add_convert_fusion.1), channel_id=1, source_target_pairs={{0,64},{64,128},{128,192},{192,256},{256,320},{320,384},{384,448},... | collective-permute-start | bytes 835592 | tf_op jit(solution)/shard_map/ppermute | solution.py:354
  141.5 9.7 %collective-permute-start.13 = (bf16[544,256]{1,0:T(8,128)(2,1)S(1)}, bf16[544,256]{1,0:T(8,128)(2,1)S(1)}, u32[]{:S(2)}, u32[]{:S(2)}) collective-permute-start(bf16[544,256]{1,0:T(8,128)(2,1)S(1)} %add_convert_fusion.3), channel_id=1, source_target_pairs={{0,448},{64,0},{128,64},{192,128},{256,192},{320,256},{384,320},{4... | collective-permute-start | bytes 835592 | tf_op jit(solution)/shard_map/ppermute | solution.py:352
  166.1 9.3 %all-to-all-start.3 = ((f32[4,32,256]{2,1,0:T(8,128)}), f32[4,32,256]{2,1,0:T(8,128)S(1)}, u32[]{:S(2)}, u32[]{:S(2)}) async-start(f32[4,32,256]{2,1,0:T(8,128)} %broadcast_in_dim.21), calls=%async_computation.3 | async-start | bytes 262144 | tf_op jit(solution)/shard_map/all_to_all | solution.py:207

commit v6 on v5

--- a/solution.py
+++ b/solution.py
@@ -10,7 +10,7 @@
 
 ROW = ("z", "yl")
 COL = ("yh", "x", "c")
-UNROLL = 16
+UNROLL = 32
 MINE, FIRST, REST = range(3)
 
 

time: 177 us -> 178 us (level)
  waiting for transfers between devices: 41.3 us -> 34.9 us
  Pallas kernels: 8.62 us -> 13.6 us
    ppermute x4, waiting for transfers between devices: 13.9 us -> 10.7 us  [on_device(): ahead.append(lax.ppermute(down_sum, 'z', down))]
    ppermute x1, waiting for transfers between devices: 6.23 us -> 3.72 us  [on_device(): swapped = lax.ppermute(sums, 'yh', [(0, 1), (1, 0)])]
    pallas_call x4, Pallas kernels: 4.47 us -> 6.76 us  [call(): pl.pallas_call(kernel, out_shape=outs, in_specs=ins, out_specs=jax.tree.m...]
  transfers between devices with their start and end apart: 18 -> 18, of which waited for: 12 -> 11; matrix products, arithmetic and copies ran while one was open for 1% -> 1% of each run, Pallas kernels for 2% -> 4%
where the time goes in v6:
time: 178 us; the launch traced here: 176 us
  starting transfers between devices  66.2 us (37%)
  blocking collectives  53.7 us (30%)
  waiting for transfers between devices  34.9 us (20%)
  Pallas kernels  13.6 us (8%)
  other arithmetic  2.32 us (1%)
  local copies, waits for them, and re-layouts  2.09 us (1%)
    all_to_all x3, blocking collectives, exchange(): return lax.all_to_all(blocks, axes, 0, 0, tiled=True)  39.7 us
    ppermute x3, starting transfers between devices, on_device(): pieces[step] = lax.ppermute(pieces[step - 1], 'z', down)  18.9 us
    ppermute x4, starting transfers between devices, on_device(): ahead.append(lax.ppermute(down_sum, 'z', down))  15.8 us
    all_gather x1, blocking collectives, on_device(): lax.all_gather(both, 'yl', axis=0, tiled=True).reshape(yl_n, side, width)  14 us
    ppermute x4, waiting for transfers between devices, on_device(): ahead.append(lax.ppermute(down_sum, 'z', down))  10.7 us
    ppermute x3, starting transfers between devices, on_device(): behind.append(lax.ppermute(up_sum, 'z', up))  8.27 us
    ppermute x3, starting transfers between devices, on_device(): pieces[-step % z_n] = lax.ppermute(pieces[(1 - step) % z_n], 'z', up)  8.09 us
    ppermute x3, waiting for transfers between devices, on_device(): pieces[-step % z_n] = lax.ppermute(pieces[(1 - step) % z_n], 'z', up)  7.31 us
  transfers between devices with their start and end apart: 18, of which 11 were waited for; matrix products, arithmetic and copies ran while one was open for 1% of the time, Pallas kernels for 4%

profile of v6, /device:TPU:56, one launch (start us, length us, event | category | flops | bytes accessed | tf_op | source)
XLA Modules:
  0.0 176.2 jit_solution(10476855010388451496)
XLA Ops:
  0.6 0.0 copy-start
  0.6 0.8 pad_maximum_fusion.1
  1.4 14.0 %all_gather.3 = bf16[512,256]{1,0:T(8,128)(2,1)S(1)} all-gather(bf16[128,256]{1,0:T(8,128)(2,1)S(1)} %pad_maximum_fusion.1), channel_id=1, replica_groups=mesh['z'=8,'yl'=4,'yh'=2,'x'=4,'c'=2] {'yl'}, dimensions={0}, use_global_device_ids=true | all-gather | bytes 327680 | tf_op jit(solution)/shard_map/all_gather | solution.py:240
  15.4 4.3 %collective-permute-start.3 = (bf16[4,128,256]{2,1,0:T(8,128)(2,1)S(1)}, bf16[4,128,256]{2,1,0:T(8,128)(2,1)S(1)}, u32[]{:S(2)}, u32[]{:S(2)}) collective-permute-start(bf16[4,128,256]{2,1,0:T(8,128)(2,1)S(1)} %bitcast.65), channel_id=1, source_target_pairs={{0,64},{64,128},{128,192},{192,256},{256,320},{320,384},{384,448},... | collective-permute-start | bytes 786440 | tf_op jit(solution)/shard_map/ppermute | solution.py:245
  19.7 8.6 %collective-permute-start = (bf16[4,128,256]{2,1,0:T(8,128)(2,1)S(1)}, bf16[4,128,256]{2,1,0:T(8,128)(2,1)S(1)}, u32[]{:S(2)}, u32[]{:S(2)}) collective-permute-start(bf16[4,128,256]{2,1,0:T(8,128)(2,1)S(1)} %bitcast.66), channel_id=1, source_target_pairs={{0,448},{64,0},{128,64},{192,128},{256,192},{320,256},{384,320},{4... | collective-permute-start | bytes 786440 | tf_op jit(solution)/shard_map/ppermute | solution.py:246
  28.3 2.5 %collective-permute-done.3.refs_7_ = bf16[4,128,256]{2,1,0:T(8,128)(2,1)S(1)} collective-permute-done((bf16[4,128,256]{2,1,0:T(8,128)(2,1)S(1)}, bf16[4,128,256]{2,1,0:T(8,128)(2,1)S(1)}, u32[]{:S(2)}, u32[]{:S(2)}) %collective-permute-start.3) | collective-permute-done | bytes 262176 | tf_op jit(solution)/shard_map/ppermute | solution.py:245
  30.8 1.9 %collective-permute-start.4 = (bf16[4,128,256]{2,1,0:T(8,128)(2,1)S(1)}, bf16[4,128,256]{2,1,0:T(8,128)(2,1)S(1)}, u32[]{:S(2)}, u32[]{:S(2)}) collective-permute-start(bf16[4,128,256]{2,1,0:T(8,128)(2,1)S(1)} %collective-permute-done.3.refs_7_), channel_id=1, source_target_pairs={{0,64},{64,128},{128,192},{192,256},{256,320},{320,384},{384,448},... | collective-permute-start | bytes 786440 | tf_op jit(solution)/shard_map/ppermute | solution.py:245
  32.7 0.0 collective-permute-done.refs_1_
  32.7 5.1 %collective-permute-start.1 = (bf16[4,128,256]{2,1,0:T(8,128)(2,1)S(1)}, bf16[4,128,256]{2,1,0:T(8,128)(2,1)S(1)}, u32[]{:S(2)}, u32[]{:S(2)}) collective-permute-start(bf16[4,128,256]{2,1,0:T(8,128)(2,1)S(1)} %collective-permute-done.refs_1_), channel_id=1, source_target_pairs={{0,448},{64,0},{128,64},{192,128},{256,192},{320,256},{384,320},{4... | collective-permute-start | bytes 786440 | tf_op jit(solution)/shard_map/ppermute | solution.py:246
  37.9 2.4 %collective-permute-done.4.refs_6_ = bf16[4,128,256]{2,1,0:T(8,128)(2,1)S(1)} collective-permute-done((bf16[4,128,256]{2,1,0:T(8,128)(2,1)S(1)}, bf16[4,128,256]{2,1,0:T(8,128)(2,1)S(1)}, u32[]{:S(2)}, u32[]{:S(2)}) %collective-permute-start.4) | collective-permute-done | bytes 262176 | tf_op jit(solution)/shard_map/ppermute | solution.py:245
  40.3 1.9 %collective-permute-start.5 = (bf16[4,128,256]{2,1,0:T(8,128)(2,1)S(1)}, bf16[4,128,256]{2,1,0:T(8,128)(2,1)S(1)}, u32[]{:S(2)}, u32[]{:S(2)}) collective-permute-start(bf16[4,128,256]{2,1,0:T(8,128)(2,1)S(1)} %collective-permute-done.4.refs_6_), channel_id=1, source_target_pairs={{0,64},{64,128},{128,192},{192,256},{256,320},{320,384},{384,448},... | collective-permute-start | bytes 786440 | tf_op jit(solution)/shard_map/ppermute | solution.py:245
  42.2 0.0 collective-permute-done.1.refs_2_
  42.2 5.1 %collective-permute-start.2 = (bf16[4,128,256]{2,1,0:T(8,128)(2,1)S(1)}, bf16[4,128,256]{2,1,0:T(8,128)(2,1)S(1)}, u32[]{:S(2)}, u32[]{:S(2)}) collective-permute-start(bf16[4,128,256]{2,1,0:T(8,128)(2,1)S(1)} %collective-permute-done.1.refs_2_), channel_id=1, source_target_pairs={{0,448},{64,0},{128,64},{192,128},{256,192},{320,256},{384,320},{4... | collective-permute-start | bytes 786440 | tf_op jit(solution)/shard_map/ppermute | solution.py:246
  47.3 2.4 %collective-permute-done.5.refs_5_ = bf16[4,128,256]{2,1,0:T(8,128)(2,1)S(1)} collective-permute-done((bf16[4,128,256]{2,1,0:T(8,128)(2,1)S(1)}, bf16[4,128,256]{2,1,0:T(8,128)(2,1)S(1)}, u32[]{:S(2)}, u32[]{:S(2)}) %collective-permute-start.5) | collective-permute-done | bytes 262176 | tf_op jit(solution)/shard_map/ppermute | solution.py:245
  49.7 1.9 %collective-permute-start.6 = (bf16[4,128,256]{2,1,0:T(8,128)(2,1)S(1)}, bf16[4,128,256]{2,1,0:T(8,128)(2,1)S(1)}, u32[]{:S(2)}, u32[]{:S(2)}) collective-permute-start(bf16[4,128,256]{2,1,0:T(8,128)(2,1)S(1)} %collective-permute-done.5.refs_5_), channel_id=1, source_target_pairs={{0,64},{64,128},{128,192},{192,256},{256,320},{320,384},{384,448},... | collective-permute-start | bytes 786440 | tf_op jit(solution)/shard_map/ppermute | solution.py:247
  52.3 0.8 fusion.18
  53.1 6.1 %collective-permute-done.6.refs_4_ = bf16[4,128,256]{2,1,0:T(8,128)(2,1)S(1)} collective-permute-done((bf16[4,128,256]{2,1,0:T(8,128)(2,1)S(1)}, bf16[4,128,256]{2,1,0:T(8,128)(2,1)S(1)}, u32[]{:S(2)}, u32[]{:S(2)}) %collective-permute-start.6) | collective-permute-done | bytes 262176 | tf_op jit(solution)/shard_map/ppermute | solution.py:247
  59.2 4.0 %shard_map.102 = (bf16[8,128,256]{2,1,0:T(8,128)(2,1)S(1)}, bf16[8,128,256]{2,1,0:T(8,128)(2,1)S(1)}) custom-call(s32[96]{0:T(128)S(1)} %get-tuple-element.44.source_ref, s32[96]{0:T(128)S(1)} %get-tuple-element.43.target_ref, s32[1]{0:T(128)} %bitcast.59.count_ref, bf16[96,128,128]{2,1,0:T(8,128)(2,1)} %bitcast.61, bf16[4,128,256]{2,1,0:T(8,128)(2,1)S(1)} %bitcast.67, ...), custom_call_target="tpu_custom_call" | custom-call | flops 805306368 | bytes 3145728 | tf_op jit(solution)/shard_map/pallas_call | solution.py:257
  63.2 1.9 %collective-permute-start.7 = (bf16[8,128,256]{2,1,0:T(8,128)(2,1)S(1)}, bf16[8,128,256]{2,1,0:T(8,128)(2,1)S(1)}, u32[]{:S(2)}, u32[]{:S(2)}) collective-permute-start(bf16[8,128,256]{2,1,0:T(8,128)(2,1)S(1)} %get-tuple-element.23), channel_id=1, source_target_pairs={{0,1},{1,0},{2,3},{3,2},{4,5},{5,4},{6,7},{7,6},{8,9},{9,8},{10,11... | collective-permute-start | bytes 1572872 | tf_op jit(solution)/shard_map/ppermute | solution.py:215
  65.2 1.9 %collective-permute-done.7 = bf16[8,128,256]{2,1,0:T(8,128)(2,1)S(1)} collective-permute-done((bf16[8,128,256]{2,1,0:T(8,128)(2,1)S(1)}, bf16[8,128,256]{2,1,0:T(8,128)(2,1)S(1)}, u32[]{:S(2)}, u32[]{:S(2)}) %collective-permute-start.7) | collective-permute-done | bytes 524320 | tf_op jit(solution)/shard_map/ppermute | solution.py:215
  67.0 0.1 add_convert_fusion
  67.2 0.0 copy-start.2
  67.2 13.9 %all_to_all.20 = bf16[8,128,256]{2,1,0:T(8,128)(2,1)S(1)} all-to-all(bf16[8,128,256]{2,1,0:T(8,128)(2,1)S(1)} %add_convert_fusion), channel_id=1, replica_groups=mesh['z'=8,'yl'=4,'yh'=2,'x'=4,'c'=2] {'x'}, dimensions={0} | all-to-all | bytes 1048576 | tf_op jit(solution)/shard_map/all_to_all | solution.py:207
  81.1 0.1 bitcast_reduce_fusion
  81.1 6.1 %collective-permute-start.8 = (bf16[256,256]{1,0:T(8,128)(2,1)S(1)}, bf16[256,256]{1,0:T(8,128)(2,1)S(1)}, u32[]{:S(2)}, u32[]{:S(2)}) collective-permute-start(bf16[256,256]{1,0:T(8,128)(2,1)S(1)} %bitcast_reduce_fusion), channel_id=1, source_target_pairs={{0,8},{8,0},{1,9},{9,1},{2,10},{10,2},{3,11},{11,3},{4,12},{12,4},... | collective-permute-start | bytes 393224 | tf_op jit(solution)/shard_map/ppermute | solution.py:284
  87.3 2.8 %shard_map.103 = (s32[289]{0:T(512)S(1)}, s32[3]{0:T(128)S(1)}) custom-call(s32[96]{0:T(128)S(1)} %get-tuple-element.24.coords_ref, s32[1]{0:T(128)} %bitcast.60.count_ref), custom_call_target="tpu_custom_call" | custom-call | bytes 1048576 | tf_op jit(solution)/shard_map/pallas_call | solution.py:285
  90.1 3.7 %collective-permute-done.8 = bf16[256,256]{1,0:T(8,128)(2,1)S(1)} collective-permute-done((bf16[256,256]{1,0:T(8,128)(2,1)S(1)}, bf16[256,256]{1,0:T(8,128)(2,1)S(1)}, u32[]{:S(2)}, u32[]{:S(2)}) %collective-permute-start.8) | collective-permute-done | bytes 131104 | tf_op jit(solution)/shard_map/ppermute | solution.py:284
  93.9 0.2 multiply_convert_fusion
  94.1 0.2 fusion
  94.3 0.2 convolution_convert_fusion.3
  94.5 0.1 convolution_convert_fusion
  94.7 0.1 convolution_convert_fusion.2
  94.8 0.0 copy-start.1
  94.8 0.1 copy.12
  95.1 12.0 %all_to_all.21.mine_ref = bf16[4,288,256]{2,1,0:T(8,128)(2,1)S(1)} all-to-all(bf16[4,288,256]{2,1,0:T(8,128)(2,1)S(1)} %maximum_maximum_fusion), channel_id=1, replica_groups=mesh['z'=8,'yl'=4,'yh'=2,'x'=4,'c'=2] {'x'}, dimensions={0} | all-to-all | bytes 1179648 | tf_op jit(solution)/shard_map/all_to_all | solution.py:207
  107.1 1.9 %collective-permute-start.9 = (bf16[4,288,256]{2,1,0:T(8,128)(2,1)S(1)}, bf16[4,288,256]{2,1,0:T(8,128)(2,1)S(1)}, u32[]{:S(2)}, u32[]{:S(2)}) collective-permute-start(bf16[4,288,256]{2,1,0:T(8,128)(2,1)S(1)} %all_to_all.21.mine_ref), channel_id=1, source_target_pairs={{0,1},{1,0},{2,3},{3,2},{4,5},{5,4},{6,7},{7,6},{8,9},{9,8},{10,11... | collective-permute-start | bytes 1769480 | tf_op jit(solution)/shard_map/ppermute | solution.py:215
  109.0 2.8 %shard_map.104.begun_ref = f32[33,128,256]{2,1,0:T(8,128)S(1)} custom-call(s32[289]{0:T(512)S(1)} %get-tuple-element.28.list_ref, s32[3]{0:T(128)S(1)} %get-tuple-element.29.size_ref, bf16[96,128,128]{2,1,0:T(8,128)(2,1)S(1)} %bitcast.62, bf16[4,288,256]{2,1,0:T(8,128)(2,1)S(1)} %all_to_all.21.mine_ref), custom_call_target="tpu_custom_call" | custom-call | flops 402653184 | bytes 4325376 | tf_op jit(solution)/shard_map/pallas_call | solution.py:193
  111.8 1.4 shard_map.106
  113.2 1.9 %collective-permute-start.10 = (bf16[544,256]{1,0:T(8,128)(2,1)S(1)}, bf16[544,256]{1,0:T(8,128)(2,1)S(1)}, u32[]{:S(2)}, u32[]{:S(2)}) collective-permute-start(bf16[544,256]{1,0:T(8,128)(2,1)S(1)} %get-tuple-element.33), channel_id=1, source_target_pairs={{0,448},{64,0},{128,64},{192,128},{256,192},{320,256},{384,320},{4... | collective-permute-start | bytes 835592 | tf_op jit(solution)/shard_map/ppermute | solution.py:352
  115.1 3.9 %collective-permute-start.14 = (bf16[544,256]{1,0:T(8,128)(2,1)S(1)}, bf16[544,256]{1,0:T(8,128)(2,1)S(1)}, u32[]{:S(2)}, u32[]{:S(2)}) collective-permute-start(bf16[544,256]{1,0:T(8,128)(2,1)S(1)} %get-tuple-element.37), channel_id=1, source_target_pairs={{0,64},{64,128},{128,192},{192,256},{256,320},{320,384},{384,448},... | collective-permute-start | bytes 835592 | tf_op jit(solution)/shard_map/ppermute | solution.py:354
  119.1 1.9 %shard_map.105 = (bf16[512,256]{1,0:T(8,128)(2,1)S(1)}, bf16[544,256]{1,0:T(8,128)(2,1)S(1)}, bf16[544,256]{1,0:T(8,128)(2,1)S(1)}, bf16[544,256]{1,0:T(8,128)(2...) custom-call(s32[289]{0:T(512)S(1)} %get-tuple-element.28.list_ref, s32[3]{0:T(128)S(1)} %get-tuple-element.29.size_ref, ...), custom_call_target="tpu_custom_call" | custom-call | flops 402653184 | bytes 524288 | tf_op jit(solution)/shard_map/pallas_call | solution.py:193
  121.0 1.9 %collective-permute-done.10.refs_0_ = bf16[544,256]{1,0:T(8,128)(2,1)S(1)} collective-permute-done((bf16[544,256]{1,0:T(8,128)(2,1)S(1)}, bf16[544,256]{1,0:T(8,128)(2,1)S(1)}, u32[]{:S(2)}, u32[]{:S(2)}) %collective-permute-start.10) | collective-permute-done | bytes 278560 | tf_op jit(solution)/shard_map/ppermute | solution.py:352
  122.9 0.1 add_convert_fusion.5
  122.9 3.4 %collective-permute-start.11 = (bf16[544,256]{1,0:T(8,128)(2,1)S(1)}, bf16[544,256]{1,0:T(8,128)(2,1)S(1)}, u32[]{:S(2)}, u32[]{:S(2)}) collective-permute-start(bf16[544,256]{1,0:T(8,128)(2,1)S(1)} %add_convert_fusion.5), channel_id=1, source_target_pairs={{0,448},{64,0},{128,64},{192,128},{256,192},{320,256},{384,320},{4... | collective-permute-start | bytes 835592 | tf_op jit(solution)/shard_map/ppermute | solution.py:352
  126.4 0.1 add_convert_fusion.2
  126.4 2.4 %collective-permute-start.15 = (bf16[544,256]{1,0:T(8,128)(2,1)S(1)}, bf16[544,256]{1,0:T(8,128)(2,1)S(1)}, u32[]{:S(2)}, u32[]{:S(2)}) collective-permute-start(bf16[544,256]{1,0:T(8,128)(2,1)S(1)} %add_convert_fusion.2), channel_id=1, source_target_pairs={{0,64},{64,128},{128,192},{192,256},{256,320},{320,384},{384,448},... | collective-permute-start | bytes 835592 | tf_op jit(solution)/shard_map/ppermute | solution.py:354
  128.9 2.8 %collective-permute-done.11.refs_1_ = bf16[544,256]{1,0:T(8,128)(2,1)S(1)} collective-permute-done((bf16[544,256]{1,0:T(8,128)(2,1)S(1)}, bf16[544,256]{1,0:T(8,128)(2,1)S(1)}, u32[]{:S(2)}, u32[]{:S(2)}) %collective-permute-start.11) | collective-permute-done | bytes 278560 | tf_op jit(solution)/shard_map/ppermute | solution.py:352
  131.7 0.1 add_convert_fusion.4
  131.7 4.9 %collective-permute-start.12 = (bf16[544,256]{1,0:T(8,128)(2,1)S(1)}, bf16[544,256]{1,0:T(8,128)(2,1)S(1)}, u32[]{:S(2)}, u32[]{:S(2)}) collective-permute-start(bf16[544,256]{1,0:T(8,128)(2,1)S(1)} %add_convert_fusion.4), channel_id=1, source_target_pairs={{0,448},{64,0},{128,64},{192,128},{256,192},{320,256},{384,320},{4... | collective-permute-start | bytes 835592 | tf_op jit(solution)/shard_map/ppermute | solution.py:352
  136.7 0.1 add_convert_fusion.1
  136.7 1.9 %collective-permute-start.16 = (bf16[544,256]{1,0:T(8,128)(2,1)S(1)}, bf16[544,256]{1,0:T(8,128)(2,1)S(1)}, u32[]{:S(2)}, u32[]{:S(2)}) collective-permute-start(bf16[544,256]{1,0:T(8,128)(2,1)S(1)} %add_convert_fusion.1), channel_id=1, source_target_pairs={{0,64},{64,128},{128,192},{192,256},{256,320},{320,384},{384,448},... | collective-permute-start | bytes 835592 | tf_op jit(solution)/shard_map/ppermute | solution.py:354
  138.7 2.0 %collective-permute-done.12.refs_2_ = bf16[544,256]{1,0:T(8,128)(2,1)S(1)} collective-permute-done((bf16[544,256]{1,0:T(8,128)(2,1)S(1)}, bf16[544,256]{1,0:T(8,128)(2,1)S(1)}, u32[]{:S(2)}, u32[]{:S(2)}) %collective-permute-start.12) | collective-permute-done | bytes 278560 | tf_op jit(solution)/shard_map/ppermute | solution.py:352
  140.7 0.1 add_convert_fusion.3
  140.8 5.6 %collective-permute-start.13 = (bf16[544,256]{1,0:T(8,128)(2,1)S(1)}, bf16[544,256]{1,0:T(8,128)(2,1)S(1)}, u32[]{:S(2)}, u32[]{:S(2)}) collective-permute-start(bf16[544,256]{1,0:T(8,128)(2,1)S(1)} %add_convert_fusion.3), channel_id=1, source_target_pairs={{0,448},{64,0},{128,64},{192,128},{256,192},{320,256},{384,320},{4... | collective-permute-start | bytes 835592 | tf_op jit(solution)/shard_map/ppermute | solution.py:352
  146.4 0.0 collective-permute-done.16.refs_4_
  146.4 4.0 %collective-permute-done.13.refs_3_ = bf16[544,256]{1,0:T(8,128)(2,1)S(1)} collective-permute-done((bf16[544,256]{1,0:T(8,128)(2,1)S(1)}, bf16[544,256]{1,0:T(8,128)(2,1)S(1)}, u32[]{:S(2)}, u32[]{:S(2)}) %collective-permute-start.13) | collective-permute-done | bytes 278560 | tf_op jit(solution)/shard_map/ppermute | solution.py:352
  150.4 0.7 shard_map.107
  151.1 13.8 %all_to_all.22 = bf16[4,160,256]{2,1,0:T(8,128)(2,1)S(1)} all-to-all(bf16[4,160,256]{2,1,0:T(8,128)(2,1)S(1)} %shard_map.107), channel_id=1, replica_groups=mesh['z'=8,'yl'=4,'yh'=2,'x'=4,'c'=2] {'yl'}, dimensions={0} | all-to-all | bytes 655360 | tf_op jit(solution)/shard_map/all_to_all | solution.py:207
  164.9 0.6 slice_bitcast_fusion
  165.6 0.7 broadcast_in_dim.21
  166.2 3.3 %all-to-all-start.3 = ((f32[4,32,256]{2,1,0:T(8,128)}), f32[4,32,256]{2,1,0:T(8,128)S(1)}, u32[]{:S(2)}, u32[]{:S(2)}) async-start(f32[4,32,256]{2,1,0:T(8,128)} %broadcast_in_dim.21), calls=%async_computation.3 | async-start | bytes 262144 | tf_op jit(solution)/shard_map/all_to_all | solution.py:207
  169.6 0.8 fusion.1
  170.3 5.2 %all-to-all-done.3 = f32[4,32,256]{2,1,0:T(8,128)S(1)} async-done(((f32[4,32,256]{2,1,0:T(8,128)}), f32[4,32,256]{2,1,0:T(8,128)S(1)}, u32[]{:S(2)}, u32[]{:S(2)}) %all-to-all-start.3) | async-done | bytes 131104 | tf_op jit(solution)/shard_map/all_to_all | solution.py:207
  175.5 0.7 fusion.19
  (14 shorter events, 0.2 us)
Async XLA Ops:
  0.6 93.3 %copy-start = (bf16[128,128]{1,0:T(8,128)(2,1)S(1)}, bf16[128,128]{1,0:T(8,128)(2,1)}, u32[]{:S(2)}) copy-start(bf16[128,128]{1,0:T(8,128)(2,1)} %param.8) | copy-start | bytes 98308
  15.4 15.4 %collective-permute-start.3 = (bf16[4,128,256]{2,1,0:T(8,128)(2,1)S(1)}, bf16[4,128,256]{2,1,0:T(8,128)(2,1)S(1)}, u32[]{:S(2)}, u32[]{:S(2)}) collective-permute-start(bf16[4,128,256]{2,1,0:T(8,128)(2,1)S(1)} %bitcast.65), channel_id=1, source_target_pairs={{0,64},{64,128},{128,192},{192,256},{256,320},{320,384},{384,448},... | collective-permute-start | bytes 786440 | tf_op jit(solution)/shard_map/ppermute | solution.py:245
  19.7 13.0 %collective-permute-start = (bf16[4,128,256]{2,1,0:T(8,128)(2,1)S(1)}, bf16[4,128,256]{2,1,0:T(8,128)(2,1)S(1)}, u32[]{:S(2)}, u32[]{:S(2)}) collective-permute-start(bf16[4,128,256]{2,1,0:T(8,128)(2,1)S(1)} %bitcast.66), channel_id=1, source_target_pairs={{0,448},{64,0},{128,64},{192,128},{256,192},{320,256},{384,320},{4... | collective-permute-start | bytes 786440 | tf_op jit(solution)/shard_map/ppermute | solution.py:246
  30.8 9.5 %collective-permute-start.4 = (bf16[4,128,256]{2,1,0:T(8,128)(2,1)S(1)}, bf16[4,128,256]{2,1,0:T(8,128)(2,1)S(1)}, u32[]{:S(2)}, u32[]{:S(2)}) collective-permute-start(bf16[4,128,256]{2,1,0:T(8,128)(2,1)S(1)} %collective-permute-done.3.refs_7_), channel_id=1, source_target_pairs={{0,64},{64,128},{128,192},{192,256},{256,320},{320,384},{384,448},... | collective-permute-start | bytes 786440 | tf_op jit(solution)/shard_map/ppermute | solution.py:245
  32.7 9.5 %collective-permute-start.1 = (bf16[4,128,256]{2,1,0:T(8,128)(2,1)S(1)}, bf16[4,128,256]{2,1,0:T(8,128)(2,1)S(1)}, u32[]{:S(2)}, u32[]{:S(2)}) collective-permute-start(bf16[4,128,256]{2,1,0:T(8,128)(2,1)S(1)} %collective-permute-done.refs_1_), channel_id=1, source_target_pairs={{0,448},{64,0},{128,64},{192,128},{256,192},{320,256},{384,320},{4... | collective-permute-start | bytes 786440 | tf_op jit(solution)/shard_map/ppermute | solution.py:246
  40.3 9.5 %collective-permute-start.5 = (bf16[4,128,256]{2,1,0:T(8,128)(2,1)S(1)}, bf16[4,128,256]{2,1,0:T(8,128)(2,1)S(1)}, u32[]{:S(2)}, u32[]{:S(2)}) collective-permute-start(bf16[4,128,256]{2,1,0:T(8,128)(2,1)S(1)} %collective-permute-done.4.refs_6_), channel_id=1, source_target_pairs={{0,64},{64,128},{128,192},{192,256},{256,320},{320,384},{384,448},... | collective-permute-start | bytes 786440 | tf_op jit(solution)/shard_map/ppermute | solution.py:245
  42.2 10.9 %collective-permute-start.2 = (bf16[4,128,256]{2,1,0:T(8,128)(2,1)S(1)}, bf16[4,128,256]{2,1,0:T(8,128)(2,1)S(1)}, u32[]{:S(2)}, u32[]{:S(2)}) collective-permute-start(bf16[4,128,256]{2,1,0:T(8,128)(2,1)S(1)} %collective-permute-done.1.refs_2_), channel_id=1, source_target_pairs={{0,448},{64,0},{128,64},{192,128},{256,192},{320,256},{384,320},{4... | collective-permute-start | bytes 786440 | tf_op jit(solution)/shard_map/ppermute | solution.py:246
  49.7 9.5 %collective-permute-start.6 = (bf16[4,128,256]{2,1,0:T(8,128)(2,1)S(1)}, bf16[4,128,256]{2,1,0:T(8,128)(2,1)S(1)}, u32[]{:S(2)}, u32[]{:S(2)}) collective-permute-start(bf16[4,128,256]{2,1,0:T(8,128)(2,1)S(1)} %collective-permute-done.5.refs_5_), channel_id=1, source_target_pairs={{0,64},{64,128},{128,192},{192,256},{256,320},{320,384},{384,448},... | collective-permute-start | bytes 786440 | tf_op jit(solution)/shard_map/ppermute | solution.py:247
  63.2 3.8 %collective-permute-start.7 = (bf16[8,128,256]{2,1,0:T(8,128)(2,1)S(1)}, bf16[8,128,256]{2,1,0:T(8,128)(2,1)S(1)}, u32[]{:S(2)}, u32[]{:S(2)}) collective-permute-start(bf16[8,128,256]{2,1,0:T(8,128)(2,1)S(1)} %get-tuple-element.23), channel_id=1, source_target_pairs={{0,1},{1,0},{2,3},{3,2},{4,5},{5,4},{6,7},{7,6},{8,9},{9,8},{10,11... | collective-permute-start | bytes 1572872 | tf_op jit(solution)/shard_map/ppermute | solution.py:215
  67.2 26.9 %copy-start.2 = (bf16[128,128]{1,0:T(8,128)(2,1)S(1)}, bf16[128,128]{1,0:T(8,128)(2,1)}, u32[]{:S(2)}) copy-start(bf16[128,128]{1,0:T(8,128)(2,1)} %param.9) | copy-start | bytes 98308
  81.1 12.7 %collective-permute-start.8 = (bf16[256,256]{1,0:T(8,128)(2,1)S(1)}, bf16[256,256]{1,0:T(8,128)(2,1)S(1)}, u32[]{:S(2)}, u32[]{:S(2)}) collective-permute-start(bf16[256,256]{1,0:T(8,128)(2,1)S(1)} %bitcast_reduce_fusion), channel_id=1, source_target_pairs={{0,8},{8,0},{1,9},{9,1},{2,10},{10,2},{3,11},{11,3},{4,12},{12,4},... | collective-permute-start | bytes 393224 | tf_op jit(solution)/shard_map/ppermute | solution.py:284
  94.8 14.2 %copy-start.1 = (bf16[1,1,96,128,128]{4,3,2,1,0:T(8,128)(2,1)S(1)}, bf16[1,1,96,128,128]{4,3,2,1,0:T(8,128)(2,1)}, u32[]{:S(2)}) copy-start(bf16[1,1,96,128,128]{4,3,2,1,0:T(8,128)(2,1)} %param.10) | copy-start | bytes 9437188
  107.1 4.7 %collective-permute-start.9 = (bf16[4,288,256]{2,1,0:T(8,128)(2,1)S(1)}, bf16[4,288,256]{2,1,0:T(8,128)(2,1)S(1)}, u32[]{:S(2)}, u32[]{:S(2)}) collective-permute-start(bf16[4,288,256]{2,1,0:T(8,128)(2,1)S(1)} %all_to_all.21.mine_ref), channel_id=1, source_target_pairs={{0,1},{1,0},{2,3},{3,2},{4,5},{5,4},{6,7},{7,6},{8,9},{9,8},{10,11... | collective-permute-start | bytes 1769480 | tf_op jit(solution)/shard_map/ppermute | solution.py:215
  113.2 9.6 %collective-permute-start.10 = (bf16[544,256]{1,0:T(8,128)(2,1)S(1)}, bf16[544,256]{1,0:T(8,128)(2,1)S(1)}, u32[]{:S(2)}, u32[]{:S(2)}) collective-permute-start(bf16[544,256]{1,0:T(8,128)(2,1)S(1)} %get-tuple-element.33), channel_id=1, source_target_pairs={{0,448},{64,0},{128,64},{192,128},{256,192},{320,256},{384,320},{4... | collective-permute-start | bytes 835592 | tf_op jit(solution)/shard_map/ppermute | solution.py:352
  115.1 11.2 %collective-permute-start.14 = (bf16[544,256]{1,0:T(8,128)(2,1)S(1)}, bf16[544,256]{1,0:T(8,128)(2,1)S(1)}, u32[]{:S(2)}, u32[]{:S(2)}) collective-permute-start(bf16[544,256]{1,0:T(8,128)(2,1)S(1)} %get-tuple-element.37), channel_id=1, source_target_pairs={{0,64},{64,128},{128,192},{192,256},{256,320},{320,384},{384,448},... | collective-permute-start | bytes 835592 | tf_op jit(solution)/shard_map/ppermute | solution.py:354
  122.9 8.7 %collective-permute-start.11 = (bf16[544,256]{1,0:T(8,128)(2,1)S(1)}, bf16[544,256]{1,0:T(8,128)(2,1)S(1)}, u32[]{:S(2)}, u32[]{:S(2)}) collective-permute-start(bf16[544,256]{1,0:T(8,128)(2,1)S(1)} %add_convert_fusion.5), channel_id=1, source_target_pairs={{0,448},{64,0},{128,64},{192,128},{256,192},{320,256},{384,320},{4... | collective-permute-start | bytes 835592 | tf_op jit(solution)/shard_map/ppermute | solution.py:352
  126.4 10.2 %collective-permute-start.15 = (bf16[544,256]{1,0:T(8,128)(2,1)S(1)}, bf16[544,256]{1,0:T(8,128)(2,1)S(1)}, u32[]{:S(2)}, u32[]{:S(2)}) collective-permute-start(bf16[544,256]{1,0:T(8,128)(2,1)S(1)} %add_convert_fusion.2), channel_id=1, source_target_pairs={{0,64},{64,128},{128,192},{192,256},{256,320},{320,384},{384,448},... | collective-permute-start | bytes 835592 | tf_op jit(solution)/shard_map/ppermute | solution.py:354
  131.7 9.0 %collective-permute-start.12 = (bf16[544,256]{1,0:T(8,128)(2,1)S(1)}, bf16[544,256]{1,0:T(8,128)(2,1)S(1)}, u32[]{:S(2)}, u32[]{:S(2)}) collective-permute-start(bf16[544,256]{1,0:T(8,128)(2,1)S(1)} %add_convert_fusion.4), channel_id=1, source_target_pairs={{0,448},{64,0},{128,64},{192,128},{256,192},{320,256},{384,320},{4... | collective-permute-start | bytes 835592 | tf_op jit(solution)/shard_map/ppermute | solution.py:352
  136.7 9.7 %collective-permute-start.16 = (bf16[544,256]{1,0:T(8,128)(2,1)S(1)}, bf16[544,256]{1,0:T(8,128)(2,1)S(1)}, u32[]{:S(2)}, u32[]{:S(2)}) collective-permute-start(bf16[544,256]{1,0:T(8,128)(2,1)S(1)} %add_convert_fusion.1), channel_id=1, source_target_pairs={{0,64},{64,128},{128,192},{192,256},{256,320},{320,384},{384,448},... | collective-permute-start | bytes 835592 | tf_op jit(solution)/shard_map/ppermute | solution.py:354
  140.8 9.7 %collective-permute-start.13 = (bf16[544,256]{1,0:T(8,128)(2,1)S(1)}, bf16[544,256]{1,0:T(8,128)(2,1)S(1)}, u32[]{:S(2)}, u32[]{:S(2)}) collective-permute-start(bf16[544,256]{1,0:T(8,128)(2,1)S(1)} %add_convert_fusion.3), channel_id=1, source_target_pairs={{0,448},{64,0},{128,64},{192,128},{256,192},{320,256},{384,320},{4... | collective-permute-start | bytes 835592 | tf_op jit(solution)/shard_map/ppermute | solution.py:352
  166.2 9.3 %all-to-all-start.3 = ((f32[4,32,256]{2,1,0:T(8,128)}), f32[4,32,256]{2,1,0:T(8,128)S(1)}, u32[]{:S(2)}, u32[]{:S(2)}) async-start(f32[4,32,256]{2,1,0:T(8,128)} %broadcast_in_dim.21), calls=%async_computation.3 | async-start | bytes 262144 | tf_op jit(solution)/shard_map/all_to_all | solution.py:207
